TPU v7x, 768 devices: a whole 4x8x12 slice. The times are simulated.
768 devices in a mesh: section: 12 (over z_hi, x), tm: 8 (over z_lo, core), space: 8 (over y).
Axes of the slice: x: 4, y: 8, z: 12 (z_hi: 3, z_lo: 4; z = z_hi * 4 + z_lo), core: 2. Of those that a mesh axis runs over, the one named last changes fastest.
Arguments:
- video: bfloat16 [12, 16, 512, 1152], P('section', 'tm', 'space'), may hold values from -6 to 6
- conv_taps: float32 [12, 3, 1152], P('section'), may hold values from -3 to 3
- modulation: float32 [12, 6, 1152], P('section'), may hold values from -3 to 3
- w_qkv: bfloat16 [12, 1152, 3, 1152], P('section', None, None, 'space'), may hold values from -6 to 6
- w_out: bfloat16 [12, 1152, 1152], P('section', 'space'), may hold values from -0.1875 to 0.1875
- w_up: bfloat16 [12, 1152, 4608], P('section', None, 'space'), may hold values from -0.1875 to 0.1875
- w_down: bfloat16 [12, 4608, 1152], P('section', 'space'), may hold values from -0.09375 to 0.09375
Outputs:
- next_in: bfloat16 [12, 16, 512, 1152], P('section', 'tm', 'space')
All inputs are finite; a program needn't handle non-finite values.
Results may differ from a plain program's by a relative error of at most 0.013.
Values may be sent and summed in bfloat16 or wider, within the bound.
No kernel may reach another device: no remote copies, remote signals or barrier semaphores. Data moves between devices by JAX's collectives and lax.ppermute only.
A program may use at most 32 MiB of HBM per device.

v0:
```python
import math

import jax
import jax.numpy as jnp
from jax import lax
from jax.sharding import PartitionSpec as P

D = 1152
HEADS = 16
HEAD = D // HEADS
BF16 = jnp.bfloat16
F32 = jnp.float32


def shifted(value, axis, steps):
    count = lax.axis_size(axis)
    initial, last = (max(0, -steps), min(count, count - steps))
    return lax.ppermute(value, axis, [(source, source + steps) for source in range(initial, last)])


def rotate(block, axis, steps):
    count = lax.axis_size(axis)
    return lax.ppermute(block, axis, [(i, (i + steps) % count) for i in range(count)])


def flip(block, axis):
    return lax.ppermute(block, axis, [(i, i ^ 1) for i in range(lax.axis_size(axis))])


def turn_z(block, steps):
    count = lax.axis_size("tm")
    return lax.ppermute(block, "tm", [(i, (i + 2 * steps) % count) for i in range(count)])


def normalize(values_in):
    centre = jnp.mean(values_in, axis=-1, keepdims=True)
    variance = jnp.mean(jnp.square(values_in - centre), axis=-1, keepdims=True)
    return (values_in - centre) * lax.rsqrt(variance + 1e-06)


def modulated(values_in, shift_row, scale_row):
    return (normalize(values_in) * (1.0 + scale_row) + shift_row).astype(BF16)


def attend(rows, qkv, out_w):
    tokens, heads = rows.shape[0], qkv.shape[1] // HEAD
    projected = jnp.einsum("te,cne->tcn", rows, qkv, preferred_element_type=F32).astype(BF16)
    projected = projected.reshape(tokens, 3, heads, HEAD)
    scores = jnp.einsum(
        "qhe,khe->hqk", projected[:, 0], projected[:, 1], preferred_element_type=F32
    ) * (1.0 / math.sqrt(HEAD))
    probs = jax.nn.softmax(scores, axis=-1).astype(BF16)
    heads_out = jnp.einsum("hqk,khe->qhe", probs, projected[:, 2], preferred_element_type=F32)
    heads_out = heads_out.astype(BF16).reshape(tokens, heads * HEAD)
    return jnp.dot(heads_out, out_w, preferred_element_type=F32)


def feed_forward(rows, up_w, down_w):
    activated = jax.nn.gelu(
        jnp.einsum("te,ne->tn", rows, up_w, preferred_element_type=F32), approximate=True
    ).astype(BF16)
    return jnp.dot(activated, down_w, preferred_element_type=F32)


def core_half(block, rows):
    return lax.dynamic_slice_in_dim(block, (lax.axis_index("tm") % 2) * rows, rows, block.ndim - 2)


def after(value, *earlier):
    return lax.optimization_barrier((value, *earlier))[0]


def body(video, conv_taps, modulation, w_qkv, w_out, w_up, w_down):
    frames_in = video[0]
    tap_set = conv_taps[0]
    mod_table = modulation[0]
    frames, tokens = frames_in.shape[:2]
    n_space = lax.axis_size("space")
    qkv_own = w_qkv[0].transpose(1, 2, 0)
    out_own = w_out[0]
    up_own = w_up[0].T
    down_own = w_down[0]

    half = qkv_own.shape[1] // 2
    place, members = lax.axis_index("tm"), lax.axis_size("tm")
    share = up_own.shape[0] // members

    earlier = shifted(frames_in, "tm", 1)
    near = jnp.concatenate([core_half(qkv_own, half), core_half(out_own, half)[None]], axis=0)
    near = flip(near, "space")
    near_more = flip(near, "tm")
    near = jnp.concatenate([near, near_more], axis=1)
    far = jnp.concatenate(
        [lax.dynamic_slice_in_dim(w, place * share, share, 0) for w in (up_own, down_own)], axis=0
    )
    far = rotate(far, "space", n_space // 2)

    extended = jnp.concatenate([earlier, frames_in], axis=0).astype(F32)
    mixed_rows = (
        extended[2:]
        + tap_set[0] * extended[2:]
        + tap_set[1] * extended[1:-1]
        + tap_set[2] * extended[:-2]
    ).astype(BF16)
    mixed_f32 = mixed_rows.astype(F32)

    attn_in = modulated(mixed_f32, mod_table[0], mod_table[1])
    outgoing = jnp.broadcast_to(attn_in[None], (n_space // frames, frames, tokens, D))
    rows = lax.all_to_all(outgoing.reshape(n_space, tokens, D), "space", 0, 0, tiled=True)
    rows = rows.reshape(n_space * tokens, D)
    attn_part = attend(rows, qkv_own, out_own) + attend(rows, near[:3], near[3])
    attn_part = attn_part.astype(BF16).reshape(n_space, tokens, D)
    far = after(far, attn_part)
    turned = [far]
    for k in range(1, members // 2):
        turned.append(turn_z(far, k))
    far = jnp.stack(turned)
    parts = lax.all_to_all(attn_part, "space", 0, 0, tiled=True)
    attn_sum = jnp.sum(parts.reshape(n_space // frames, frames, tokens, D).astype(F32), axis=0)
    hidden_state = mixed_f32 + mod_table[2] * attn_sum
    mlp_in = modulated(hidden_state, mod_table[3], mod_table[4])
    far_more = flip(far, "tm")
    up_all = jnp.concatenate([up_own] + [w[:, :share].reshape(-1, D) for w in (far, far_more)])
    down_all = jnp.concatenate([down_own] + [w[:, share:].reshape(-1, D) for w in (far, far_more)])

    visits = []
    for frame, way in ((0, 1), (1, -1)):
        visits.append([mlp_in[frame]])
        for move in (way, -way, 2 * way):
            visits[frame].append(rotate(mlp_in[frame], "space", move))
    next_in = []
    for frame, way in ((0, 1), (1, -1)):
        visitors = jnp.stack(visits[frame]).reshape(-1, D)
        part = feed_forward(visitors, up_all, down_all).astype(BF16).reshape(-1, tokens, D)
        total = part[0].astype(F32)
        for k, move in enumerate((way, -way, 2 * way)):
            returned = rotate(part[k + 1], "space", -move)
            if frame:
                returned = after(returned, *next_in)
            total = total + returned.astype(F32)
        next_in.append((hidden_state[frame] + mod_table[5] * total).astype(BF16))
    moved = []
    for frame in range(frames):
        moved.append(rotate(next_in[frame], "section", 1))
    return jnp.stack(moved)[None]


def solution(mesh):
    placed = (
        P("section", "tm", "space", None),
        P("section", None, None),
        P("section", None, None),
        P("section", None, None, "space"),
        P("section", "space", None),
        P("section", None, "space"),
        P("section", "space", None),
    )

    return jax.shard_map(
        body,
        mesh=mesh,
        in_specs=placed,
        out_specs=P("section", "tm", "space", None),
        check_vma=False,
    )
```

profile of v0, /device:TPU:201, one launch (start us, length us, event | category | flops | bytes accessed | tf_op | source)
XLA Modules:
  0.0 261.6 jit_solution(2281326614916890267)
XLA Ops:
  6.0 7.1 %all-to-all-start = ((bf16[8,64,1152]{2,1,0:T(8,128)(2,1)}), bf16[8,64,1152]{2,1,0:T(8,128)(2,1)S(1)}, u32[]{:S(2)}, u32[]{:S(2)}) async-start(bf16[8,64,1152]{2,1,0:T(8,128)(2,1)} %bitcast.1), calls=%async_computation | async-start | bytes 2359296 | tf_op jit(solution)/shard_map/all_to_all | solution.py:109
  13.2 1.9 collective-permute-start.1
  15.2 35.6 %collective-permute-done.1 = bf16[4,72,1152]{2,1,0:T(8,128)(2,1)} collective-permute-done((bf16[4,72,1152]{2,1,0:T(8,128)(2,1)S(1)}, bf16[4,72,1152]{2,1,0:T(8,128)(2,1)}, u32[]{:S(2)}, u32[]{:S(2)}) %collective-permute-start.1) | collective-permute-done | bytes 663584 | tf_op jit(solution)/shard_map/ppermute | solution.py:27
  50.8 5.7 %collective-permute-start.2 = (bf16[4,72,1152]{2,1,0:T(8,128)(2,1)}, bf16[4,72,1152]{2,1,0:T(8,128)(2,1)}, u32[]{:S(2)}, u32[]{:S(2)}) collective-permute-start(bf16[4,72,1152]{2,1,0:T(8,128)(2,1)} %collective-permute-done.1), channel_id=1, source_target_pairs={{0,8},{8,0},{16,24},{24,16},{32,40},{40,32},{48,56},{56,48},{1,9},... | collective-permute-start | bytes 1990664 | tf_op jit(solution)/shard_map/ppermute | solution.py:27
  56.5 2.0 constant_dynamic-update-slice_fusion.1
  58.6 2.0 constant_dynamic-update-slice_fusion
  62.1 2.0 convolution_convert_fusion.2
  65.8 2.2 convolution_convert_fusion.4
  70.6 2.6 fusion.2
  73.2 6.9 %all-to-all-start.1 = ((bf16[8,64,1152]{2,1,0:T(8,128)(2,1)}), bf16[8,64,1152]{2,1,0:T(8,128)(2,1)}, u32[]{:S(2)}, u32[]{:S(2)}) async-start(bf16[8,64,1152]{2,1,0:T(8,128)(2,1)} %bitcast.23), calls=%async_computation.1 | async-start | bytes 2359296 | tf_op jit(solution)/shard_map/all_to_all | solution.py:118
  82.0 6.1 %collective-permute-start.6 = (bf16[144,1152]{1,0:T(8,128)(2,1)S(1)}, bf16[144,1152]{1,0:T(8,128)(2,1)S(1)}, u32[]{:S(2)}, u32[]{:S(2)}) collective-permute-start(bf16[144,1152]{1,0:T(8,128)(2,1)S(1)} %pad_maximum_fusion.18), channel_id=1, source_target_pairs={{0,4},{1,5},{2,6},{3,7},{4,0},{5,1},{6,2},{7,3},{8,12},{9,13},{10,... | collective-permute-start | bytes 995336 | tf_op jit(solution)/shard_map/ppermute | solution.py:23
  88.1 36.0 %collective-permute-done.6 = bf16[144,1152]{1,0:T(8,128)(2,1)S(1)} collective-permute-done((bf16[144,1152]{1,0:T(8,128)(2,1)S(1)}, bf16[144,1152]{1,0:T(8,128)(2,1)S(1)}, u32[]{:S(2)}, u32[]{:S(2)}) %collective-permute-start.6) | collective-permute-done | bytes 331808 | tf_op jit(solution)/shard_map/ppermute | solution.py:23
  124.1 4.4 %collective-permute-start.7 = (bf16[144,1152]{1,0:T(8,128)(2,1)S(1)}, bf16[144,1152]{1,0:T(8,128)(2,1)S(1)}, u32[]{:S(2)}, u32[]{:S(2)}) collective-permute-start(bf16[144,1152]{1,0:T(8,128)(2,1)S(1)} %collective-permute-done.6), channel_id=1, source_target_pairs={{0,16},{8,24},{16,32},{24,40},{32,48},{40,56},{48,0},{56,8},{1,17}... | collective-permute-start | bytes 995336 | tf_op jit(solution)/shard_map/ppermute | solution.py:32
  128.6 4.6 %collective-permute-start.8 = (bf16[144,1152]{1,0:T(8,128)(2,1)S(1)}, bf16[144,1152]{1,0:T(8,128)(2,1)S(1)}, u32[]{:S(2)}, u32[]{:S(2)}) collective-permute-start(bf16[144,1152]{1,0:T(8,128)(2,1)S(1)} %collective-permute-done.6), channel_id=1, source_target_pairs={{0,32},{8,40},{16,48},{24,56},{32,0},{40,8},{48,16},{56,24},{1,33}... | collective-permute-start | bytes 995336 | tf_op jit(solution)/shard_map/ppermute | solution.py:32
  136.7 22.2 %collective-permute-done.8 = bf16[144,1152]{1,0:T(8,128)(2,1)S(1)} collective-permute-done((bf16[144,1152]{1,0:T(8,128)(2,1)S(1)}, bf16[144,1152]{1,0:T(8,128)(2,1)S(1)}, u32[]{:S(2)}, u32[]{:S(2)}) %collective-permute-start.8) | collective-permute-done | bytes 331808 | tf_op jit(solution)/shard_map/ppermute | solution.py:32
  159.1 4.3 %collective-permute-start.10 = (bf16[4,144,1152]{2,1,0:T(8,128)(2,1)S(1)}, bf16[4,144,1152]{2,1,0:T(8,128)(2,1)}, u32[]{:S(2)}, u32[]{:S(2)}) collective-permute-start(bf16[4,144,1152]{2,1,0:T(8,128)(2,1)S(1)} %pad_maximum_fusion.2), channel_id=1, source_target_pairs={{0,8},{8,0},{16,24},{24,16},{32,40},{40,32},{48,56},{56,48},{1,9},... | collective-permute-start | bytes 3981320 | tf_op jit(solution)/shard_map/ppermute | solution.py:27
  167.7 2.0 collective-permute-start.3
  169.8 4.1 %collective-permute-start.4 = (bf16[64,1152]{1,0:T(8,128)(2,1)S(1)}, bf16[64,1152]{1,0:T(8,128)(2,1)S(1)}, u32[]{:S(2)}, u32[]{:S(2)}) collective-permute-start(bf16[64,1152]{1,0:T(8,128)(2,1)S(1)} %get-tuple-element.37), channel_id=1, source_target_pairs={{0,7},{1,0},{2,1},{3,2},{4,3},{5,4},{6,5},{7,6},{8,15},{9,8},{10,9... | collective-permute-start | bytes 442376 | tf_op jit(solution)/shard_map/ppermute | solution.py:23
  175.8 2.3 fusion.87
  178.1 4.6 %collective-permute-start.15 = (bf16[64,1152]{1,0:T(8,128)(2,1)}, bf16[64,1152]{1,0:T(8,128)(2,1)S(1)}, u32[]{:S(2)}, u32[]{:S(2)}) collective-permute-start(bf16[64,1152]{1,0:T(8,128)(2,1)} %get-tuple-element.38), channel_id=1, source_target_pairs={{0,7},{1,0},{2,1},{3,2},{4,3},{5,4},{6,5},{7,6},{8,15},{9,8},{10,9... | collective-permute-start | bytes 442376 | tf_op jit(solution)/shard_map/ppermute | solution.py:23
  184.6 5.5 %collective-permute-start.17 = (bf16[64,1152]{1,0:T(8,128)(2,1)}, bf16[64,1152]{1,0:T(8,128)(2,1)S(1)}, u32[]{:S(2)}, u32[]{:S(2)}) collective-permute-start(bf16[64,1152]{1,0:T(8,128)(2,1)} %get-tuple-element.38), channel_id=1, source_target_pairs={{0,6},{1,7},{2,0},{3,1},{4,2},{5,3},{6,4},{7,5},{8,14},{9,15},{10,... | collective-permute-start | bytes 442376 | tf_op jit(solution)/shard_map/ppermute | solution.py:23
  190.2 5.1 %convolution_convert_fusion.1 = bf16[256,1152]{1,0:T(8,128)(2,1)} fusion(bf16[288,1152]{1,0:T(8,128)(2,1)} %bitcast.44, bf16[288,1152]{1,0:T(8,128)(2,1)} %bitcast.141, bf16[576,1152]{1,0:T(8,128)(2,1)} %bitcast.163, bf16[256,1152]{1,0:T(8,128)(2,1)S(1)} %bitcast.146, bf16[288,1152]{1,0:T(8,128)(2,1)S(1)} %bitcast.143, bf16[288,1152]{1,0:T(8,128)(2,1)} %bitcast.139, ...), kind=kOutput, calls=%fused_computation.7 | convolution fusion | flops 1377828864 | bytes 6488064 | tf_op jit(solution)/shard_map/dot_general | solution.py:62
  197.2 3.4 %collective-permute-start.11 = (bf16[64,1152]{1,0:T(8,128)(2,1)}, bf16[64,1152]{1,0:T(8,128)(2,1)}, u32[]{:S(2)}, u32[]{:S(2)}) collective-permute-start(bf16[64,1152]{1,0:T(8,128)(2,1)} %get-tuple-element.33), channel_id=1, source_target_pairs={{0,7},{1,0},{2,1},{3,2},{4,3},{5,4},{6,5},{7,6},{8,15},{9,8},{10,9... | collective-permute-start | bytes 442376 | tf_op jit(solution)/shard_map/ppermute | solution.py:23
  202.5 4.5 %collective-permute-start.13 = (bf16[64,1152]{1,0:T(8,128)(2,1)}, bf16[64,1152]{1,0:T(8,128)(2,1)}, u32[]{:S(2)}, u32[]{:S(2)}) collective-permute-start(bf16[64,1152]{1,0:T(8,128)(2,1)} %get-tuple-element.34), channel_id=1, source_target_pairs={{0,6},{1,7},{2,0},{3,1},{4,2},{5,3},{6,4},{7,5},{8,14},{9,15},{10,... | collective-permute-start | bytes 442376 | tf_op jit(solution)/shard_map/ppermute | solution.py:23
  208.0 4.3 %convolution_convert_fusion = bf16[256,1152]{1,0:T(8,128)(2,1)S(1)} fusion(bf16[288,1152]{1,0:T(8,128)(2,1)} %bitcast.44, bf16[288,1152]{1,0:T(8,128)(2,1)S(1)} %bitcast.142, bf16[576,1152]{1,0:T(8,128)(2,1)} %bitcast.164, bf16[256,1152]{1,0:T(8,128)(2,1)} %bitcast.145, bf16[288,1152]{1,0:T(8,128)(2,1)} %bitcast.144, bf16[288,1152]{1,0:T(8,128)(2,1)S(1)} %bitcast.140, ...), kind=kOutput, calls=%fused_computation.6 | convolution fusion | flops 1377828864 | bytes 6488064 | tf_op jit(solution)/shard_map/dot_general | solution.py:62
  212.3 2.1 collective-permute-start.18
  214.4 3.1 %collective-permute-start.19 = (bf16[64,1152]{1,0:T(8,128)(2,1)S(1)}, bf16[64,1152]{1,0:T(8,128)(2,1)S(1)}, u32[]{:S(2)}, u32[]{:S(2)}) collective-permute-start(bf16[64,1152]{1,0:T(8,128)(2,1)S(1)} %get-tuple-element.32), channel_id=1, source_target_pairs={{0,7},{1,0},{2,1},{3,2},{4,3},{5,4},{6,5},{7,6},{8,15},{9,8},{10,9... | collective-permute-start | bytes 442376 | tf_op jit(solution)/shard_map/ppermute | solution.py:23
  220.8 6.5 %collective-permute-done.20 = bf16[64,1152]{1,0:T(8,128)(2,1)S(1)} collective-permute-done((bf16[64,1152]{1,0:T(8,128)(2,1)S(1)}, bf16[64,1152]{1,0:T(8,128)(2,1)S(1)}, u32[]{:S(2)}, u32[]{:S(2)}) %collective-permute-start.20) | collective-permute-done | bytes 147488 | tf_op jit(solution)/shard_map/ppermute | solution.py:23
  227.3 3.1 %collective-permute-start.21 = (bf16[64,1152]{1,0:T(8,128)(2,1)S(1)}, bf16[64,1152]{1,0:T(8,128)(2,1)S(1)}, u32[]{:S(2)}, u32[]{:S(2)}) collective-permute-start(bf16[64,1152]{1,0:T(8,128)(2,1)S(1)} %fusion.47), channel_id=1, source_target_pairs={{0,64},{64,128},{128,192},{192,256},{256,320},{320,384},{384,448},... | collective-permute-start | bytes 442376 | tf_op jit(solution)/shard_map/ppermute | solution.py:23
  230.5 3.1 %collective-permute-start.14 = (bf16[64,1152]{1,0:T(8,128)(2,1)S(1)}, bf16[64,1152]{1,0:T(8,128)(2,1)S(1)}, u32[]{:S(2)}, u32[]{:S(2)}) collective-permute-start(bf16[64,1152]{1,0:T(8,128)(2,1)S(1)} %fusion.49), channel_id=1, source_target_pairs={{0,64},{64,128},{128,192},{192,256},{256,320},{320,384},{384,448},... | collective-permute-start | bytes 442376 | tf_op jit(solution)/shard_map/ppermute | solution.py:23
  233.6 24.1 %collective-permute-done.21 = bf16[64,1152]{1,0:T(8,128)(2,1)S(1)} collective-permute-done((bf16[64,1152]{1,0:T(8,128)(2,1)S(1)}, bf16[64,1152]{1,0:T(8,128)(2,1)S(1)}, u32[]{:S(2)}, u32[]{:S(2)}) %collective-permute-start.21) | collective-permute-done | bytes 147488 | tf_op jit(solution)/shard_map/ppermute | solution.py:23
  257.7 3.2 %collective-permute-done.14 = bf16[64,1152]{1,0:T(8,128)(2,1)S(1)} collective-permute-done((bf16[64,1152]{1,0:T(8,128)(2,1)S(1)}, bf16[64,1152]{1,0:T(8,128)(2,1)S(1)}, u32[]{:S(2)}, u32[]{:S(2)}) %collective-permute-start.14) | collective-permute-done | bytes 147488 | tf_op jit(solution)/shard_map/ppermute | solution.py:23
  (80 shorter events, 34.5 us)
Async XLA Ops:
  0.0 3.7 %copy-start = (bf16[1,1152,3,144]{1,3,2,0:T(8,128)(2,1)S(1)}, bf16[1,1152,3,144]{1,3,2,0:T(8,128)(2,1)}, u32[]{:S(2)}) copy-start(bf16[1,1152,3,144]{1,3,2,0:T(8,128)(2,1)} %param.10) | copy-start | bytes 2985988
  0.0 4.0 %copy-start.5 = (bf16[1,2,64,1152]{3,2,1,0:T(8,128)(2,1)S(1)}, bf16[1,2,64,1152]{3,2,1,0:T(8,128)(2,1)}, u32[]{:S(2)}) copy-start(bf16[1,2,64,1152]{3,2,1,0:T(8,128)(2,1)} %param.7) | copy-start | bytes 884740
  0.0 4.0 %collective-permute-start = (bf16[2,64,1152]{2,1,0:T(8,128)(2,1)}, bf16[2,64,1152]{2,1,0:T(8,128)(2,1)S(1)}, u32[]{:S(2)}, u32[]{:S(2)}) collective-permute-start(bf16[2,64,1152]{2,1,0:T(8,128)(2,1)} %bitcast.151), channel_id=1, source_target_pairs={{0,8},{8,16},{16,24},{24,32},{32,40},{40,48},{48,56},{1,9},{9,17},... | collective-permute-start | bytes 884744 | tf_op jit(solution)/shard_map/ppermute | solution.py:18
  6.0 7.1 %copy-start.1 = (bf16[1,144,1152]{2,1,0:T(8,128)(2,1)S(1)}, bf16[1,144,1152]{2,1,0:T(8,128)(2,1)}, u32[]{:S(2)}) copy-start(bf16[1,144,1152]{2,1,0:T(8,128)(2,1)} %param.11) | copy-start | bytes 995332
  6.0 54.6 %all-to-all-start = ((bf16[8,64,1152]{2,1,0:T(8,128)(2,1)}), bf16[8,64,1152]{2,1,0:T(8,128)(2,1)S(1)}, u32[]{:S(2)}, u32[]{:S(2)}) async-start(bf16[8,64,1152]{2,1,0:T(8,128)(2,1)} %bitcast.1), calls=%async_computation | async-start | bytes 2359296 | tf_op jit(solution)/shard_map/all_to_all | solution.py:109
  13.2 37.6 %collective-permute-start.1 = (bf16[4,72,1152]{2,1,0:T(8,128)(2,1)S(1)}, bf16[4,72,1152]{2,1,0:T(8,128)(2,1)}, u32[]{:S(2)}, u32[]{:S(2)}) collective-permute-start(bf16[4,72,1152]{2,1,0:T(8,128)(2,1)S(1)} %pad_maximum_fusion.11), channel_id=1, source_target_pairs={{0,1},{1,0},{2,3},{3,2},{4,5},{5,4},{6,7},{7,6},{8,9},{9,8},{10,11... | collective-permute-start | bytes 1990664 | tf_op jit(solution)/shard_map/ppermute | solution.py:27
  50.8 7.8 %collective-permute-start.2 = (bf16[4,72,1152]{2,1,0:T(8,128)(2,1)}, bf16[4,72,1152]{2,1,0:T(8,128)(2,1)}, u32[]{:S(2)}, u32[]{:S(2)}) collective-permute-start(bf16[4,72,1152]{2,1,0:T(8,128)(2,1)} %collective-permute-done.1), channel_id=1, source_target_pairs={{0,8},{8,0},{16,24},{24,16},{32,40},{40,32},{48,56},{56,48},{1,9},... | collective-permute-start | bytes 1990664 | tf_op jit(solution)/shard_map/ppermute | solution.py:27
  65.7 2.2 copy-start.8
  73.2 91.5 %all-to-all-start.1 = ((bf16[8,64,1152]{2,1,0:T(8,128)(2,1)}), bf16[8,64,1152]{2,1,0:T(8,128)(2,1)}, u32[]{:S(2)}, u32[]{:S(2)}) async-start(bf16[8,64,1152]{2,1,0:T(8,128)(2,1)} %bitcast.23), calls=%async_computation.1 | async-start | bytes 2359296 | tf_op jit(solution)/shard_map/all_to_all | solution.py:118
  82.0 42.1 %collective-permute-start.6 = (bf16[144,1152]{1,0:T(8,128)(2,1)S(1)}, bf16[144,1152]{1,0:T(8,128)(2,1)S(1)}, u32[]{:S(2)}, u32[]{:S(2)}) collective-permute-start(bf16[144,1152]{1,0:T(8,128)(2,1)S(1)} %pad_maximum_fusion.18), channel_id=1, source_target_pairs={{0,4},{1,5},{2,6},{3,7},{4,0},{5,1},{6,2},{7,3},{8,12},{9,13},{10,... | collective-permute-start | bytes 995336 | tf_op jit(solution)/shard_map/ppermute | solution.py:23
  124.1 12.6 %collective-permute-start.7 = (bf16[144,1152]{1,0:T(8,128)(2,1)S(1)}, bf16[144,1152]{1,0:T(8,128)(2,1)S(1)}, u32[]{:S(2)}, u32[]{:S(2)}) collective-permute-start(bf16[144,1152]{1,0:T(8,128)(2,1)S(1)} %collective-permute-done.6), channel_id=1, source_target_pairs={{0,16},{8,24},{16,32},{24,40},{32,48},{40,56},{48,0},{56,8},{1,17}... | collective-permute-start | bytes 995336 | tf_op jit(solution)/shard_map/ppermute | solution.py:32
  128.6 30.4 %collective-permute-start.8 = (bf16[144,1152]{1,0:T(8,128)(2,1)S(1)}, bf16[144,1152]{1,0:T(8,128)(2,1)S(1)}, u32[]{:S(2)}, u32[]{:S(2)}) collective-permute-start(bf16[144,1152]{1,0:T(8,128)(2,1)S(1)} %collective-permute-done.6), channel_id=1, source_target_pairs={{0,32},{8,40},{16,48},{24,56},{32,0},{40,8},{48,16},{56,24},{1,33}... | collective-permute-start | bytes 995336 | tf_op jit(solution)/shard_map/ppermute | solution.py:32
  133.2 25.8 %collective-permute-start.9 = (bf16[144,1152]{1,0:T(8,128)(2,1)S(1)}, bf16[144,1152]{1,0:T(8,128)(2,1)S(1)}, u32[]{:S(2)}, u32[]{:S(2)}) collective-permute-start(bf16[144,1152]{1,0:T(8,128)(2,1)S(1)} %collective-permute-done.6), channel_id=1, source_target_pairs={{0,48},{8,56},{16,0},{24,8},{32,16},{40,24},{48,32},{56,40},{1,49}... | collective-permute-start | bytes 995336 | tf_op jit(solution)/shard_map/ppermute | solution.py:32
  159.1 16.6 %collective-permute-start.10 = (bf16[4,144,1152]{2,1,0:T(8,128)(2,1)S(1)}, bf16[4,144,1152]{2,1,0:T(8,128)(2,1)}, u32[]{:S(2)}, u32[]{:S(2)}) collective-permute-start(bf16[4,144,1152]{2,1,0:T(8,128)(2,1)S(1)} %pad_maximum_fusion.2), channel_id=1, source_target_pairs={{0,8},{8,0},{16,24},{24,16},{32,40},{40,32},{48,56},{56,48},{1,9},... | collective-permute-start | bytes 3981320 | tf_op jit(solution)/shard_map/ppermute | solution.py:27
  164.6 1.5 copy-start.7
  167.7 16.8 %collective-permute-start.3 = (bf16[64,1152]{1,0:T(8,128)(2,1)S(1)}, bf16[64,1152]{1,0:T(8,128)(2,1)S(1)}, u32[]{:S(2)}, u32[]{:S(2)}) collective-permute-start(bf16[64,1152]{1,0:T(8,128)(2,1)S(1)} %get-tuple-element.37), channel_id=1, source_target_pairs={{0,1},{1,2},{2,3},{3,4},{4,5},{5,6},{6,7},{7,0},{8,9},{9,10},{10,1... | collective-permute-start | bytes 442376 | tf_op jit(solution)/shard_map/ppermute | solution.py:23
  169.8 20.3 %collective-permute-start.4 = (bf16[64,1152]{1,0:T(8,128)(2,1)S(1)}, bf16[64,1152]{1,0:T(8,128)(2,1)S(1)}, u32[]{:S(2)}, u32[]{:S(2)}) collective-permute-start(bf16[64,1152]{1,0:T(8,128)(2,1)S(1)} %get-tuple-element.37), channel_id=1, source_target_pairs={{0,7},{1,0},{2,1},{3,2},{4,3},{5,4},{6,5},{7,6},{8,15},{9,8},{10,9... | collective-permute-start | bytes 442376 | tf_op jit(solution)/shard_map/ppermute | solution.py:23
  173.8 16.2 %collective-permute-start.5 = (bf16[64,1152]{1,0:T(8,128)(2,1)S(1)}, bf16[64,1152]{1,0:T(8,128)(2,1)S(1)}, u32[]{:S(2)}, u32[]{:S(2)}) collective-permute-start(bf16[64,1152]{1,0:T(8,128)(2,1)S(1)} %get-tuple-element.37), channel_id=1, source_target_pairs={{0,2},{1,3},{2,4},{3,5},{4,6},{5,7},{6,0},{7,1},{8,10},{9,11},{10,... | collective-permute-start | bytes 442376 | tf_op jit(solution)/shard_map/ppermute | solution.py:23
  178.0 12.1 %copy-start.4 = (bf16[4,72,1152]{2,1,0:T(8,128)(2,1)}, bf16[4,72,1152]{2,1,0:T(8,128)(2,1)S(1)}, u32[]{:S(2)}) copy-start(bf16[4,72,1152]{2,1,0:T(8,128)(2,1)S(1)} %get-tuple-element.28) | copy-start | bytes 1990660
  178.1 24.5 %collective-permute-start.15 = (bf16[64,1152]{1,0:T(8,128)(2,1)}, bf16[64,1152]{1,0:T(8,128)(2,1)S(1)}, u32[]{:S(2)}, u32[]{:S(2)}) collective-permute-start(bf16[64,1152]{1,0:T(8,128)(2,1)} %get-tuple-element.38), channel_id=1, source_target_pairs={{0,7},{1,0},{2,1},{3,2},{4,3},{5,4},{6,5},{7,6},{8,15},{9,8},{10,9... | collective-permute-start | bytes 442376 | tf_op jit(solution)/shard_map/ppermute | solution.py:23
  182.6 24.4 %collective-permute-start.16 = (bf16[64,1152]{1,0:T(8,128)(2,1)}, bf16[64,1152]{1,0:T(8,128)(2,1)S(1)}, u32[]{:S(2)}, u32[]{:S(2)}) collective-permute-start(bf16[64,1152]{1,0:T(8,128)(2,1)} %get-tuple-element.38), channel_id=1, source_target_pairs={{0,1},{1,2},{2,3},{3,4},{4,5},{5,6},{6,7},{7,0},{8,9},{9,10},{10,1... | collective-permute-start | bytes 442376 | tf_op jit(solution)/shard_map/ppermute | solution.py:23
  184.6 22.5 %collective-permute-start.17 = (bf16[64,1152]{1,0:T(8,128)(2,1)}, bf16[64,1152]{1,0:T(8,128)(2,1)S(1)}, u32[]{:S(2)}, u32[]{:S(2)}) collective-permute-start(bf16[64,1152]{1,0:T(8,128)(2,1)} %get-tuple-element.38), channel_id=1, source_target_pairs={{0,6},{1,7},{2,0},{3,1},{4,2},{5,3},{6,4},{7,5},{8,14},{9,15},{10,... | collective-permute-start | bytes 442376 | tf_op jit(solution)/shard_map/ppermute | solution.py:23
  195.3 12.7 %copy-start.2 = (bf16[4,72,1152]{2,1,0:T(8,128)(2,1)S(1)}, bf16[4,72,1152]{2,1,0:T(8,128)(2,1)}, u32[]{:S(2)}) copy-start(bf16[4,72,1152]{2,1,0:T(8,128)(2,1)} %get-tuple-element.26) | copy-start | bytes 1990660
  195.3 12.7 %copy-start.3 = (bf16[4,72,1152]{2,1,0:T(8,128)(2,1)S(1)}, bf16[4,72,1152]{2,1,0:T(8,128)(2,1)}, u32[]{:S(2)}) copy-start(bf16[4,72,1152]{2,1,0:T(8,128)(2,1)} %get-tuple-element.27) | copy-start | bytes 1990660
  197.2 20.3 %collective-permute-start.11 = (bf16[64,1152]{1,0:T(8,128)(2,1)}, bf16[64,1152]{1,0:T(8,128)(2,1)}, u32[]{:S(2)}, u32[]{:S(2)}) collective-permute-start(bf16[64,1152]{1,0:T(8,128)(2,1)} %get-tuple-element.33), channel_id=1, source_target_pairs={{0,7},{1,0},{2,1},{3,2},{4,3},{5,4},{6,5},{7,6},{8,15},{9,8},{10,9... | collective-permute-start | bytes 442376 | tf_op jit(solution)/shard_map/ppermute | solution.py:23
  200.6 18.9 %collective-permute-start.12 = (bf16[64,1152]{1,0:T(8,128)(2,1)}, bf16[64,1152]{1,0:T(8,128)(2,1)}, u32[]{:S(2)}, u32[]{:S(2)}) collective-permute-start(bf16[64,1152]{1,0:T(8,128)(2,1)} %get-tuple-element.35), channel_id=1, source_target_pairs={{0,1},{1,2},{2,3},{3,4},{4,5},{5,6},{6,7},{7,0},{8,9},{9,10},{10,1... | collective-permute-start | bytes 442376 | tf_op jit(solution)/shard_map/ppermute | solution.py:23
  202.5 17.0 %collective-permute-start.13 = (bf16[64,1152]{1,0:T(8,128)(2,1)}, bf16[64,1152]{1,0:T(8,128)(2,1)}, u32[]{:S(2)}, u32[]{:S(2)}) collective-permute-start(bf16[64,1152]{1,0:T(8,128)(2,1)} %get-tuple-element.34), channel_id=1, source_target_pairs={{0,6},{1,7},{2,0},{3,1},{4,2},{5,3},{6,4},{7,5},{8,14},{9,15},{10,... | collective-permute-start | bytes 442376 | tf_op jit(solution)/shard_map/ppermute | solution.py:23
  212.3 8.5 %collective-permute-start.18 = (bf16[64,1152]{1,0:T(8,128)(2,1)S(1)}, bf16[64,1152]{1,0:T(8,128)(2,1)S(1)}, u32[]{:S(2)}, u32[]{:S(2)}) collective-permute-start(bf16[64,1152]{1,0:T(8,128)(2,1)S(1)} %get-tuple-element.30), channel_id=1, source_target_pairs={{0,1},{1,2},{2,3},{3,4},{4,5},{5,6},{6,7},{7,0},{8,9},{9,10},{10,1... | collective-permute-start | bytes 442376 | tf_op jit(solution)/shard_map/ppermute | solution.py:23
  214.4 6.4 %collective-permute-start.19 = (bf16[64,1152]{1,0:T(8,128)(2,1)S(1)}, bf16[64,1152]{1,0:T(8,128)(2,1)S(1)}, u32[]{:S(2)}, u32[]{:S(2)}) collective-permute-start(bf16[64,1152]{1,0:T(8,128)(2,1)S(1)} %get-tuple-element.32), channel_id=1, source_target_pairs={{0,7},{1,0},{2,1},{3,2},{4,3},{5,4},{6,5},{7,6},{8,15},{9,8},{10,9... | collective-permute-start | bytes 442376 | tf_op jit(solution)/shard_map/ppermute | solution.py:23
  217.6 9.7 %collective-permute-start.20 = (bf16[64,1152]{1,0:T(8,128)(2,1)S(1)}, bf16[64,1152]{1,0:T(8,128)(2,1)S(1)}, u32[]{:S(2)}, u32[]{:S(2)}) collective-permute-start(bf16[64,1152]{1,0:T(8,128)(2,1)S(1)} %get-tuple-element.31), channel_id=1, source_target_pairs={{0,2},{1,3},{2,4},{3,5},{4,6},{5,7},{6,0},{7,1},{8,10},{9,11},{10,... | collective-permute-start | bytes 442376 | tf_op jit(solution)/shard_map/ppermute | solution.py:23
  227.3 30.4 %collective-permute-start.21 = (bf16[64,1152]{1,0:T(8,128)(2,1)S(1)}, bf16[64,1152]{1,0:T(8,128)(2,1)S(1)}, u32[]{:S(2)}, u32[]{:S(2)}) collective-permute-start(bf16[64,1152]{1,0:T(8,128)(2,1)S(1)} %fusion.47), channel_id=1, source_target_pairs={{0,64},{64,128},{128,192},{192,256},{256,320},{320,384},{384,448},... | collective-permute-start | bytes 442376 | tf_op jit(solution)/shard_map/ppermute | solution.py:23
  230.5 30.4 %collective-permute-start.14 = (bf16[64,1152]{1,0:T(8,128)(2,1)S(1)}, bf16[64,1152]{1,0:T(8,128)(2,1)S(1)}, u32[]{:S(2)}, u32[]{:S(2)}) collective-permute-start(bf16[64,1152]{1,0:T(8,128)(2,1)S(1)} %fusion.49), channel_id=1, source_target_pairs={{0,64},{64,128},{128,192},{192,256},{256,320},{320,384},{384,448},... | collective-permute-start | bytes 442376 | tf_op jit(solution)/shard_map/ppermute | solution.py:23
  (2 other events, 1.5 us)
where the time goes:
time: 263 us; the launch traced here: 262 us
  waiting for transfers between devices  130 us (49%)
  starting transfers between devices  87.7 us (33%)
  matrix products  21.2 us (8%)
  local copies, waits for them, and re-layouts  15 us (6%)
  other arithmetic  7.7 us (3%)
    ppermute x15, waiting for transfers between devices, rotate(): lax.ppermute(block, axis, [(i, (i + steps) % count) for i in range(count)])  69.8 us
    ppermute x15, starting transfers between devices, rotate(): lax.ppermute(block, axis, [(i, (i + steps) % count) for i in range(count)])  49.3 us
    ppermute x3, waiting for transfers between devices, flip(): lax.ppermute(block, axis, [(i, i ^ 1) for i in range(lax.axis_size(axis))])  35.7 us
    ppermute x3, waiting for transfers between devices, turn_z(): lax.ppermute(block, 'tm', [(i, (i + 2 * steps) % count) for i in range(co...  23.8 us
    ppermute x3, starting transfers between devices, flip(): lax.ppermute(block, axis, [(i, i ^ 1) for i in range(lax.axis_size(axis))])  12 us
    ppermute x3, starting transfers between devices, turn_z(): lax.ppermute(block, 'tm', [(i, (i + 2 * steps) % count) for i in range(co...  11 us
    dot_general x2, matrix products, feed_forward(): return jnp.dot(activated, down_w, preferred_element_type=F32)  9.4 us
    all_to_all x1, starting transfers between devices, body(): lax.all_to_all(outgoing.reshape(n_space, tokens, D), 'space', 0, 0, tiled...  7.12 us
  transfers between devices with their start and end apart: 24, of which 9 were waited for; matrix products, arithmetic and copies ran while one was open for 11% of the time, Pallas kernels for 0%

commit v1 on v0

--- a/solution.py
+++ b/solution.py
@@ -25,6 +25,16 @@
 
 def flip(block, axis):
     return lax.ppermute(block, axis, [(i, i ^ 1) for i in range(lax.axis_size(axis))])
+
+
+def mirrored(block, steps):
+    members, count = lax.axis_size("tm"), lax.axis_size("space")
+    route = [
+        (t * count + y, t * count + (y + (steps if t % 2 == 0 else -steps)) % count)
+        for t in range(members)
+        for y in range(count)
+    ]
+    return lax.ppermute(block, ("tm", "space"), route)
 
 
 def turn_z(block, steps):
@@ -93,7 +103,8 @@
     far = jnp.concatenate(
         [lax.dynamic_slice_in_dim(w, place * share, share, 0) for w in (up_own, down_own)], axis=0
     )
-    far = rotate(far, "space", n_space // 2)
+    for _ in range(2):
+        far = mirrored(far, n_space // 4)
 
     extended = jnp.concatenate([earlier, frames_in], axis=0).astype(F32)
     mixed_rows = (
@@ -123,26 +134,30 @@
     up_all = jnp.concatenate([up_own] + [w[:, :share].reshape(-1, D) for w in (far, far_more)])
     down_all = jnp.concatenate([down_own] + [w[:, share:].reshape(-1, D) for w in (far, far_more)])
 
-    visits = []
-    for frame, way in ((0, 1), (1, -1)):
-        visits.append([mlp_in[frame]])
-        for move in (way, -way, 2 * way):
-            visits[frame].append(rotate(mlp_in[frame], "space", move))
+    moves = (2, 1, -1)
+    visits = [mlp_in]
+    for move in moves:
+        visits.append(mirrored(mlp_in, move))
     next_in = []
-    for frame, way in ((0, 1), (1, -1)):
-        visitors = jnp.stack(visits[frame]).reshape(-1, D)
+    for frame in range(frames):
+        visitors = jnp.stack([visit[frame] for visit in visits]).reshape(-1, D)
         part = feed_forward(visitors, up_all, down_all).astype(BF16).reshape(-1, tokens, D)
         total = part[0].astype(F32)
-        for k, move in enumerate((way, -way, 2 * way)):
-            returned = rotate(part[k + 1], "space", -move)
+        for k, move in enumerate(moves):
+            returned = mirrored(part[k + 1], -move)
             if frame:
                 returned = after(returned, *next_in)
             total = total + returned.astype(F32)
         next_in.append((hidden_state[frame] + mod_table[5] * total).astype(BF16))
-    moved = []
-    for frame in range(frames):
-        moved.append(rotate(next_in[frame], "section", 1))
-    return jnp.stack(moved)[None]
+
+    sections = lax.axis_size("section")
+    crossed = lax.ppermute(
+        next_in[0], "section", [(s, (s + 4) % sections) for s in range(3, sections, 4)]
+    )
+    second = rotate(next_in[1], "section", 1)
+    first = jnp.where(lax.axis_index("section") % 4 == 3, crossed, next_in[0])
+    first = lax.ppermute(first, "section", [(s, s // 4 * 4 + (s + 1) % 4) for s in range(sections)])
+    return jnp.stack([first, second])[None]
 
 
 def solution(mesh):

time: 263 us -> 232 us (0.88)
  the two profiles are of different devices: /device:TPU:201 before, /device:TPU:24 now
where the time goes in v1:
time: 232 us; the launch traced here: 231 us
  waiting for transfers between devices  103 us (44%)
  starting transfers between devices  88.3 us (38%)
  matrix products  20.4 us (9%)
  local copies, waits for them, and re-layouts  12.1 us (5%)
  other arithmetic  7.23 us (3%)
    ppermute x11, starting transfers between devices, mirrored(): return lax.ppermute(block, ('tm', 'space'), route)  42.7 us
    ppermute x3, waiting for transfers between devices, flip(): lax.ppermute(block, axis, [(i, i ^ 1) for i in range(lax.axis_size(axis))])  38.2 us
    ppermute x1, waiting for transfers between devices, rotate(): lax.ppermute(block, axis, [(i, (i + steps) % count) for i in range(count)])  29.5 us
    ppermute x11, waiting for transfers between devices, mirrored(): return lax.ppermute(block, ('tm', 'space'), route)  18.4 us
    ppermute x3, starting transfers between devices, turn_z(): lax.ppermute(block, 'tm', [(i, (i + 2 * steps) % count) for i in range(co...  12.5 us
    all_to_all x1, starting transfers between devices, body(): lax.all_to_all(outgoing.reshape(n_space, tokens, D), 'space', 0, 0, tiled...  12.4 us
    all_to_all x1, waiting for transfers between devices, body(): parts = lax.all_to_all(attn_part, 'space', 0, 0, tiled=True)  9.97 us
    dot_general x2, matrix products, feed_forward(): return jnp.dot(activated, down_w, preferred_element_type=F32)  8.53 us
  transfers between devices with their start and end apart: 23, of which 9 were waited for; matrix products, arithmetic and copies ran while one was open for 12% of the time, Pallas kernels for 0%

profile of v1, /device:TPU:24, one launch (start us, length us, event | category | flops | bytes accessed | tf_op | source)
XLA Modules:
  0.0 231.3 jit_solution(17148930274232884771)
XLA Ops:
  6.1 12.4 %all-to-all-start = ((bf16[8,64,1152]{2,1,0:T(8,128)(2,1)}), bf16[8,64,1152]{2,1,0:T(8,128)(2,1)S(1)}, u32[]{:S(2)}, u32[]{:S(2)}) async-start(bf16[8,64,1152]{2,1,0:T(8,128)(2,1)} %bitcast.1), calls=%async_computation | async-start | bytes 2359296 | tf_op jit(solution)/shard_map/all_to_all | solution.py:120
  18.6 2.5 %collective-permute-start.1 = (bf16[4,72,1152]{2,1,0:T(8,128)(2,1)S(1)}, bf16[4,72,1152]{2,1,0:T(8,128)(2,1)S(1)}, u32[]{:S(2)}, u32[]{:S(2)}) collective-permute-start(bf16[4,72,1152]{2,1,0:T(8,128)(2,1)S(1)} %pad_maximum_fusion.11), channel_id=1, source_target_pairs={{0,1},{1,0},{2,3},{3,2},{4,5},{5,4},{6,7},{7,6},{8,9},{9,8},{10,11... | collective-permute-start | bytes 1990664 | tf_op jit(solution)/shard_map/ppermute | solution.py:27
  22.9 36.2 %collective-permute-done.1 = bf16[4,72,1152]{2,1,0:T(8,128)(2,1)S(1)} collective-permute-done((bf16[4,72,1152]{2,1,0:T(8,128)(2,1)S(1)}, bf16[4,72,1152]{2,1,0:T(8,128)(2,1)S(1)}, u32[]{:S(2)}, u32[]{:S(2)}) %collective-permute-start.1) | collective-permute-done | bytes 663584 | tf_op jit(solution)/shard_map/ppermute | solution.py:27
  61.1 5.7 %collective-permute-start.6 = (bf16[144,1152]{1,0:T(8,128)(2,1)S(1)}, bf16[144,1152]{1,0:T(8,128)(2,1)}, u32[]{:S(2)}, u32[]{:S(2)}) collective-permute-start(bf16[144,1152]{1,0:T(8,128)(2,1)S(1)} %pad_maximum_fusion.18), channel_id=1, source_target_pairs={{0,2},{1,3},{2,4},{3,5},{4,6},{5,7},{6,0},{7,1},{8,14},{9,15},{10,... | collective-permute-start | bytes 995336 | tf_op jit(solution)/shard_map/ppermute | solution.py:37
  66.8 8.2 %collective-permute-done.6 = bf16[144,1152]{1,0:T(8,128)(2,1)} collective-permute-done((bf16[144,1152]{1,0:T(8,128)(2,1)S(1)}, bf16[144,1152]{1,0:T(8,128)(2,1)}, u32[]{:S(2)}, u32[]{:S(2)}) %collective-permute-start.6) | collective-permute-done | bytes 331808 | tf_op jit(solution)/shard_map/ppermute | solution.py:37
  75.0 6.6 %collective-permute-start.7 = (bf16[144,1152]{1,0:T(8,128)(2,1)}, bf16[144,1152]{1,0:T(8,128)(2,1)}, u32[]{:S(2)}, u32[]{:S(2)}) collective-permute-start(bf16[144,1152]{1,0:T(8,128)(2,1)} %collective-permute-done.6), channel_id=1, source_target_pairs={{0,2},{1,3},{2,4},{3,5},{4,6},{5,7},{6,0},{7,1},{8,14},{9,15},{10,... | collective-permute-start | bytes 995336 | tf_op jit(solution)/shard_map/ppermute | solution.py:37
  84.1 2.0 convolution_convert_fusion.2
  90.5 2.2 convolution_convert_fusion.4
  92.7 2.6 %fusion.2 = bf16[512,1152]{1,0:T(8,128)(2,1)} fusion(f32[512,1152]{1,0:T(8,128)S(1)} %fusion.44, bf16[512,144]{0,1:T(8,128)(2,1)S(1)} %bitcast.146, bf16[4,144,1152]{2,1,0:T(8,128)(2,1)} %constant_dynamic-update-slice_fusion), kind=kOutput, calls=%fused_computation.3 | convolution fusion | flops 171048960 | bytes 4018176 | tf_op jit(solution)/shard_map/dot_general | solution.py:65
  95.3 3.9 %collective-permute-start.8 = (bf16[144,1152]{1,0:T(8,128)(2,1)}, bf16[144,1152]{1,0:T(8,128)(2,1)S(1)}, u32[]{:S(2)}, u32[]{:S(2)}) collective-permute-start(bf16[144,1152]{1,0:T(8,128)(2,1)} %collective-permute-done.7), channel_id=1, source_target_pairs={{0,16},{8,24},{16,32},{24,40},{32,48},{40,56},{48,0},{56,8},{1,17}... | collective-permute-start | bytes 995336 | tf_op jit(solution)/shard_map/ppermute | solution.py:42
  99.2 3.7 %collective-permute-start.9 = (bf16[144,1152]{1,0:T(8,128)(2,1)}, bf16[144,1152]{1,0:T(8,128)(2,1)S(1)}, u32[]{:S(2)}, u32[]{:S(2)}) collective-permute-start(bf16[144,1152]{1,0:T(8,128)(2,1)} %collective-permute-done.7), channel_id=1, source_target_pairs={{0,32},{8,40},{16,48},{24,56},{32,0},{40,8},{48,16},{56,24},{1,33}... | collective-permute-start | bytes 995336 | tf_op jit(solution)/shard_map/ppermute | solution.py:42
  103.0 4.8 %collective-permute-start.10 = (bf16[144,1152]{1,0:T(8,128)(2,1)}, bf16[144,1152]{1,0:T(8,128)(2,1)S(1)}, u32[]{:S(2)}, u32[]{:S(2)}) collective-permute-start(bf16[144,1152]{1,0:T(8,128)(2,1)} %collective-permute-done.7), channel_id=1, source_target_pairs={{0,48},{8,56},{16,0},{24,8},{32,16},{40,24},{48,32},{56,40},{1,49}... | collective-permute-start | bytes 995336 | tf_op jit(solution)/shard_map/ppermute | solution.py:42
  107.8 5.1 %all-to-all-start.1 = ((bf16[8,64,1152]{2,1,0:T(8,128)(2,1)}), bf16[8,64,1152]{2,1,0:T(8,128)(2,1)S(1)}, u32[]{:S(2)}, u32[]{:S(2)}) async-start(bf16[8,64,1152]{2,1,0:T(8,128)(2,1)} %bitcast.127), calls=%async_computation.1 | async-start | bytes 2359296 | tf_op jit(solution)/shard_map/all_to_all | solution.py:129
  112.9 6.6 %collective-permute-done.9 = bf16[144,1152]{1,0:T(8,128)(2,1)S(1)} collective-permute-done((bf16[144,1152]{1,0:T(8,128)(2,1)}, bf16[144,1152]{1,0:T(8,128)(2,1)S(1)}, u32[]{:S(2)}, u32[]{:S(2)}) %collective-permute-start.9) | collective-permute-done | bytes 331808 | tf_op jit(solution)/shard_map/ppermute | solution.py:42
  125.0 2.0 collective-permute-done.11
  126.9 2.5 %fusion.87 = (bf16[4,72,1152]{2,1,0:T(8,128)(2,1)}, bf16[4,72,1152]{2,1,0:T(8,128)(2,1)}) fusion(bf16[4,144,1152]{2,1,0:T(8,128)(2,1)} %collective-permute-done.11), kind=kLoop, calls=%fused_computation.134 | loop fusion | bytes 2654208 | tf_op jit(solution)/shard_map/slice | solution.py:134
  129.4 10.0 %all-to-all-done.1 = bf16[8,64,1152]{2,1,0:T(8,128)(2,1)S(1)} async-done(((bf16[8,64,1152]{2,1,0:T(8,128)(2,1)}), bf16[8,64,1152]{2,1,0:T(8,128)(2,1)S(1)}, u32[]{:S(2)}, u32[]{:S(2)}) %all-to-all-start.1) | async-done | bytes 1179680 | tf_op jit(solution)/shard_map/all_to_all | solution.py:129
  140.1 2.5 %collective-permute-start.3 = (bf16[2,64,1152]{2,1,0:T(8,128)(2,1)S(1)}, bf16[2,64,1152]{2,1,0:T(8,128)(2,1)S(1)}, u32[]{:S(2)}, u32[]{:S(2)}) collective-permute-start(bf16[2,64,1152]{2,1,0:T(8,128)(2,1)S(1)} %add_convert_fusion), channel_id=1, source_target_pairs={{0,2},{1,3},{2,4},{3,5},{4,6},{5,7},{6,0},{7,1},{8,14},{9,15},{10,... | collective-permute-start | bytes 884744 | tf_op jit(solution)/shard_map/ppermute | solution.py:37
  142.7 4.0 %collective-permute-start.4 = (bf16[2,64,1152]{2,1,0:T(8,128)(2,1)S(1)}, bf16[2,64,1152]{2,1,0:T(8,128)(2,1)S(1)}, u32[]{:S(2)}, u32[]{:S(2)}) collective-permute-start(bf16[2,64,1152]{2,1,0:T(8,128)(2,1)S(1)} %add_convert_fusion), channel_id=1, source_target_pairs={{0,1},{1,2},{2,3},{3,4},{4,5},{5,6},{6,7},{7,0},{8,15},{9,8},{10,9... | collective-permute-start | bytes 884744 | tf_op jit(solution)/shard_map/ppermute | solution.py:37
  148.7 6.8 %collective-permute-done.3 = bf16[2,64,1152]{2,1,0:T(8,128)(2,1)S(1)} collective-permute-done((bf16[2,64,1152]{2,1,0:T(8,128)(2,1)S(1)}, bf16[2,64,1152]{2,1,0:T(8,128)(2,1)S(1)}, u32[]{:S(2)}, u32[]{:S(2)}) %collective-permute-start.3) | collective-permute-done | bytes 294944 | tf_op jit(solution)/shard_map/ppermute | solution.py:37
  155.5 2.1 collective-permute-done.4
  159.4 4.3 %convolution_convert_fusion.1 = bf16[256,1152]{1,0:T(8,128)(2,1)S(1)} fusion(bf16[288,1152]{1,0:T(8,128)(2,1)} %bitcast.137, bf16[288,1152]{1,0:T(8,128)(2,1)S(1)} %bitcast.133, bf16[576,1152]{1,0:T(8,128)(2,1)} %bitcast.150, bf16[256,1152]{1,0:T(8,128)(2,1)} %bitcast.140, bf16[288,1152]{1,0:T(8,128)(2,1)} %bitcast.135, bf16[288,1152]{1,0:T(8,128)(2,1)S(1)} %bitcast.131, ...), kind=kOutput, calls=%fused_computation.7 | convolution fusion | flops 1377828864 | bytes 6488064 | tf_op jit(solution)/shard_map/dot_general | solution.py:72
  164.5 4.3 %collective-permute-start.12 = (bf16[64,1152]{1,0:T(8,128)(2,1)}, bf16[64,1152]{1,0:T(8,128)(2,1)}, u32[]{:S(2)}, u32[]{:S(2)}) collective-permute-start(bf16[64,1152]{1,0:T(8,128)(2,1)} %get-tuple-element.33), channel_id=1, source_target_pairs={{0,6},{1,7},{2,0},{3,1},{4,2},{5,3},{6,4},{7,5},{8,10},{9,11},{10,... | collective-permute-start | bytes 442376 | tf_op jit(solution)/shard_map/ppermute | solution.py:37
  168.9 5.1 %collective-permute-start.13 = (bf16[64,1152]{1,0:T(8,128)(2,1)}, bf16[64,1152]{1,0:T(8,128)(2,1)}, u32[]{:S(2)}, u32[]{:S(2)}) collective-permute-start(bf16[64,1152]{1,0:T(8,128)(2,1)} %get-tuple-element.35), channel_id=1, source_target_pairs={{0,7},{1,0},{2,1},{3,2},{4,3},{5,4},{6,5},{7,6},{8,9},{9,10},{10,1... | collective-permute-start | bytes 442376 | tf_op jit(solution)/shard_map/ppermute | solution.py:37
  174.0 2.1 collective-permute-start.14
  176.1 4.3 %convolution_convert_fusion = bf16[256,1152]{1,0:T(8,128)(2,1)S(1)} fusion(bf16[288,1152]{1,0:T(8,128)(2,1)} %bitcast.138, bf16[288,1152]{1,0:T(8,128)(2,1)S(1)} %bitcast.134, bf16[576,1152]{1,0:T(8,128)(2,1)} %bitcast.151, bf16[256,1152]{1,0:T(8,128)(2,1)} %bitcast.139, bf16[288,1152]{1,0:T(8,128)(2,1)} %bitcast.136, bf16[288,1152]{1,0:T(8,128)(2,1)S(1)} %bitcast.132, ...), kind=kOutput, calls=%fused_computation.6 | convolution fusion | flops 1377828864 | bytes 6488064 | tf_op jit(solution)/shard_map/dot_general | solution.py:72
  180.5 3.3 %collective-permute-start.17 = (bf16[64,1152]{1,0:T(8,128)(2,1)S(1)}, bf16[64,1152]{1,0:T(8,128)(2,1)S(1)}, u32[]{:S(2)}, u32[]{:S(2)}) collective-permute-start(bf16[64,1152]{1,0:T(8,128)(2,1)S(1)} %get-tuple-element.30), channel_id=1, source_target_pairs={{0,6},{1,7},{2,0},{3,1},{4,2},{5,3},{6,4},{7,5},{8,10},{9,11},{10,... | collective-permute-start | bytes 442376 | tf_op jit(solution)/shard_map/ppermute | solution.py:37
  183.8 2.5 %collective-permute-start.18 = (bf16[64,1152]{1,0:T(8,128)(2,1)S(1)}, bf16[64,1152]{1,0:T(8,128)(2,1)S(1)}, u32[]{:S(2)}, u32[]{:S(2)}) collective-permute-start(bf16[64,1152]{1,0:T(8,128)(2,1)S(1)} %get-tuple-element.32), channel_id=1, source_target_pairs={{0,7},{1,0},{2,1},{3,2},{4,3},{5,4},{6,5},{7,6},{8,9},{9,10},{10,1... | collective-permute-start | bytes 442376 | tf_op jit(solution)/shard_map/ppermute | solution.py:37
  186.3 4.6 %collective-permute-start.19 = (bf16[64,1152]{1,0:T(8,128)(2,1)S(1)}, bf16[64,1152]{1,0:T(8,128)(2,1)S(1)}, u32[]{:S(2)}, u32[]{:S(2)}) collective-permute-start(bf16[64,1152]{1,0:T(8,128)(2,1)S(1)} %get-tuple-element.31), channel_id=1, source_target_pairs={{0,1},{1,2},{2,3},{3,4},{4,5},{5,6},{6,7},{7,0},{8,15},{9,8},{10,9... | collective-permute-start | bytes 442376 | tf_op jit(solution)/shard_map/ppermute | solution.py:37
  194.2 3.4 %collective-permute-start.20 = (bf16[64,1152]{1,0:T(8,128)(2,1)S(1)}, bf16[64,1152]{1,0:T(8,128)(2,1)S(1)}, u32[]{:S(2)}, u32[]{:S(2)}) collective-permute-start(bf16[64,1152]{1,0:T(8,128)(2,1)S(1)} %fusion.47), channel_id=1, source_target_pairs={{0,64},{64,128},{128,192},{192,256},{256,320},{320,384},{384,448},... | collective-permute-start | bytes 442376 | tf_op jit(solution)/shard_map/ppermute | solution.py:23
  197.7 3.4 %collective-permute-start.16 = (bf16[64,1152]{1,0:T(8,128)(2,1)S(1)}, bf16[64,1152]{1,0:T(8,128)(2,1)S(1)}, u32[]{:S(2)}, u32[]{:S(2)}) collective-permute-start(bf16[64,1152]{1,0:T(8,128)(2,1)S(1)} %broadcast_select_fusion), channel_id=1, source_target_pairs={{0,64},{64,128},{128,192},{192,0},{256,320},{320,384},{384,448},{4... | collective-permute-start | bytes 442376 | tf_op jit(solution)/shard_map/ppermute | solution.py:159
  201.1 29.5 %collective-permute-done.20 = bf16[64,1152]{1,0:T(8,128)(2,1)S(1)} collective-permute-done((bf16[64,1152]{1,0:T(8,128)(2,1)S(1)}, bf16[64,1152]{1,0:T(8,128)(2,1)S(1)}, u32[]{:S(2)}, u32[]{:S(2)}) %collective-permute-start.20) | collective-permute-done | bytes 147488 | tf_op jit(solution)/shard_map/ppermute | solution.py:23
  (85 shorter events, 31.7 us)
Async XLA Ops:
  0.0 3.5 %copy-start = (bf16[1,1152,3,144]{1,3,2,0:T(8,128)(2,1)S(1)}, bf16[1,1152,3,144]{1,3,2,0:T(8,128)(2,1)}, u32[]{:S(2)}) copy-start(bf16[1,1152,3,144]{1,3,2,0:T(8,128)(2,1)} %param.10) | copy-start | bytes 2985988
  0.0 3.6 %copy-start.10 = (bf16[1,2,64,1152]{3,2,1,0:T(8,128)(2,1)S(1)}, bf16[1,2,64,1152]{3,2,1,0:T(8,128)(2,1)}, u32[]{:S(2)}) copy-start(bf16[1,2,64,1152]{3,2,1,0:T(8,128)(2,1)} %param.7) | copy-start | bytes 884740
  0.0 3.6 %collective-permute-start = (bf16[2,64,1152]{2,1,0:T(8,128)(2,1)}, bf16[2,64,1152]{2,1,0:T(8,128)(2,1)S(1)}, u32[]{:S(2)}, u32[]{:S(2)}) collective-permute-start(bf16[2,64,1152]{2,1,0:T(8,128)(2,1)} %bitcast.144), channel_id=1, source_target_pairs={{0,8},{8,16},{16,24},{24,32},{32,40},{40,48},{48,56},{1,9},{9,17},... | collective-permute-start | bytes 884744 | tf_op jit(solution)/shard_map/ppermute | solution.py:18
  6.1 12.4 %copy-start.3 = (bf16[1,144,1152]{2,1,0:T(8,128)(2,1)S(1)}, bf16[1,144,1152]{2,1,0:T(8,128)(2,1)}, u32[]{:S(2)}) copy-start(bf16[1,144,1152]{2,1,0:T(8,128)(2,1)} %param.11) | copy-start | bytes 995332
  6.1 77.3 %all-to-all-start = ((bf16[8,64,1152]{2,1,0:T(8,128)(2,1)}), bf16[8,64,1152]{2,1,0:T(8,128)(2,1)S(1)}, u32[]{:S(2)}, u32[]{:S(2)}) async-start(bf16[8,64,1152]{2,1,0:T(8,128)(2,1)} %bitcast.1), calls=%async_computation | async-start | bytes 2359296 | tf_op jit(solution)/shard_map/all_to_all | solution.py:120
  18.6 40.6 %collective-permute-start.1 = (bf16[4,72,1152]{2,1,0:T(8,128)(2,1)S(1)}, bf16[4,72,1152]{2,1,0:T(8,128)(2,1)S(1)}, u32[]{:S(2)}, u32[]{:S(2)}) collective-permute-start(bf16[4,72,1152]{2,1,0:T(8,128)(2,1)S(1)} %pad_maximum_fusion.11), channel_id=1, source_target_pairs={{0,1},{1,0},{2,3},{3,2},{4,5},{5,4},{6,7},{7,6},{8,9},{9,8},{10,11... | collective-permute-start | bytes 1990664 | tf_op jit(solution)/shard_map/ppermute | solution.py:27
  59.1 23.3 %collective-permute-start.2 = (bf16[4,72,1152]{2,1,0:T(8,128)(2,1)S(1)}, bf16[4,72,1152]{2,1,0:T(8,128)(2,1)S(1)}, u32[]{:S(2)}, u32[]{:S(2)}) collective-permute-start(bf16[4,72,1152]{2,1,0:T(8,128)(2,1)S(1)} %collective-permute-done.1), channel_id=1, source_target_pairs={{0,8},{8,0},{16,24},{24,16},{32,40},{40,32},{48,56},{56,48},{1,9},... | collective-permute-start | bytes 1990664 | tf_op jit(solution)/shard_map/ppermute | solution.py:27
  61.1 13.9 %collective-permute-start.6 = (bf16[144,1152]{1,0:T(8,128)(2,1)S(1)}, bf16[144,1152]{1,0:T(8,128)(2,1)}, u32[]{:S(2)}, u32[]{:S(2)}) collective-permute-start(bf16[144,1152]{1,0:T(8,128)(2,1)S(1)} %pad_maximum_fusion.18), channel_id=1, source_target_pairs={{0,2},{1,3},{2,4},{3,5},{4,6},{5,7},{6,0},{7,1},{8,14},{9,15},{10,... | collective-permute-start | bytes 995336 | tf_op jit(solution)/shard_map/ppermute | solution.py:37
  75.0 20.3 %collective-permute-start.7 = (bf16[144,1152]{1,0:T(8,128)(2,1)}, bf16[144,1152]{1,0:T(8,128)(2,1)}, u32[]{:S(2)}, u32[]{:S(2)}) collective-permute-start(bf16[144,1152]{1,0:T(8,128)(2,1)} %collective-permute-done.6), channel_id=1, source_target_pairs={{0,2},{1,3},{2,4},{3,5},{4,6},{5,7},{6,0},{7,1},{8,14},{9,15},{10,... | collective-permute-start | bytes 995336 | tf_op jit(solution)/shard_map/ppermute | solution.py:37
  86.1 0.9 copy-start.11
  95.3 17.6 %collective-permute-start.8 = (bf16[144,1152]{1,0:T(8,128)(2,1)}, bf16[144,1152]{1,0:T(8,128)(2,1)S(1)}, u32[]{:S(2)}, u32[]{:S(2)}) collective-permute-start(bf16[144,1152]{1,0:T(8,128)(2,1)} %collective-permute-done.7), channel_id=1, source_target_pairs={{0,16},{8,24},{16,32},{24,40},{32,48},{40,56},{48,0},{56,8},{1,17}... | collective-permute-start | bytes 995336 | tf_op jit(solution)/shard_map/ppermute | solution.py:42
  99.2 20.3 %collective-permute-start.9 = (bf16[144,1152]{1,0:T(8,128)(2,1)}, bf16[144,1152]{1,0:T(8,128)(2,1)S(1)}, u32[]{:S(2)}, u32[]{:S(2)}) collective-permute-start(bf16[144,1152]{1,0:T(8,128)(2,1)} %collective-permute-done.7), channel_id=1, source_target_pairs={{0,32},{8,40},{16,48},{24,56},{32,0},{40,8},{48,16},{56,24},{1,33}... | collective-permute-start | bytes 995336 | tf_op jit(solution)/shard_map/ppermute | solution.py:42
  103.0 16.6 %collective-permute-start.10 = (bf16[144,1152]{1,0:T(8,128)(2,1)}, bf16[144,1152]{1,0:T(8,128)(2,1)S(1)}, u32[]{:S(2)}, u32[]{:S(2)}) collective-permute-start(bf16[144,1152]{1,0:T(8,128)(2,1)} %collective-permute-done.7), channel_id=1, source_target_pairs={{0,48},{8,56},{16,0},{24,8},{32,16},{40,24},{48,32},{56,40},{1,49}... | collective-permute-start | bytes 995336 | tf_op jit(solution)/shard_map/ppermute | solution.py:42
  107.8 31.6 %all-to-all-start.1 = ((bf16[8,64,1152]{2,1,0:T(8,128)(2,1)}), bf16[8,64,1152]{2,1,0:T(8,128)(2,1)S(1)}, u32[]{:S(2)}, u32[]{:S(2)}) async-start(bf16[8,64,1152]{2,1,0:T(8,128)(2,1)} %bitcast.127), calls=%async_computation.1 | async-start | bytes 2359296 | tf_op jit(solution)/shard_map/all_to_all | solution.py:129
  112.9 6.6 %copy-start.7 = (bf16[144,1152]{1,0:T(8,128)(2,1)}, bf16[144,1152]{1,0:T(8,128)(2,1)S(1)}, u32[]{:S(2)}) copy-start(bf16[144,1152]{1,0:T(8,128)(2,1)S(1)} %collective-permute-done.8) | copy-start | bytes 995332
  121.8 5.1 %collective-permute-start.11 = (bf16[4,144,1152]{2,1,0:T(8,128)(2,1)S(1)}, bf16[4,144,1152]{2,1,0:T(8,128)(2,1)}, u32[]{:S(2)}, u32[]{:S(2)}) collective-permute-start(bf16[4,144,1152]{2,1,0:T(8,128)(2,1)S(1)} %pad_maximum_fusion.2), channel_id=1, source_target_pairs={{0,8},{8,0},{16,24},{24,16},{32,40},{40,32},{48,56},{56,48},{1,9},... | collective-permute-start | bytes 3981320 | tf_op jit(solution)/shard_map/ppermute | solution.py:27
  129.4 10.1 %copy-start.2 = (bf16[2,64,1152]{2,1,0:T(8,128)(2,1)S(1)}, bf16[2,64,1152]{2,1,0:T(8,128)(2,1)}, u32[]{:S(2)}) copy-start(bf16[2,64,1152]{2,1,0:T(8,128)(2,1)} %copy-done.1) | copy-start | bytes 884740
  140.1 15.3 %collective-permute-start.3 = (bf16[2,64,1152]{2,1,0:T(8,128)(2,1)S(1)}, bf16[2,64,1152]{2,1,0:T(8,128)(2,1)S(1)}, u32[]{:S(2)}, u32[]{:S(2)}) collective-permute-start(bf16[2,64,1152]{2,1,0:T(8,128)(2,1)S(1)} %add_convert_fusion), channel_id=1, source_target_pairs={{0,2},{1,3},{2,4},{3,5},{4,6},{5,7},{6,0},{7,1},{8,14},{9,15},{10,... | collective-permute-start | bytes 884744 | tf_op jit(solution)/shard_map/ppermute | solution.py:37
  142.7 15.0 %collective-permute-start.4 = (bf16[2,64,1152]{2,1,0:T(8,128)(2,1)S(1)}, bf16[2,64,1152]{2,1,0:T(8,128)(2,1)S(1)}, u32[]{:S(2)}, u32[]{:S(2)}) collective-permute-start(bf16[2,64,1152]{2,1,0:T(8,128)(2,1)S(1)} %add_convert_fusion), channel_id=1, source_target_pairs={{0,1},{1,2},{2,3},{3,4},{4,5},{5,6},{6,7},{7,0},{8,15},{9,8},{10,9... | collective-permute-start | bytes 884744 | tf_op jit(solution)/shard_map/ppermute | solution.py:37
  146.7 11.0 %collective-permute-start.5 = (bf16[2,64,1152]{2,1,0:T(8,128)(2,1)S(1)}, bf16[2,64,1152]{2,1,0:T(8,128)(2,1)S(1)}, u32[]{:S(2)}, u32[]{:S(2)}) collective-permute-start(bf16[2,64,1152]{2,1,0:T(8,128)(2,1)S(1)} %add_convert_fusion), channel_id=1, source_target_pairs={{0,7},{1,0},{2,1},{3,2},{4,3},{5,4},{6,5},{7,6},{8,9},{9,10},{10,1... | collective-permute-start | bytes 884744 | tf_op jit(solution)/shard_map/ppermute | solution.py:37
  157.7 1.2 copy-start.4
  157.7 1.7 copy-start.5
  163.7 12.4 %copy-start.6 = (bf16[256,1152]{1,0:T(8,128)(2,1)}, bf16[256,1152]{1,0:T(8,128)(2,1)S(1)}, u32[]{:S(2)}) copy-start(bf16[256,1152]{1,0:T(8,128)(2,1)S(1)} %convolution_convert_fusion.1) | copy-start | bytes 1769476
  164.5 21.7 %collective-permute-start.12 = (bf16[64,1152]{1,0:T(8,128)(2,1)}, bf16[64,1152]{1,0:T(8,128)(2,1)}, u32[]{:S(2)}, u32[]{:S(2)}) collective-permute-start(bf16[64,1152]{1,0:T(8,128)(2,1)} %get-tuple-element.33), channel_id=1, source_target_pairs={{0,6},{1,7},{2,0},{3,1},{4,2},{5,3},{6,4},{7,5},{8,10},{9,11},{10,... | collective-permute-start | bytes 442376 | tf_op jit(solution)/shard_map/ppermute | solution.py:37
  168.9 22.0 %collective-permute-start.13 = (bf16[64,1152]{1,0:T(8,128)(2,1)}, bf16[64,1152]{1,0:T(8,128)(2,1)}, u32[]{:S(2)}, u32[]{:S(2)}) collective-permute-start(bf16[64,1152]{1,0:T(8,128)(2,1)} %get-tuple-element.35), channel_id=1, source_target_pairs={{0,7},{1,0},{2,1},{3,2},{4,3},{5,4},{6,5},{7,6},{8,9},{9,10},{10,1... | collective-permute-start | bytes 442376 | tf_op jit(solution)/shard_map/ppermute | solution.py:37
  174.0 16.9 %collective-permute-start.14 = (bf16[64,1152]{1,0:T(8,128)(2,1)}, bf16[64,1152]{1,0:T(8,128)(2,1)}, u32[]{:S(2)}, u32[]{:S(2)}) collective-permute-start(bf16[64,1152]{1,0:T(8,128)(2,1)} %get-tuple-element.34), channel_id=1, source_target_pairs={{0,1},{1,2},{2,3},{3,4},{4,5},{5,6},{6,7},{7,0},{8,15},{9,8},{10,9... | collective-permute-start | bytes 442376 | tf_op jit(solution)/shard_map/ppermute | solution.py:37
  180.5 12.4 %collective-permute-start.17 = (bf16[64,1152]{1,0:T(8,128)(2,1)S(1)}, bf16[64,1152]{1,0:T(8,128)(2,1)S(1)}, u32[]{:S(2)}, u32[]{:S(2)}) collective-permute-start(bf16[64,1152]{1,0:T(8,128)(2,1)S(1)} %get-tuple-element.30), channel_id=1, source_target_pairs={{0,6},{1,7},{2,0},{3,1},{4,2},{5,3},{6,4},{7,5},{8,10},{9,11},{10,... | collective-permute-start | bytes 442376 | tf_op jit(solution)/shard_map/ppermute | solution.py:37
  183.8 10.3 %collective-permute-start.18 = (bf16[64,1152]{1,0:T(8,128)(2,1)S(1)}, bf16[64,1152]{1,0:T(8,128)(2,1)S(1)}, u32[]{:S(2)}, u32[]{:S(2)}) collective-permute-start(bf16[64,1152]{1,0:T(8,128)(2,1)S(1)} %get-tuple-element.32), channel_id=1, source_target_pairs={{0,7},{1,0},{2,1},{3,2},{4,3},{5,4},{6,5},{7,6},{8,9},{9,10},{10,1... | collective-permute-start | bytes 442376 | tf_op jit(solution)/shard_map/ppermute | solution.py:37
  186.3 7.8 %collective-permute-start.19 = (bf16[64,1152]{1,0:T(8,128)(2,1)S(1)}, bf16[64,1152]{1,0:T(8,128)(2,1)S(1)}, u32[]{:S(2)}, u32[]{:S(2)}) collective-permute-start(bf16[64,1152]{1,0:T(8,128)(2,1)S(1)} %get-tuple-element.31), channel_id=1, source_target_pairs={{0,1},{1,2},{2,3},{3,4},{4,5},{5,6},{6,7},{7,0},{8,15},{9,8},{10,9... | collective-permute-start | bytes 442376 | tf_op jit(solution)/shard_map/ppermute | solution.py:37
  192.1 5.5 %collective-permute-start.15 = (bf16[64,1152]{1,0:T(8,128)(2,1)S(1)}, bf16[64,1152]{1,0:T(8,128)(2,1)S(1)}, u32[]{:S(2)}, u32[]{:S(2)}) collective-permute-start(bf16[64,1152]{1,0:T(8,128)(2,1)S(1)} %fusion.49), channel_id=1, source_target_pairs={{192,448},{448,704},{704,192},{193,449},{449,705},{705,193},{194,4... | collective-permute-start | bytes 442376 | tf_op jit(solution)/shard_map/ppermute | solution.py:154
  194.2 36.3 %collective-permute-start.20 = (bf16[64,1152]{1,0:T(8,128)(2,1)S(1)}, bf16[64,1152]{1,0:T(8,128)(2,1)S(1)}, u32[]{:S(2)}, u32[]{:S(2)}) collective-permute-start(bf16[64,1152]{1,0:T(8,128)(2,1)S(1)} %fusion.47), channel_id=1, source_target_pairs={{0,64},{64,128},{128,192},{192,256},{256,320},{320,384},{384,448},... | collective-permute-start | bytes 442376 | tf_op jit(solution)/shard_map/ppermute | solution.py:23
  197.7 32.9 %collective-permute-start.16 = (bf16[64,1152]{1,0:T(8,128)(2,1)S(1)}, bf16[64,1152]{1,0:T(8,128)(2,1)S(1)}, u32[]{:S(2)}, u32[]{:S(2)}) collective-permute-start(bf16[64,1152]{1,0:T(8,128)(2,1)S(1)} %broadcast_select_fusion), channel_id=1, source_target_pairs={{0,64},{64,128},{128,192},{192,0},{256,320},{320,384},{384,448},{4... | collective-permute-start | bytes 442376 | tf_op jit(solution)/shard_map/ppermute | solution.py:159
  (3 other events, 2.3 us)

commit v2 on v1

--- a/solution.py
+++ b/solution.py
@@ -103,8 +103,7 @@
     far = jnp.concatenate(
         [lax.dynamic_slice_in_dim(w, place * share, share, 0) for w in (up_own, down_own)], axis=0
     )
-    for _ in range(2):
-        far = mirrored(far, n_space // 4)
+    far = rotate(far, "space", n_space // 2)
 
     extended = jnp.concatenate([earlier, frames_in], axis=0).astype(F32)
     mixed_rows = (
@@ -151,13 +150,19 @@
         next_in.append((hidden_state[frame] + mod_table[5] * total).astype(BF16))
 
     sections = lax.axis_size("section")
-    crossed = lax.ppermute(
-        next_in[0], "section", [(s, (s + 4) % sections) for s in range(3, sections, 4)]
-    )
-    second = rotate(next_in[1], "section", 1)
-    first = jnp.where(lax.axis_index("section") % 4 == 3, crossed, next_in[0])
-    first = lax.ppermute(first, "section", [(s, s // 4 * 4 + (s + 1) % 4) for s in range(sections)])
-    return jnp.stack([first, second])[None]
+    at_end = lax.axis_index("section") % 4 == 3
+    handed = []
+    for frame in range(frames):
+        crossed = lax.ppermute(
+            next_in[frame], "section", [(s, (s + 4) % sections) for s in range(3, sections, 4)]
+        )
+        leaving = jnp.where(at_end, crossed, next_in[frame])
+        handed.append(
+            lax.ppermute(
+                leaving, "section", [(s, s // 4 * 4 + (s + 1) % 4) for s in range(sections)]
+            )
+        )
+    return jnp.stack(handed)[None]
 
 
 def solution(mesh):

time: 232 us -> 230 us (level)
  the two profiles are of different devices: /device:TPU:24 before, /device:TPU:32 now
where the time goes in v2:
time: 230 us; the launch traced here: 229 us
  waiting for transfers between devices  100 us (43%)
  starting transfers between devices  87 us (38%)
  matrix products  20.4 us (9%)
  local copies, waits for them, and re-layouts  12.1 us (5%)
  other arithmetic  8.83 us (4%)
    ppermute x3, waiting for transfers between devices, flip(): lax.ppermute(block, axis, [(i, i ^ 1) for i in range(lax.axis_size(axis))])  38.5 us
    ppermute x9, starting transfers between devices, mirrored(): return lax.ppermute(block, ('tm', 'space'), route)  32.5 us
    ppermute x2, waiting for transfers between devices, body(): lax.ppermute(leaving, 'section', [(s, s // 4 * 4 + (s + 1) % 4) for s in...  32.2 us
    ppermute x3, starting transfers between devices, turn_z(): lax.ppermute(block, 'tm', [(i, (i + 2 * steps) % count) for i in range(co...  12.5 us
    all_to_all x1, starting transfers between devices, body(): lax.all_to_all(outgoing.reshape(n_space, tokens, D), 'space', 0, 0, tiled...  12.3 us
    ppermute x9, waiting for transfers between devices, mirrored(): return lax.ppermute(block, ('tm', 'space'), route)  10.8 us
    all_to_all x1, waiting for transfers between devices, body(): parts = lax.all_to_all(attn_part, 'space', 0, 0, tiled=True)  10.5 us
    all_to_all x1, starting transfers between devices, body(): parts = lax.all_to_all(attn_part, 'space', 0, 0, tiled=True)  10.2 us
  transfers between devices with their start and end apart: 23, of which 11 were waited for; matrix products, arithmetic and copies ran while one was open for 13% of the time, Pallas kernels for 0%

profile of v2, /device:TPU:32, one launch (start us, length us, event | category | flops | bytes accessed | tf_op | source)
XLA Modules:
  0.0 229.1 jit_solution(18097935110742776638)
XLA Ops:
  6.1 12.3 %all-to-all-start = ((bf16[8,64,1152]{2,1,0:T(8,128)(2,1)}), bf16[8,64,1152]{2,1,0:T(8,128)(2,1)S(1)}, u32[]{:S(2)}, u32[]{:S(2)}) async-start(bf16[8,64,1152]{2,1,0:T(8,128)(2,1)} %bitcast.1), calls=%async_computation | async-start | bytes 2359296 | tf_op jit(solution)/shard_map/all_to_all | solution.py:119
  19.3 2.5 %collective-permute-start.1 = (bf16[4,72,1152]{2,1,0:T(8,128)(2,1)}, bf16[4,72,1152]{2,1,0:T(8,128)(2,1)S(1)}, u32[]{:S(2)}, u32[]{:S(2)}) collective-permute-start(bf16[4,72,1152]{2,1,0:T(8,128)(2,1)} %pad_maximum_fusion.11), channel_id=1, source_target_pairs={{0,1},{1,0},{2,3},{3,2},{4,5},{5,4},{6,7},{7,6},{8,9},{9,8},{10,11... | collective-permute-start | bytes 1990664 | tf_op jit(solution)/shard_map/ppermute | solution.py:27
  22.7 36.5 %collective-permute-done.1 = bf16[4,72,1152]{2,1,0:T(8,128)(2,1)S(1)} collective-permute-done((bf16[4,72,1152]{2,1,0:T(8,128)(2,1)}, bf16[4,72,1152]{2,1,0:T(8,128)(2,1)S(1)}, u32[]{:S(2)}, u32[]{:S(2)}) %collective-permute-start.1) | collective-permute-done | bytes 663584 | tf_op jit(solution)/shard_map/ppermute | solution.py:27
  62.9 3.3 %collective-permute-start.6 = (bf16[144,1152]{1,0:T(8,128)(2,1)}, bf16[144,1152]{1,0:T(8,128)(2,1)}, u32[]{:S(2)}, u32[]{:S(2)}) collective-permute-start(bf16[144,1152]{1,0:T(8,128)(2,1)} %pad_maximum_fusion.18), channel_id=1, source_target_pairs={{0,4},{1,5},{2,6},{3,7},{4,0},{5,1},{6,2},{7,3},{8,12},{9,13},{10,... | collective-permute-start | bytes 995336 | tf_op jit(solution)/shard_map/ppermute | solution.py:23
  68.8 2.0 convolution_convert_fusion.2
  75.2 2.2 convolution_convert_fusion.4
  77.3 2.6 %fusion.2 = bf16[512,1152]{1,0:T(8,128)(2,1)} fusion(f32[512,1152]{1,0:T(8,128)S(1)} %fusion.44, bf16[512,144]{0,1:T(8,128)(2,1)S(1)} %bitcast.146, bf16[4,144,1152]{2,1,0:T(8,128)(2,1)} %constant_dynamic-update-slice_fusion), kind=kOutput, calls=%fused_computation.3 | convolution fusion | flops 171048960 | bytes 4018176 | tf_op jit(solution)/shard_map/dot_general | solution.py:65
  79.9 3.5 %collective-permute-done.6 = bf16[144,1152]{1,0:T(8,128)(2,1)} collective-permute-done((bf16[144,1152]{1,0:T(8,128)(2,1)}, bf16[144,1152]{1,0:T(8,128)(2,1)}, u32[]{:S(2)}, u32[]{:S(2)}) %collective-permute-start.6) | collective-permute-done | bytes 331808 | tf_op jit(solution)/shard_map/ppermute | solution.py:23
  83.4 3.9 %collective-permute-start.7 = (bf16[144,1152]{1,0:T(8,128)(2,1)}, bf16[144,1152]{1,0:T(8,128)(2,1)S(1)}, u32[]{:S(2)}, u32[]{:S(2)}) collective-permute-start(bf16[144,1152]{1,0:T(8,128)(2,1)} %collective-permute-done.6), channel_id=1, source_target_pairs={{0,16},{8,24},{16,32},{24,40},{32,48},{40,56},{48,0},{56,8},{1,17}... | collective-permute-start | bytes 995336 | tf_op jit(solution)/shard_map/ppermute | solution.py:42
  87.3 3.7 %collective-permute-start.8 = (bf16[144,1152]{1,0:T(8,128)(2,1)}, bf16[144,1152]{1,0:T(8,128)(2,1)S(1)}, u32[]{:S(2)}, u32[]{:S(2)}) collective-permute-start(bf16[144,1152]{1,0:T(8,128)(2,1)} %collective-permute-done.6), channel_id=1, source_target_pairs={{0,32},{8,40},{16,48},{24,56},{32,0},{40,8},{48,16},{56,24},{1,33}... | collective-permute-start | bytes 995336 | tf_op jit(solution)/shard_map/ppermute | solution.py:42
  91.1 4.8 %collective-permute-start.9 = (bf16[144,1152]{1,0:T(8,128)(2,1)}, bf16[144,1152]{1,0:T(8,128)(2,1)S(1)}, u32[]{:S(2)}, u32[]{:S(2)}) collective-permute-start(bf16[144,1152]{1,0:T(8,128)(2,1)} %collective-permute-done.6), channel_id=1, source_target_pairs={{0,48},{8,56},{16,0},{24,8},{32,16},{40,24},{48,32},{56,40},{1,49}... | collective-permute-start | bytes 995336 | tf_op jit(solution)/shard_map/ppermute | solution.py:42
  95.9 10.2 %all-to-all-start.1 = ((bf16[8,64,1152]{2,1,0:T(8,128)(2,1)}), bf16[8,64,1152]{2,1,0:T(8,128)(2,1)S(1)}, u32[]{:S(2)}, u32[]{:S(2)}) async-start(bf16[8,64,1152]{2,1,0:T(8,128)(2,1)} %bitcast.127), calls=%async_computation.1 | async-start | bytes 2359296 | tf_op jit(solution)/shard_map/all_to_all | solution.py:128
  106.1 4.7 %collective-permute-done.8 = bf16[144,1152]{1,0:T(8,128)(2,1)S(1)} collective-permute-done((bf16[144,1152]{1,0:T(8,128)(2,1)}, bf16[144,1152]{1,0:T(8,128)(2,1)S(1)}, u32[]{:S(2)}, u32[]{:S(2)}) %collective-permute-start.8) | collective-permute-done | bytes 331808 | tf_op jit(solution)/shard_map/ppermute | solution.py:42
  118.2 2.5 %fusion.87 = (bf16[4,72,1152]{2,1,0:T(8,128)(2,1)}, bf16[4,72,1152]{2,1,0:T(8,128)(2,1)}) fusion(bf16[4,144,1152]{2,1,0:T(8,128)(2,1)} %collective-permute-done.10), kind=kLoop, calls=%fused_computation.135 | loop fusion | bytes 2654208 | tf_op jit(solution)/shard_map/slice | solution.py:133
  120.7 10.5 %all-to-all-done.1 = bf16[8,64,1152]{2,1,0:T(8,128)(2,1)S(1)} async-done(((bf16[8,64,1152]{2,1,0:T(8,128)(2,1)}), bf16[8,64,1152]{2,1,0:T(8,128)(2,1)S(1)}, u32[]{:S(2)}, u32[]{:S(2)}) %all-to-all-start.1) | async-done | bytes 1179680 | tf_op jit(solution)/shard_map/all_to_all | solution.py:128
  132.0 4.1 %collective-permute-start.3 = (bf16[2,64,1152]{2,1,0:T(8,128)(2,1)S(1)}, bf16[2,64,1152]{2,1,0:T(8,128)(2,1)S(1)}, u32[]{:S(2)}, u32[]{:S(2)}) collective-permute-start(bf16[2,64,1152]{2,1,0:T(8,128)(2,1)S(1)} %add_convert_fusion), channel_id=1, source_target_pairs={{0,2},{1,3},{2,4},{3,5},{4,6},{5,7},{6,0},{7,1},{8,14},{9,15},{10,... | collective-permute-start | bytes 884744 | tf_op jit(solution)/shard_map/ppermute | solution.py:37
  136.1 2.0 collective-permute-start.4
  138.1 5.1 %collective-permute-start.5 = (bf16[2,64,1152]{2,1,0:T(8,128)(2,1)S(1)}, bf16[2,64,1152]{2,1,0:T(8,128)(2,1)S(1)}, u32[]{:S(2)}, u32[]{:S(2)}) collective-permute-start(bf16[2,64,1152]{2,1,0:T(8,128)(2,1)S(1)} %add_convert_fusion), channel_id=1, source_target_pairs={{0,7},{1,0},{2,1},{3,2},{4,3},{5,4},{6,5},{7,6},{8,9},{9,10},{10,1... | collective-permute-start | bytes 884744 | tf_op jit(solution)/shard_map/ppermute | solution.py:37
  143.2 2.5 %collective-permute-done.3 = bf16[2,64,1152]{2,1,0:T(8,128)(2,1)S(1)} collective-permute-done((bf16[2,64,1152]{2,1,0:T(8,128)(2,1)S(1)}, bf16[2,64,1152]{2,1,0:T(8,128)(2,1)S(1)}, u32[]{:S(2)}, u32[]{:S(2)}) %collective-permute-start.3) | collective-permute-done | bytes 294944 | tf_op jit(solution)/shard_map/ppermute | solution.py:37
  145.7 5.8 %collective-permute-done.4 = bf16[2,64,1152]{2,1,0:T(8,128)(2,1)S(1)} collective-permute-done((bf16[2,64,1152]{2,1,0:T(8,128)(2,1)S(1)}, bf16[2,64,1152]{2,1,0:T(8,128)(2,1)S(1)}, u32[]{:S(2)}, u32[]{:S(2)}) %collective-permute-start.4) | collective-permute-done | bytes 294944 | tf_op jit(solution)/shard_map/ppermute | solution.py:37
  153.4 4.3 %convolution_convert_fusion.1 = bf16[256,1152]{1,0:T(8,128)(2,1)S(1)} fusion(bf16[288,1152]{1,0:T(8,128)(2,1)} %bitcast.137, bf16[288,1152]{1,0:T(8,128)(2,1)S(1)} %bitcast.133, bf16[576,1152]{1,0:T(8,128)(2,1)} %bitcast.150, bf16[256,1152]{1,0:T(8,128)(2,1)} %bitcast.140, bf16[288,1152]{1,0:T(8,128)(2,1)} %bitcast.135, bf16[288,1152]{1,0:T(8,128)(2,1)S(1)} %bitcast.131, ...), kind=kOutput, calls=%fused_computation.7 | convolution fusion | flops 1377828864 | bytes 6488064 | tf_op jit(solution)/shard_map/dot_general | solution.py:72
  158.5 3.7 %collective-permute-start.11 = (bf16[64,1152]{1,0:T(8,128)(2,1)}, bf16[64,1152]{1,0:T(8,128)(2,1)}, u32[]{:S(2)}, u32[]{:S(2)}) collective-permute-start(bf16[64,1152]{1,0:T(8,128)(2,1)} %get-tuple-element.33), channel_id=1, source_target_pairs={{0,6},{1,7},{2,0},{3,1},{4,2},{5,3},{6,4},{7,5},{8,10},{9,11},{10,... | collective-permute-start | bytes 442376 | tf_op jit(solution)/shard_map/ppermute | solution.py:37
  162.2 3.5 %collective-permute-start.12 = (bf16[64,1152]{1,0:T(8,128)(2,1)}, bf16[64,1152]{1,0:T(8,128)(2,1)}, u32[]{:S(2)}, u32[]{:S(2)}) collective-permute-start(bf16[64,1152]{1,0:T(8,128)(2,1)} %get-tuple-element.35), channel_id=1, source_target_pairs={{0,7},{1,0},{2,1},{3,2},{4,3},{5,4},{6,5},{7,6},{8,9},{9,10},{10,1... | collective-permute-start | bytes 442376 | tf_op jit(solution)/shard_map/ppermute | solution.py:37
  165.7 2.5 %collective-permute-start.13 = (bf16[64,1152]{1,0:T(8,128)(2,1)}, bf16[64,1152]{1,0:T(8,128)(2,1)}, u32[]{:S(2)}, u32[]{:S(2)}) collective-permute-start(bf16[64,1152]{1,0:T(8,128)(2,1)} %get-tuple-element.34), channel_id=1, source_target_pairs={{0,1},{1,2},{2,3},{3,4},{4,5},{5,6},{6,7},{7,0},{8,15},{9,8},{10,9... | collective-permute-start | bytes 442376 | tf_op jit(solution)/shard_map/ppermute | solution.py:37
  168.3 4.3 %convolution_convert_fusion = bf16[256,1152]{1,0:T(8,128)(2,1)S(1)} fusion(bf16[288,1152]{1,0:T(8,128)(2,1)} %bitcast.138, bf16[288,1152]{1,0:T(8,128)(2,1)S(1)} %bitcast.134, bf16[576,1152]{1,0:T(8,128)(2,1)} %bitcast.151, bf16[256,1152]{1,0:T(8,128)(2,1)} %bitcast.139, bf16[288,1152]{1,0:T(8,128)(2,1)} %bitcast.136, bf16[288,1152]{1,0:T(8,128)(2,1)S(1)} %bitcast.132, ...), kind=kOutput, calls=%fused_computation.6 | convolution fusion | flops 1377828864 | bytes 6488064 | tf_op jit(solution)/shard_map/dot_general | solution.py:72
  172.6 5.7 %collective-permute-start.16 = (bf16[64,1152]{1,0:T(8,128)(2,1)S(1)}, bf16[64,1152]{1,0:T(8,128)(2,1)S(1)}, u32[]{:S(2)}, u32[]{:S(2)}) collective-permute-start(bf16[64,1152]{1,0:T(8,128)(2,1)S(1)} %get-tuple-element.30), channel_id=1, source_target_pairs={{0,6},{1,7},{2,0},{3,1},{4,2},{5,3},{6,4},{7,5},{8,10},{9,11},{10,... | collective-permute-start | bytes 442376 | tf_op jit(solution)/shard_map/ppermute | solution.py:37
  180.2 3.9 %collective-permute-start.18 = (bf16[64,1152]{1,0:T(8,128)(2,1)S(1)}, bf16[64,1152]{1,0:T(8,128)(2,1)S(1)}, u32[]{:S(2)}, u32[]{:S(2)}) collective-permute-start(bf16[64,1152]{1,0:T(8,128)(2,1)S(1)} %get-tuple-element.31), channel_id=1, source_target_pairs={{0,1},{1,2},{2,3},{3,4},{4,5},{5,6},{6,7},{7,0},{8,15},{9,8},{10,9... | collective-permute-start | bytes 442376 | tf_op jit(solution)/shard_map/ppermute | solution.py:37
  186.5 2.0 collective-permute-done.18
  189.3 3.4 %collective-permute-start.15 = (bf16[64,1152]{1,0:T(8,128)(2,1)S(1)}, bf16[64,1152]{1,0:T(8,128)(2,1)S(1)}, u32[]{:S(2)}, u32[]{:S(2)}) collective-permute-start(bf16[64,1152]{1,0:T(8,128)(2,1)S(1)} %broadcast_select_fusion.1), channel_id=1, source_target_pairs={{0,64},{64,128},{128,192},{192,0},{256,320},{320,384},{384,448},{4... | collective-permute-start | bytes 442376 | tf_op jit(solution)/shard_map/ppermute | solution.py:161
  192.7 3.4 %collective-permute-start.20 = (bf16[64,1152]{1,0:T(8,128)(2,1)S(1)}, bf16[64,1152]{1,0:T(8,128)(2,1)S(1)}, u32[]{:S(2)}, u32[]{:S(2)}) collective-permute-start(bf16[64,1152]{1,0:T(8,128)(2,1)S(1)} %broadcast_select_fusion), channel_id=1, source_target_pairs={{0,64},{64,128},{128,192},{192,0},{256,320},{320,384},{384,448},{4... | collective-permute-start | bytes 442376 | tf_op jit(solution)/shard_map/ppermute | solution.py:161
  196.1 26.0 %collective-permute-done.15 = bf16[64,1152]{1,0:T(8,128)(2,1)S(1)} collective-permute-done((bf16[64,1152]{1,0:T(8,128)(2,1)S(1)}, bf16[64,1152]{1,0:T(8,128)(2,1)S(1)}, u32[]{:S(2)}, u32[]{:S(2)}) %collective-permute-start.15) | collective-permute-done | bytes 147488 | tf_op jit(solution)/shard_map/ppermute | solution.py:161
  222.2 6.2 %collective-permute-done.20 = bf16[64,1152]{1,0:T(8,128)(2,1)S(1)} collective-permute-done((bf16[64,1152]{1,0:T(8,128)(2,1)S(1)}, bf16[64,1152]{1,0:T(8,128)(2,1)S(1)}, u32[]{:S(2)}, u32[]{:S(2)}) %collective-permute-start.20) | collective-permute-done | bytes 147488 | tf_op jit(solution)/shard_map/ppermute | solution.py:161
  (86 shorter events, 35.0 us)
Async XLA Ops:
  0.0 3.5 %copy-start = (bf16[1,1152,3,144]{1,3,2,0:T(8,128)(2,1)S(1)}, bf16[1,1152,3,144]{1,3,2,0:T(8,128)(2,1)}, u32[]{:S(2)}) copy-start(bf16[1,1152,3,144]{1,3,2,0:T(8,128)(2,1)} %param.10) | copy-start | bytes 2985988
  0.0 3.6 %copy-start.10 = (bf16[1,2,64,1152]{3,2,1,0:T(8,128)(2,1)S(1)}, bf16[1,2,64,1152]{3,2,1,0:T(8,128)(2,1)}, u32[]{:S(2)}) copy-start(bf16[1,2,64,1152]{3,2,1,0:T(8,128)(2,1)} %param.7) | copy-start | bytes 884740
  0.0 3.6 %collective-permute-start = (bf16[2,64,1152]{2,1,0:T(8,128)(2,1)}, bf16[2,64,1152]{2,1,0:T(8,128)(2,1)S(1)}, u32[]{:S(2)}, u32[]{:S(2)}) collective-permute-start(bf16[2,64,1152]{2,1,0:T(8,128)(2,1)} %bitcast.144), channel_id=1, source_target_pairs={{0,8},{8,16},{16,24},{24,32},{32,40},{40,48},{48,56},{1,9},{9,17},... | collective-permute-start | bytes 884744 | tf_op jit(solution)/shard_map/ppermute | solution.py:18
  6.1 12.3 %copy-start.3 = (bf16[1,144,1152]{2,1,0:T(8,128)(2,1)S(1)}, bf16[1,144,1152]{2,1,0:T(8,128)(2,1)}, u32[]{:S(2)}) copy-start(bf16[1,144,1152]{2,1,0:T(8,128)(2,1)} %param.11) | copy-start | bytes 995332
  6.1 61.9 %all-to-all-start = ((bf16[8,64,1152]{2,1,0:T(8,128)(2,1)}), bf16[8,64,1152]{2,1,0:T(8,128)(2,1)S(1)}, u32[]{:S(2)}, u32[]{:S(2)}) async-start(bf16[8,64,1152]{2,1,0:T(8,128)(2,1)} %bitcast.1), calls=%async_computation | async-start | bytes 2359296 | tf_op jit(solution)/shard_map/all_to_all | solution.py:119
  19.3 40.0 %collective-permute-start.1 = (bf16[4,72,1152]{2,1,0:T(8,128)(2,1)}, bf16[4,72,1152]{2,1,0:T(8,128)(2,1)S(1)}, u32[]{:S(2)}, u32[]{:S(2)}) collective-permute-start(bf16[4,72,1152]{2,1,0:T(8,128)(2,1)} %pad_maximum_fusion.11), channel_id=1, source_target_pairs={{0,1},{1,0},{2,3},{3,2},{4,5},{5,4},{6,7},{7,6},{8,9},{9,8},{10,11... | collective-permute-start | bytes 1990664 | tf_op jit(solution)/shard_map/ppermute | solution.py:27
  59.2 7.9 %collective-permute-start.2 = (bf16[4,72,1152]{2,1,0:T(8,128)(2,1)S(1)}, bf16[4,72,1152]{2,1,0:T(8,128)(2,1)S(1)}, u32[]{:S(2)}, u32[]{:S(2)}) collective-permute-start(bf16[4,72,1152]{2,1,0:T(8,128)(2,1)S(1)} %collective-permute-done.1), channel_id=1, source_target_pairs={{0,8},{8,0},{16,24},{24,16},{32,40},{40,32},{48,56},{56,48},{1,9},... | collective-permute-start | bytes 1990664 | tf_op jit(solution)/shard_map/ppermute | solution.py:27
  62.9 20.5 %collective-permute-start.6 = (bf16[144,1152]{1,0:T(8,128)(2,1)}, bf16[144,1152]{1,0:T(8,128)(2,1)}, u32[]{:S(2)}, u32[]{:S(2)}) collective-permute-start(bf16[144,1152]{1,0:T(8,128)(2,1)} %pad_maximum_fusion.18), channel_id=1, source_target_pairs={{0,4},{1,5},{2,6},{3,7},{4,0},{5,1},{6,2},{7,3},{8,12},{9,13},{10,... | collective-permute-start | bytes 995336 | tf_op jit(solution)/shard_map/ppermute | solution.py:23
  70.7 0.9 copy-start.11
  83.4 22.7 %collective-permute-start.7 = (bf16[144,1152]{1,0:T(8,128)(2,1)}, bf16[144,1152]{1,0:T(8,128)(2,1)S(1)}, u32[]{:S(2)}, u32[]{:S(2)}) collective-permute-start(bf16[144,1152]{1,0:T(8,128)(2,1)} %collective-permute-done.6), channel_id=1, source_target_pairs={{0,16},{8,24},{16,32},{24,40},{32,48},{40,56},{48,0},{56,8},{1,17}... | collective-permute-start | bytes 995336 | tf_op jit(solution)/shard_map/ppermute | solution.py:42
  87.3 23.5 %collective-permute-start.8 = (bf16[144,1152]{1,0:T(8,128)(2,1)}, bf16[144,1152]{1,0:T(8,128)(2,1)S(1)}, u32[]{:S(2)}, u32[]{:S(2)}) collective-permute-start(bf16[144,1152]{1,0:T(8,128)(2,1)} %collective-permute-done.6), channel_id=1, source_target_pairs={{0,32},{8,40},{16,48},{24,56},{32,0},{40,8},{48,16},{56,24},{1,33}... | collective-permute-start | bytes 995336 | tf_op jit(solution)/shard_map/ppermute | solution.py:42
  91.1 19.7 %collective-permute-start.9 = (bf16[144,1152]{1,0:T(8,128)(2,1)}, bf16[144,1152]{1,0:T(8,128)(2,1)S(1)}, u32[]{:S(2)}, u32[]{:S(2)}) collective-permute-start(bf16[144,1152]{1,0:T(8,128)(2,1)} %collective-permute-done.6), channel_id=1, source_target_pairs={{0,48},{8,56},{16,0},{24,8},{32,16},{40,24},{48,32},{56,40},{1,49}... | collective-permute-start | bytes 995336 | tf_op jit(solution)/shard_map/ppermute | solution.py:42
  95.9 35.3 %all-to-all-start.1 = ((bf16[8,64,1152]{2,1,0:T(8,128)(2,1)}), bf16[8,64,1152]{2,1,0:T(8,128)(2,1)S(1)}, u32[]{:S(2)}, u32[]{:S(2)}) async-start(bf16[8,64,1152]{2,1,0:T(8,128)(2,1)} %bitcast.127), calls=%async_computation.1 | async-start | bytes 2359296 | tf_op jit(solution)/shard_map/all_to_all | solution.py:128
  106.1 4.7 %copy-start.7 = (bf16[144,1152]{1,0:T(8,128)(2,1)}, bf16[144,1152]{1,0:T(8,128)(2,1)S(1)}, u32[]{:S(2)}) copy-start(bf16[144,1152]{1,0:T(8,128)(2,1)S(1)} %collective-permute-done.7) | copy-start | bytes 995332
  113.1 5.1 %collective-permute-start.10 = (bf16[4,144,1152]{2,1,0:T(8,128)(2,1)S(1)}, bf16[4,144,1152]{2,1,0:T(8,128)(2,1)}, u32[]{:S(2)}, u32[]{:S(2)}) collective-permute-start(bf16[4,144,1152]{2,1,0:T(8,128)(2,1)S(1)} %pad_maximum_fusion.2), channel_id=1, source_target_pairs={{0,8},{8,0},{16,24},{24,16},{32,40},{40,32},{48,56},{56,48},{1,9},... | collective-permute-start | bytes 3981320 | tf_op jit(solution)/shard_map/ppermute | solution.py:27
  120.7 10.7 %copy-start.2 = (bf16[2,64,1152]{2,1,0:T(8,128)(2,1)S(1)}, bf16[2,64,1152]{2,1,0:T(8,128)(2,1)}, u32[]{:S(2)}) copy-start(bf16[2,64,1152]{2,1,0:T(8,128)(2,1)} %copy-done.1) | copy-start | bytes 884740
  132.0 13.8 %collective-permute-start.3 = (bf16[2,64,1152]{2,1,0:T(8,128)(2,1)S(1)}, bf16[2,64,1152]{2,1,0:T(8,128)(2,1)S(1)}, u32[]{:S(2)}, u32[]{:S(2)}) collective-permute-start(bf16[2,64,1152]{2,1,0:T(8,128)(2,1)S(1)} %add_convert_fusion), channel_id=1, source_target_pairs={{0,2},{1,3},{2,4},{3,5},{4,6},{5,7},{6,0},{7,1},{8,14},{9,15},{10,... | collective-permute-start | bytes 884744 | tf_op jit(solution)/shard_map/ppermute | solution.py:37
  136.1 15.5 %collective-permute-start.4 = (bf16[2,64,1152]{2,1,0:T(8,128)(2,1)S(1)}, bf16[2,64,1152]{2,1,0:T(8,128)(2,1)S(1)}, u32[]{:S(2)}, u32[]{:S(2)}) collective-permute-start(bf16[2,64,1152]{2,1,0:T(8,128)(2,1)S(1)} %add_convert_fusion), channel_id=1, source_target_pairs={{0,1},{1,2},{2,3},{3,4},{4,5},{5,6},{6,7},{7,0},{8,15},{9,8},{10,9... | collective-permute-start | bytes 884744 | tf_op jit(solution)/shard_map/ppermute | solution.py:37
  138.1 13.5 %collective-permute-start.5 = (bf16[2,64,1152]{2,1,0:T(8,128)(2,1)S(1)}, bf16[2,64,1152]{2,1,0:T(8,128)(2,1)S(1)}, u32[]{:S(2)}, u32[]{:S(2)}) collective-permute-start(bf16[2,64,1152]{2,1,0:T(8,128)(2,1)S(1)} %add_convert_fusion), channel_id=1, source_target_pairs={{0,7},{1,0},{2,1},{3,2},{4,3},{5,4},{6,5},{7,6},{8,9},{9,10},{10,1... | collective-permute-start | bytes 884744 | tf_op jit(solution)/shard_map/ppermute | solution.py:37
  151.6 1.2 copy-start.4
  151.7 1.7 copy-start.5
  157.6 10.6 %copy-start.6 = (bf16[256,1152]{1,0:T(8,128)(2,1)}, bf16[256,1152]{1,0:T(8,128)(2,1)S(1)}, u32[]{:S(2)}) copy-start(bf16[256,1152]{1,0:T(8,128)(2,1)S(1)} %convolution_convert_fusion.1) | copy-start | bytes 1769476
  158.5 21.8 %collective-permute-start.11 = (bf16[64,1152]{1,0:T(8,128)(2,1)}, bf16[64,1152]{1,0:T(8,128)(2,1)}, u32[]{:S(2)}, u32[]{:S(2)}) collective-permute-start(bf16[64,1152]{1,0:T(8,128)(2,1)} %get-tuple-element.33), channel_id=1, source_target_pairs={{0,6},{1,7},{2,0},{3,1},{4,2},{5,3},{6,4},{7,5},{8,10},{9,11},{10,... | collective-permute-start | bytes 442376 | tf_op jit(solution)/shard_map/ppermute | solution.py:37
  162.2 21.9 %collective-permute-start.12 = (bf16[64,1152]{1,0:T(8,128)(2,1)}, bf16[64,1152]{1,0:T(8,128)(2,1)}, u32[]{:S(2)}, u32[]{:S(2)}) collective-permute-start(bf16[64,1152]{1,0:T(8,128)(2,1)} %get-tuple-element.35), channel_id=1, source_target_pairs={{0,7},{1,0},{2,1},{3,2},{4,3},{5,4},{6,5},{7,6},{8,9},{9,10},{10,1... | collective-permute-start | bytes 442376 | tf_op jit(solution)/shard_map/ppermute | solution.py:37
  165.7 18.4 %collective-permute-start.13 = (bf16[64,1152]{1,0:T(8,128)(2,1)}, bf16[64,1152]{1,0:T(8,128)(2,1)}, u32[]{:S(2)}, u32[]{:S(2)}) collective-permute-start(bf16[64,1152]{1,0:T(8,128)(2,1)} %get-tuple-element.34), channel_id=1, source_target_pairs={{0,1},{1,2},{2,3},{3,4},{4,5},{5,6},{6,7},{7,0},{8,15},{9,8},{10,9... | collective-permute-start | bytes 442376 | tf_op jit(solution)/shard_map/ppermute | solution.py:37
  172.6 13.5 %collective-permute-start.16 = (bf16[64,1152]{1,0:T(8,128)(2,1)S(1)}, bf16[64,1152]{1,0:T(8,128)(2,1)S(1)}, u32[]{:S(2)}, u32[]{:S(2)}) collective-permute-start(bf16[64,1152]{1,0:T(8,128)(2,1)S(1)} %get-tuple-element.30), channel_id=1, source_target_pairs={{0,6},{1,7},{2,0},{3,1},{4,2},{5,3},{6,4},{7,5},{8,10},{9,11},{10,... | collective-permute-start | bytes 442376 | tf_op jit(solution)/shard_map/ppermute | solution.py:37
  178.3 8.2 %collective-permute-start.17 = (bf16[64,1152]{1,0:T(8,128)(2,1)S(1)}, bf16[64,1152]{1,0:T(8,128)(2,1)S(1)}, u32[]{:S(2)}, u32[]{:S(2)}) collective-permute-start(bf16[64,1152]{1,0:T(8,128)(2,1)S(1)} %get-tuple-element.32), channel_id=1, source_target_pairs={{0,7},{1,0},{2,1},{3,2},{4,3},{5,4},{6,5},{7,6},{8,9},{9,10},{10,1... | collective-permute-start | bytes 442376 | tf_op jit(solution)/shard_map/ppermute | solution.py:37
  180.2 8.2 %collective-permute-start.18 = (bf16[64,1152]{1,0:T(8,128)(2,1)S(1)}, bf16[64,1152]{1,0:T(8,128)(2,1)S(1)}, u32[]{:S(2)}, u32[]{:S(2)}) collective-permute-start(bf16[64,1152]{1,0:T(8,128)(2,1)S(1)} %get-tuple-element.31), channel_id=1, source_target_pairs={{0,1},{1,2},{2,3},{3,4},{4,5},{5,6},{6,7},{7,0},{8,15},{9,8},{10,9... | collective-permute-start | bytes 442376 | tf_op jit(solution)/shard_map/ppermute | solution.py:37
  185.4 3.8 %collective-permute-start.14 = (bf16[64,1152]{1,0:T(8,128)(2,1)S(1)}, bf16[64,1152]{1,0:T(8,128)(2,1)S(1)}, u32[]{:S(2)}, u32[]{:S(2)}) collective-permute-start(bf16[64,1152]{1,0:T(8,128)(2,1)S(1)} %fusion.49), channel_id=1, source_target_pairs={{192,448},{448,704},{704,192},{193,449},{449,705},{705,193},{194,4... | collective-permute-start | bytes 442376 | tf_op jit(solution)/shard_map/ppermute | solution.py:156
  188.6 4.1 %collective-permute-start.19 = (bf16[64,1152]{1,0:T(8,128)(2,1)S(1)}, bf16[64,1152]{1,0:T(8,128)(2,1)S(1)}, u32[]{:S(2)}, u32[]{:S(2)}) collective-permute-start(bf16[64,1152]{1,0:T(8,128)(2,1)S(1)} %fusion.47), channel_id=1, source_target_pairs={{192,448},{448,704},{704,192},{193,449},{449,705},{705,193},{194,4... | collective-permute-start | bytes 442376 | tf_op jit(solution)/shard_map/ppermute | solution.py:156
  189.3 32.9 %collective-permute-start.15 = (bf16[64,1152]{1,0:T(8,128)(2,1)S(1)}, bf16[64,1152]{1,0:T(8,128)(2,1)S(1)}, u32[]{:S(2)}, u32[]{:S(2)}) collective-permute-start(bf16[64,1152]{1,0:T(8,128)(2,1)S(1)} %broadcast_select_fusion.1), channel_id=1, source_target_pairs={{0,64},{64,128},{128,192},{192,0},{256,320},{320,384},{384,448},{4... | collective-permute-start | bytes 442376 | tf_op jit(solution)/shard_map/ppermute | solution.py:161
  192.7 35.6 %collective-permute-start.20 = (bf16[64,1152]{1,0:T(8,128)(2,1)S(1)}, bf16[64,1152]{1,0:T(8,128)(2,1)S(1)}, u32[]{:S(2)}, u32[]{:S(2)}) collective-permute-start(bf16[64,1152]{1,0:T(8,128)(2,1)S(1)} %broadcast_select_fusion), channel_id=1, source_target_pairs={{0,64},{64,128},{128,192},{192,0},{256,320},{320,384},{384,448},{4... | collective-permute-start | bytes 442376 | tf_op jit(solution)/shard_map/ppermute | solution.py:161
  (3 other events, 2.3 us)

commit v3 on v1

--- a/solution.py
+++ b/solution.py
@@ -103,8 +103,7 @@
     far = jnp.concatenate(
         [lax.dynamic_slice_in_dim(w, place * share, share, 0) for w in (up_own, down_own)], axis=0
     )
-    for _ in range(2):
-        far = mirrored(far, n_space // 4)
+    far = rotate(far, "space", n_space // 2)
 
     extended = jnp.concatenate([earlier, frames_in], axis=0).astype(F32)
     mixed_rows = (
@@ -138,25 +137,26 @@
     visits = [mlp_in]
     for move in moves:
         visits.append(mirrored(mlp_in, move))
-    next_in = []
-    for frame in range(frames):
-        visitors = jnp.stack([visit[frame] for visit in visits]).reshape(-1, D)
-        part = feed_forward(visitors, up_all, down_all).astype(BF16).reshape(-1, tokens, D)
-        total = part[0].astype(F32)
-        for k, move in enumerate(moves):
-            returned = mirrored(part[k + 1], -move)
-            if frame:
-                returned = after(returned, *next_in)
-            total = total + returned.astype(F32)
-        next_in.append((hidden_state[frame] + mod_table[5] * total).astype(BF16))
+    part = feed_forward(jnp.stack(visits).reshape(-1, D), up_all, down_all)
+    part = part.astype(BF16).reshape(-1, frames, tokens, D)
+    mlp_sum = part[0].astype(F32)
+    for k, move in enumerate(moves):
+        mlp_sum = mlp_sum + mirrored(part[k + 1], -move).astype(F32)
+    layer_out = (hidden_state + mod_table[5] * mlp_sum).astype(BF16)
 
     sections = lax.axis_size("section")
-    crossed = lax.ppermute(
-        next_in[0], "section", [(s, (s + 4) % sections) for s in range(3, sections, 4)]
-    )
-    second = rotate(next_in[1], "section", 1)
-    first = jnp.where(lax.axis_index("section") % 4 == 3, crossed, next_in[0])
-    first = lax.ppermute(first, "section", [(s, s // 4 * 4 + (s + 1) % 4) for s in range(sections)])
+    place_x = lax.axis_index("section") % 4
+    along_x = [(s, s // 4 * 4 + (s + 1) % 4) for s in range(sections)]
+
+    def crossing(block, x):
+        return lax.ppermute(block, "section", [(s, (s + 4) % sections) for s in range(x, sections, 4)])
+
+    second = lax.ppermute(layer_out[1], "section", along_x)
+    crossed = crossing(layer_out[0], 3)
+    first = jnp.where(place_x == 3, crossed, layer_out[0])
+    first = lax.ppermute(first, "section", along_x)
+    crossed = crossing(second, 0)
+    second = jnp.where(place_x == 0, crossed, second)
     return jnp.stack([first, second])[None]
 
 

time: 232 us -> 240 us (1.034)
  the two profiles are of different devices: /device:TPU:24 before, /device:TPU:64 now
where the time goes in v3:
time: 240 us; the launch traced here: 239 us
  waiting for transfers between devices  133 us (55%)
  starting transfers between devices  72.9 us (30%)
  matrix products  15.6 us (6%)
  local copies, waits for them, and re-layouts  11.1 us (5%)
  other arithmetic  6.21 us (3%)
    ppermute x3, waiting for transfers between devices, flip(): lax.ppermute(block, axis, [(i, i ^ 1) for i in range(lax.axis_size(axis))])  38.6 us
    ppermute x1, waiting for transfers between devices, rotate(): lax.ppermute(block, axis, [(i, (i + steps) % count) for i in range(count)])  36.4 us
    ppermute x3, waiting for transfers between devices, turn_z(): lax.ppermute(block, 'tm', [(i, (i + 2 * steps) % count) for i in range(co...  23.6 us
    ppermute x6, waiting for transfers between devices, mirrored(): return lax.ppermute(block, ('tm', 'space'), route)  17.5 us
    ppermute x6, starting transfers between devices, mirrored(): return lax.ppermute(block, ('tm', 'space'), route)  17 us
    ppermute x2, starting transfers between devices, crossing(): lax.ppermute(block, 'section', [(s, (s + 4) % sections) for s in range(x,...  10.8 us
    ppermute x3, starting transfers between devices, turn_z(): lax.ppermute(block, 'tm', [(i, (i + 2 * steps) % count) for i in range(co...  9.57 us
    ppermute x1, starting transfers between devices, rotate(): lax.ppermute(block, axis, [(i, (i + steps) % count) for i in range(count)])  7.84 us
  transfers between devices with their start and end apart: 20, of which 15 were waited for; matrix products, arithmetic and copies ran while one was open for 5% of the time, Pallas kernels for 0%

profile of v3, /device:TPU:64, one launch (start us, length us, event | category | flops | bytes accessed | tf_op | source)
XLA Modules:
  0.0 239.3 jit_solution(4458812096590432924)
XLA Ops:
  0.0 2.0 collective-permute-start
  3.8 4.6 %collective-permute-done = bf16[2,64,1152]{2,1,0:T(8,128)(2,1)S(1)} collective-permute-done((bf16[2,64,1152]{2,1,0:T(8,128)(2,1)}, bf16[2,64,1152]{2,1,0:T(8,128)(2,1)S(1)}, u32[]{:S(2)}, u32[]{:S(2)}) %collective-permute-start) | collective-permute-done | bytes 294944 | tf_op jit(solution)/shard_map/ppermute | solution.py:18
  11.4 7.1 %all-to-all-start = ((bf16[8,64,1152]{2,1,0:T(8,128)(2,1)}), bf16[8,64,1152]{2,1,0:T(8,128)(2,1)S(1)}, u32[]{:S(2)}, u32[]{:S(2)}) async-start(bf16[8,64,1152]{2,1,0:T(8,128)(2,1)} %bitcast.1), calls=%async_computation | async-start | bytes 2359296 | tf_op jit(solution)/shard_map/all_to_all | solution.py:119
  18.6 3.9 %collective-permute-start.1 = (bf16[4,72,1152]{2,1,0:T(8,128)(2,1)S(1)}, bf16[4,72,1152]{2,1,0:T(8,128)(2,1)}, u32[]{:S(2)}, u32[]{:S(2)}) collective-permute-start(bf16[4,72,1152]{2,1,0:T(8,128)(2,1)S(1)} %pad_maximum_fusion.2), channel_id=1, source_target_pairs={{0,1},{1,0},{2,3},{3,2},{4,5},{5,4},{6,7},{7,6},{8,9},{9,8},{10,11... | collective-permute-start | bytes 1990664 | tf_op jit(solution)/shard_map/ppermute | solution.py:27
  22.5 38.2 %collective-permute-done.1 = bf16[4,72,1152]{2,1,0:T(8,128)(2,1)} collective-permute-done((bf16[4,72,1152]{2,1,0:T(8,128)(2,1)S(1)}, bf16[4,72,1152]{2,1,0:T(8,128)(2,1)}, u32[]{:S(2)}, u32[]{:S(2)}) %collective-permute-start.1) | collective-permute-done | bytes 663584 | tf_op jit(solution)/shard_map/ppermute | solution.py:27
  62.6 2.0 constant_dynamic-update-slice_fusion.1
  65.0 2.0 constant_dynamic-update-slice_fusion
  68.6 2.0 convolution_convert_fusion.1
  72.2 2.2 convolution_convert_fusion.3
  77.0 2.6 %fusion.2 = bf16[512,1152]{1,0:T(8,128)(2,1)} fusion(f32[512,1152]{1,0:T(8,128)S(1)} %fusion.46, bf16[512,144]{0,1:T(8,128)(2,1)S(1)} %bitcast.151, bf16[4,144,1152]{2,1,0:T(8,128)(2,1)} %constant_dynamic-update-slice_fusion), kind=kOutput, calls=%fused_computation.4 | convolution fusion | flops 171048960 | bytes 4018176 | tf_op jit(solution)/shard_map/dot_general | solution.py:65
  79.6 5.8 %all-to-all-start.1 = ((bf16[8,64,1152]{2,1,0:T(8,128)(2,1)}), bf16[8,64,1152]{2,1,0:T(8,128)(2,1)}, u32[]{:S(2)}, u32[]{:S(2)}) async-start(bf16[8,64,1152]{2,1,0:T(8,128)(2,1)} %bitcast.23), calls=%async_computation.1 | async-start | bytes 2359296 | tf_op jit(solution)/shard_map/all_to_all | solution.py:128
  87.3 7.8 %collective-permute-start.6 = (bf16[144,1152]{1,0:T(8,128)(2,1)S(1)}, bf16[144,1152]{1,0:T(8,128)(2,1)S(1)}, u32[]{:S(2)}, u32[]{:S(2)}) collective-permute-start(bf16[144,1152]{1,0:T(8,128)(2,1)S(1)} %pad_maximum_fusion.3), channel_id=1, source_target_pairs={{0,4},{1,5},{2,6},{3,7},{4,0},{5,1},{6,2},{7,3},{8,12},{9,13},{10,... | collective-permute-start | bytes 995336 | tf_op jit(solution)/shard_map/ppermute | solution.py:23
  95.2 36.4 %collective-permute-done.6 = bf16[144,1152]{1,0:T(8,128)(2,1)S(1)} collective-permute-done((bf16[144,1152]{1,0:T(8,128)(2,1)S(1)}, bf16[144,1152]{1,0:T(8,128)(2,1)S(1)}, u32[]{:S(2)}, u32[]{:S(2)}) %collective-permute-start.6) | collective-permute-done | bytes 331808 | tf_op jit(solution)/shard_map/ppermute | solution.py:23
  131.6 4.3 %collective-permute-start.7 = (bf16[144,1152]{1,0:T(8,128)(2,1)S(1)}, bf16[144,1152]{1,0:T(8,128)(2,1)S(1)}, u32[]{:S(2)}, u32[]{:S(2)}) collective-permute-start(bf16[144,1152]{1,0:T(8,128)(2,1)S(1)} %collective-permute-done.6), channel_id=1, source_target_pairs={{0,16},{8,24},{16,32},{24,40},{32,48},{40,56},{48,0},{56,8},{1,17}... | collective-permute-start | bytes 995336 | tf_op jit(solution)/shard_map/ppermute | solution.py:42
  137.8 3.4 %collective-permute-start.9 = (bf16[144,1152]{1,0:T(8,128)(2,1)S(1)}, bf16[144,1152]{1,0:T(8,128)(2,1)S(1)}, u32[]{:S(2)}, u32[]{:S(2)}) collective-permute-start(bf16[144,1152]{1,0:T(8,128)(2,1)S(1)} %collective-permute-done.6), channel_id=1, source_target_pairs={{0,48},{8,56},{16,0},{24,8},{32,16},{40,24},{48,32},{56,40},{1,49}... | collective-permute-start | bytes 995336 | tf_op jit(solution)/shard_map/ppermute | solution.py:42
  141.2 17.1 %collective-permute-done.7 = bf16[144,1152]{1,0:T(8,128)(2,1)S(1)} collective-permute-done((bf16[144,1152]{1,0:T(8,128)(2,1)S(1)}, bf16[144,1152]{1,0:T(8,128)(2,1)S(1)}, u32[]{:S(2)}, u32[]{:S(2)}) %collective-permute-start.7) | collective-permute-done | bytes 331808 | tf_op jit(solution)/shard_map/ppermute | solution.py:42
  158.3 6.2 %collective-permute-done.8 = bf16[144,1152]{1,0:T(8,128)(2,1)S(1)} collective-permute-done((bf16[144,1152]{1,0:T(8,128)(2,1)S(1)}, bf16[144,1152]{1,0:T(8,128)(2,1)S(1)}, u32[]{:S(2)}, u32[]{:S(2)}) %collective-permute-start.8) | collective-permute-done | bytes 331808 | tf_op jit(solution)/shard_map/ppermute | solution.py:42
  165.0 1.9 collective-permute-start.10
  170.0 2.1 collective-permute-start.3
  174.0 5.3 %collective-permute-start.5 = (bf16[2,64,1152]{2,1,0:T(8,128)(2,1)S(1)}, bf16[2,64,1152]{2,1,0:T(8,128)(2,1)S(1)}, u32[]{:S(2)}, u32[]{:S(2)}) collective-permute-start(bf16[2,64,1152]{2,1,0:T(8,128)(2,1)S(1)} %add_convert_fusion), channel_id=1, source_target_pairs={{0,7},{1,0},{2,1},{3,2},{4,3},{5,4},{6,5},{7,6},{8,9},{9,10},{10,1... | collective-permute-start | bytes 884744 | tf_op jit(solution)/shard_map/ppermute | solution.py:37
  180.8 2.1 collective-permute-done.3
  182.9 5.5 %collective-permute-done.4 = bf16[2,64,1152]{2,1,0:T(8,128)(2,1)S(1)} collective-permute-done((bf16[2,64,1152]{2,1,0:T(8,128)(2,1)S(1)}, bf16[2,64,1152]{2,1,0:T(8,128)(2,1)S(1)}, u32[]{:S(2)}, u32[]{:S(2)}) %collective-permute-start.4) | collective-permute-done | bytes 294944 | tf_op jit(solution)/shard_map/ppermute | solution.py:37
  188.6 1.9 fusion.23
  194.5 3.5 %collective-permute-start.12 = (bf16[2,64,1152]{2,1,0:T(8,128)(2,1)S(1)}, bf16[2,64,1152]{2,1,0:T(8,128)(2,1)S(1)}, u32[]{:S(2)}, u32[]{:S(2)}) collective-permute-start(bf16[2,64,1152]{2,1,0:T(8,128)(2,1)S(1)} %bitcast.147), channel_id=1, source_target_pairs={{0,7},{1,0},{2,1},{3,2},{4,3},{5,4},{6,5},{7,6},{8,9},{9,10},{10,1... | collective-permute-start | bytes 884744 | tf_op jit(solution)/shard_map/ppermute | solution.py:37
  198.0 2.4 collective-permute-start.13
  200.3 5.9 %collective-permute-done.11 = bf16[2,64,1152]{2,1,0:T(8,128)(2,1)S(1)} collective-permute-done((bf16[2,64,1152]{2,1,0:T(8,128)(2,1)S(1)}, bf16[2,64,1152]{2,1,0:T(8,128)(2,1)S(1)}, u32[]{:S(2)}, u32[]{:S(2)}) %collective-permute-start.11) | collective-permute-done | bytes 294944 | tf_op jit(solution)/shard_map/ppermute | solution.py:37
  206.2 3.8 %collective-permute-done.12 = bf16[2,64,1152]{2,1,0:T(8,128)(2,1)S(1)} collective-permute-done((bf16[2,64,1152]{2,1,0:T(8,128)(2,1)S(1)}, bf16[2,64,1152]{2,1,0:T(8,128)(2,1)S(1)}, u32[]{:S(2)}, u32[]{:S(2)}) %collective-permute-start.12) | collective-permute-done | bytes 294944 | tf_op jit(solution)/shard_map/ppermute | solution.py:37
  210.5 3.0 %collective-permute-start.16 = (bf16[64,1152]{1,0:T(8,128)(2,1)S(1)}, bf16[64,1152]{1,0:T(8,128)(2,1)S(1)}, u32[]{:S(2)}, u32[]{:S(2)}) collective-permute-start(bf16[64,1152]{1,0:T(8,128)(2,1)S(1)} %get-tuple-element.27), channel_id=1, source_target_pairs={{0,64},{64,128},{128,192},{192,0},{256,320},{320,384},{384,448},{4... | collective-permute-start | bytes 442376 | tf_op jit(solution)/shard_map/ppermute | solution.py:154
  214.2 4.6 %collective-permute-done.16 = bf16[64,1152]{1,0:T(8,128)(2,1)S(1)} collective-permute-done((bf16[64,1152]{1,0:T(8,128)(2,1)S(1)}, bf16[64,1152]{1,0:T(8,128)(2,1)S(1)}, u32[]{:S(2)}, u32[]{:S(2)}) %collective-permute-start.16) | collective-permute-done | bytes 147488 | tf_op jit(solution)/shard_map/ppermute | solution.py:154
  218.8 10.1 %collective-permute-start.17 = (bf16[64,1152]{1,0:T(8,128)(2,1)S(1)}, bf16[64,1152]{1,0:T(8,128)(2,1)S(1)}, u32[]{:S(2)}, u32[]{:S(2)}) collective-permute-start(bf16[64,1152]{1,0:T(8,128)(2,1)S(1)} %collective-permute-done.16), channel_id=1, source_target_pairs={{0,256},{256,512},{512,0},{1,257},{257,513},{513,1},{2,258},{258,5... | collective-permute-start | bytes 442376 | tf_op jit(solution)/shard_map/ppermute | solution.py:152
  230.9 5.2 %collective-permute-done.17 = bf16[64,1152]{1,0:T(8,128)(2,1)S(1)} collective-permute-done((bf16[64,1152]{1,0:T(8,128)(2,1)S(1)}, bf16[64,1152]{1,0:T(8,128)(2,1)S(1)}, u32[]{:S(2)}, u32[]{:S(2)}) %collective-permute-start.17) | collective-permute-done | bytes 147488 | tf_op jit(solution)/shard_map/ppermute | solution.py:152
  236.1 2.5 %collective-permute-done.15 = bf16[64,1152]{1,0:T(8,128)(2,1)S(1)} collective-permute-done((bf16[64,1152]{1,0:T(8,128)(2,1)S(1)}, bf16[64,1152]{1,0:T(8,128)(2,1)S(1)}, u32[]{:S(2)}, u32[]{:S(2)}) %collective-permute-start.15) | collective-permute-done | bytes 147488 | tf_op jit(solution)/shard_map/ppermute | solution.py:157
  (65 shorter events, 31.5 us)
Async XLA Ops:
  0.0 3.7 %copy-start = (bf16[1,1152,3,144]{1,3,2,0:T(8,128)(2,1)S(1)}, bf16[1,1152,3,144]{1,3,2,0:T(8,128)(2,1)}, u32[]{:S(2)}) copy-start(bf16[1,1152,3,144]{1,3,2,0:T(8,128)(2,1)} %param.10) | copy-start | bytes 2985988
  0.0 8.4 %collective-permute-start = (bf16[2,64,1152]{2,1,0:T(8,128)(2,1)}, bf16[2,64,1152]{2,1,0:T(8,128)(2,1)S(1)}, u32[]{:S(2)}, u32[]{:S(2)}) collective-permute-start(bf16[2,64,1152]{2,1,0:T(8,128)(2,1)} %bitcast.149), channel_id=1, source_target_pairs={{0,8},{8,16},{16,24},{24,32},{32,40},{40,48},{48,56},{1,9},{9,17},... | collective-permute-start | bytes 884744 | tf_op jit(solution)/shard_map/ppermute | solution.py:18
  9.9 8.6 %copy-start.1 = (bf16[1,144,1152]{2,1,0:T(8,128)(2,1)S(1)}, bf16[1,144,1152]{2,1,0:T(8,128)(2,1)}, u32[]{:S(2)}) copy-start(bf16[1,144,1152]{2,1,0:T(8,128)(2,1)} %param.11) | copy-start | bytes 995332
  11.4 55.7 %all-to-all-start = ((bf16[8,64,1152]{2,1,0:T(8,128)(2,1)}), bf16[8,64,1152]{2,1,0:T(8,128)(2,1)S(1)}, u32[]{:S(2)}, u32[]{:S(2)}) async-start(bf16[8,64,1152]{2,1,0:T(8,128)(2,1)} %bitcast.1), calls=%async_computation | async-start | bytes 2359296 | tf_op jit(solution)/shard_map/all_to_all | solution.py:119
  18.6 42.1 %collective-permute-start.1 = (bf16[4,72,1152]{2,1,0:T(8,128)(2,1)S(1)}, bf16[4,72,1152]{2,1,0:T(8,128)(2,1)}, u32[]{:S(2)}, u32[]{:S(2)}) collective-permute-start(bf16[4,72,1152]{2,1,0:T(8,128)(2,1)S(1)} %pad_maximum_fusion.2), channel_id=1, source_target_pairs={{0,1},{1,0},{2,3},{3,2},{4,5},{5,4},{6,7},{7,6},{8,9},{9,8},{10,11... | collective-permute-start | bytes 1990664 | tf_op jit(solution)/shard_map/ppermute | solution.py:27
  60.7 4.3 %collective-permute-start.2 = (bf16[4,72,1152]{2,1,0:T(8,128)(2,1)}, bf16[4,72,1152]{2,1,0:T(8,128)(2,1)}, u32[]{:S(2)}, u32[]{:S(2)}) collective-permute-start(bf16[4,72,1152]{2,1,0:T(8,128)(2,1)} %collective-permute-done.1), channel_id=1, source_target_pairs={{0,8},{8,0},{16,24},{24,16},{32,40},{40,32},{48,56},{56,48},{1,9},... | collective-permute-start | bytes 1990664 | tf_op jit(solution)/shard_map/ppermute | solution.py:27
  70.6 0.8 copy-start.6
  72.2 2.2 copy-start.5
  79.6 88.3 %all-to-all-start.1 = ((bf16[8,64,1152]{2,1,0:T(8,128)(2,1)}), bf16[8,64,1152]{2,1,0:T(8,128)(2,1)}, u32[]{:S(2)}, u32[]{:S(2)}) async-start(bf16[8,64,1152]{2,1,0:T(8,128)(2,1)} %bitcast.23), calls=%async_computation.1 | async-start | bytes 2359296 | tf_op jit(solution)/shard_map/all_to_all | solution.py:128
  87.3 44.2 %collective-permute-start.6 = (bf16[144,1152]{1,0:T(8,128)(2,1)S(1)}, bf16[144,1152]{1,0:T(8,128)(2,1)S(1)}, u32[]{:S(2)}, u32[]{:S(2)}) collective-permute-start(bf16[144,1152]{1,0:T(8,128)(2,1)S(1)} %pad_maximum_fusion.3), channel_id=1, source_target_pairs={{0,4},{1,5},{2,6},{3,7},{4,0},{5,1},{6,2},{7,3},{8,12},{9,13},{10,... | collective-permute-start | bytes 995336 | tf_op jit(solution)/shard_map/ppermute | solution.py:23
  131.6 26.7 %collective-permute-start.7 = (bf16[144,1152]{1,0:T(8,128)(2,1)S(1)}, bf16[144,1152]{1,0:T(8,128)(2,1)S(1)}, u32[]{:S(2)}, u32[]{:S(2)}) collective-permute-start(bf16[144,1152]{1,0:T(8,128)(2,1)S(1)} %collective-permute-done.6), channel_id=1, source_target_pairs={{0,16},{8,24},{16,32},{24,40},{32,48},{40,56},{48,0},{56,8},{1,17}... | collective-permute-start | bytes 995336 | tf_op jit(solution)/shard_map/ppermute | solution.py:42
  135.9 28.5 %collective-permute-start.8 = (bf16[144,1152]{1,0:T(8,128)(2,1)S(1)}, bf16[144,1152]{1,0:T(8,128)(2,1)S(1)}, u32[]{:S(2)}, u32[]{:S(2)}) collective-permute-start(bf16[144,1152]{1,0:T(8,128)(2,1)S(1)} %collective-permute-done.6), channel_id=1, source_target_pairs={{0,32},{8,40},{16,48},{24,56},{32,0},{40,8},{48,16},{56,24},{1,33}... | collective-permute-start | bytes 995336 | tf_op jit(solution)/shard_map/ppermute | solution.py:42
  137.8 27.0 %collective-permute-start.9 = (bf16[144,1152]{1,0:T(8,128)(2,1)S(1)}, bf16[144,1152]{1,0:T(8,128)(2,1)S(1)}, u32[]{:S(2)}, u32[]{:S(2)}) collective-permute-start(bf16[144,1152]{1,0:T(8,128)(2,1)S(1)} %collective-permute-done.6), channel_id=1, source_target_pairs={{0,48},{8,56},{16,0},{24,8},{32,16},{40,24},{48,32},{56,40},{1,49}... | collective-permute-start | bytes 995336 | tf_op jit(solution)/shard_map/ppermute | solution.py:42
  165.0 14.3 %collective-permute-start.10 = (bf16[4,144,1152]{2,1,0:T(8,128)(2,1)S(1)}, bf16[4,144,1152]{2,1,0:T(8,128)(2,1)}, u32[]{:S(2)}, u32[]{:S(2)}) collective-permute-start(bf16[4,144,1152]{2,1,0:T(8,128)(2,1)S(1)} %pad_maximum_fusion), channel_id=1, source_target_pairs={{0,8},{8,0},{16,24},{24,16},{32,40},{40,32},{48,56},{56,48},{1,9},... | collective-permute-start | bytes 3981320 | tf_op jit(solution)/shard_map/ppermute | solution.py:27
  170.0 18.6 %copy-start.2 = (bf16[4,72,1152]{2,1,0:T(8,128)(2,1)S(1)}, bf16[4,72,1152]{2,1,0:T(8,128)(2,1)}, u32[]{:S(2)}) copy-start(bf16[4,72,1152]{2,1,0:T(8,128)(2,1)} %get-tuple-element.19) | copy-start | bytes 1990660
  170.0 18.6 %copy-start.3 = (bf16[1,1152,576]{1,2,0:T(8,128)(2,1)S(1)}, bf16[1,1152,576]{1,2,0:T(8,128)(2,1)}, u32[]{:S(2)}) copy-start(bf16[1,1152,576]{1,2,0:T(8,128)(2,1)} %param.12) | copy-start | bytes 3981316
  170.0 12.9 %collective-permute-start.3 = (bf16[2,64,1152]{2,1,0:T(8,128)(2,1)S(1)}, bf16[2,64,1152]{2,1,0:T(8,128)(2,1)S(1)}, u32[]{:S(2)}, u32[]{:S(2)}) collective-permute-start(bf16[2,64,1152]{2,1,0:T(8,128)(2,1)S(1)} %add_convert_fusion), channel_id=1, source_target_pairs={{0,2},{1,3},{2,4},{3,5},{4,6},{5,7},{6,0},{7,1},{8,14},{9,15},{10,... | collective-permute-start | bytes 884744 | tf_op jit(solution)/shard_map/ppermute | solution.py:37
  172.1 16.3 %collective-permute-start.4 = (bf16[2,64,1152]{2,1,0:T(8,128)(2,1)S(1)}, bf16[2,64,1152]{2,1,0:T(8,128)(2,1)S(1)}, u32[]{:S(2)}, u32[]{:S(2)}) collective-permute-start(bf16[2,64,1152]{2,1,0:T(8,128)(2,1)S(1)} %add_convert_fusion), channel_id=1, source_target_pairs={{0,1},{1,2},{2,3},{3,4},{4,5},{5,6},{6,7},{7,0},{8,15},{9,8},{10,9... | collective-permute-start | bytes 884744 | tf_op jit(solution)/shard_map/ppermute | solution.py:37
  174.0 14.4 %collective-permute-start.5 = (bf16[2,64,1152]{2,1,0:T(8,128)(2,1)S(1)}, bf16[2,64,1152]{2,1,0:T(8,128)(2,1)S(1)}, u32[]{:S(2)}, u32[]{:S(2)}) collective-permute-start(bf16[2,64,1152]{2,1,0:T(8,128)(2,1)S(1)} %add_convert_fusion), channel_id=1, source_target_pairs={{0,7},{1,0},{2,1},{3,2},{4,3},{5,4},{6,5},{7,6},{8,9},{9,10},{10,1... | collective-permute-start | bytes 884744 | tf_op jit(solution)/shard_map/ppermute | solution.py:37
  188.6 2.0 copy-start.4
  192.6 13.7 %collective-permute-start.11 = (bf16[2,64,1152]{2,1,0:T(8,128)(2,1)S(1)}, bf16[2,64,1152]{2,1,0:T(8,128)(2,1)S(1)}, u32[]{:S(2)}, u32[]{:S(2)}) collective-permute-start(bf16[2,64,1152]{2,1,0:T(8,128)(2,1)S(1)} %bitcast.148), channel_id=1, source_target_pairs={{0,6},{1,7},{2,0},{3,1},{4,2},{5,3},{6,4},{7,5},{8,10},{9,11},{10,... | collective-permute-start | bytes 884744 | tf_op jit(solution)/shard_map/ppermute | solution.py:37
  194.5 15.5 %collective-permute-start.12 = (bf16[2,64,1152]{2,1,0:T(8,128)(2,1)S(1)}, bf16[2,64,1152]{2,1,0:T(8,128)(2,1)S(1)}, u32[]{:S(2)}, u32[]{:S(2)}) collective-permute-start(bf16[2,64,1152]{2,1,0:T(8,128)(2,1)S(1)} %bitcast.147), channel_id=1, source_target_pairs={{0,7},{1,0},{2,1},{3,2},{4,3},{5,4},{6,5},{7,6},{8,9},{9,10},{10,1... | collective-permute-start | bytes 884744 | tf_op jit(solution)/shard_map/ppermute | solution.py:37
  198.0 12.3 %collective-permute-start.13 = (bf16[2,64,1152]{2,1,0:T(8,128)(2,1)S(1)}, bf16[2,64,1152]{2,1,0:T(8,128)(2,1)S(1)}, u32[]{:S(2)}, u32[]{:S(2)}) collective-permute-start(bf16[2,64,1152]{2,1,0:T(8,128)(2,1)S(1)} %bitcast.145), channel_id=1, source_target_pairs={{0,1},{1,2},{2,3},{3,4},{4,5},{5,6},{6,7},{7,0},{8,15},{9,8},{10,9... | collective-permute-start | bytes 884744 | tf_op jit(solution)/shard_map/ppermute | solution.py:37
  210.5 8.2 %collective-permute-start.16 = (bf16[64,1152]{1,0:T(8,128)(2,1)S(1)}, bf16[64,1152]{1,0:T(8,128)(2,1)S(1)}, u32[]{:S(2)}, u32[]{:S(2)}) collective-permute-start(bf16[64,1152]{1,0:T(8,128)(2,1)S(1)} %get-tuple-element.27), channel_id=1, source_target_pairs={{0,64},{64,128},{128,192},{192,0},{256,320},{320,384},{384,448},{4... | collective-permute-start | bytes 442376 | tf_op jit(solution)/shard_map/ppermute | solution.py:154
  213.5 15.4 %collective-permute-start.14 = (bf16[64,1152]{1,0:T(8,128)(2,1)S(1)}, bf16[64,1152]{1,0:T(8,128)(2,1)S(1)}, u32[]{:S(2)}, u32[]{:S(2)}) collective-permute-start(bf16[64,1152]{1,0:T(8,128)(2,1)S(1)} %get-tuple-element.26), channel_id=1, source_target_pairs={{192,448},{448,704},{704,192},{193,449},{449,705},{705,193},{194,4... | collective-permute-start | bytes 442376 | tf_op jit(solution)/shard_map/ppermute | solution.py:152
  218.8 17.3 %collective-permute-start.17 = (bf16[64,1152]{1,0:T(8,128)(2,1)S(1)}, bf16[64,1152]{1,0:T(8,128)(2,1)S(1)}, u32[]{:S(2)}, u32[]{:S(2)}) collective-permute-start(bf16[64,1152]{1,0:T(8,128)(2,1)S(1)} %collective-permute-done.16), channel_id=1, source_target_pairs={{0,256},{256,512},{512,0},{1,257},{257,513},{513,1},{2,258},{258,5... | collective-permute-start | bytes 442376 | tf_op jit(solution)/shard_map/ppermute | solution.py:152
  228.9 9.7 %collective-permute-start.15 = (bf16[64,1152]{1,0:T(8,128)(2,1)S(1)}, bf16[64,1152]{1,0:T(8,128)(2,1)S(1)}, u32[]{:S(2)}, u32[]{:S(2)}) collective-permute-start(bf16[64,1152]{1,0:T(8,128)(2,1)S(1)} %broadcast_select_fusion), channel_id=1, source_target_pairs={{0,64},{64,128},{128,192},{192,0},{256,320},{320,384},{384,448},{4... | collective-permute-start | bytes 442376 | tf_op jit(solution)/shard_map/ppermute | solution.py:157

commit v4 on v3

--- a/solution.py
+++ b/solution.py
@@ -3,6 +3,8 @@
 import jax
 import jax.numpy as jnp
 from jax import lax
+from jax.experimental import pallas as pl
+from jax.experimental.pallas import tpu as pltpu
 from jax.sharding import PartitionSpec as P
 
 D = 1152
@@ -52,17 +54,42 @@
     return (normalize(values_in) * (1.0 + scale_row) + shift_row).astype(BF16)
 
 
-def attend(rows, qkv, out_w):
-    tokens, heads = rows.shape[0], qkv.shape[1] // HEAD
-    projected = jnp.einsum("te,cne->tcn", rows, qkv, preferred_element_type=F32).astype(BF16)
-    projected = projected.reshape(tokens, 3, heads, HEAD)
-    scores = jnp.einsum(
-        "qhe,khe->hqk", projected[:, 0], projected[:, 1], preferred_element_type=F32
-    ) * (1.0 / math.sqrt(HEAD))
-    probs = jax.nn.softmax(scores, axis=-1).astype(BF16)
-    heads_out = jnp.einsum("hqk,khe->qhe", probs, projected[:, 2], preferred_element_type=F32)
-    heads_out = heads_out.astype(BF16).reshape(tokens, heads * HEAD)
-    return jnp.dot(heads_out, out_w, preferred_element_type=F32)
+def attention_kernel(rows_ref, own_ref, own_out_ref, near_ref, part_ref, heads_ref):
+    rows = rows_ref[...]
+    columns = own_out_ref.shape[0]
+    total = None
+    for side in range(2):
+        qkv_w = own_ref[...] if side == 0 else near_ref[: 3 * columns]
+        out_w = own_out_ref[...] if side == 0 else near_ref[3 * columns :]
+        projected = lax.dot_general(
+            qkv_w, rows, (((1,), (1,)), ((), ())), preferred_element_type=F32
+        )
+        for head in range(columns // HEAD):
+            q, k, v = (
+                projected[c * columns + head * HEAD : c * columns + (head + 1) * HEAD].astype(BF16)
+                for c in range(3)
+            )
+            scores = lax.dot_general(k, q, (((0,), (0,)), ((), ())), preferred_element_type=F32)
+            top = jnp.max(scores, axis=0, keepdims=True)
+            weight = jnp.exp((scores - top) * (1.0 / math.sqrt(HEAD)))
+            mass = jnp.sum(weight, axis=0, keepdims=True)
+            mixed = jnp.dot(v, weight.astype(BF16), preferred_element_type=F32)
+            heads_ref[head * HEAD : (head + 1) * HEAD] = mixed / mass
+        part = lax.dot_general(
+            heads_ref[...].astype(BF16), out_w, (((0,), (0,)), ((), ())), preferred_element_type=F32
+        )
+        total = part if total is None else total + part
+    part_ref[...] = total.astype(BF16)
+
+
+def attend(rows, qkv_own, out_own, near):
+    tokens, columns = rows.shape[0], out_own.shape[0]
+    return pl.pallas_call(
+        attention_kernel,
+        out_shape=jax.ShapeDtypeStruct((tokens, D), BF16),
+        scratch_shapes=[pltpu.VMEM((columns, tokens), F32)],
+        name="frame_attention",
+    )(rows, qkv_own, out_own, near)
 
 
 def feed_forward(rows, up_w, down_w):
@@ -118,8 +145,8 @@
     outgoing = jnp.broadcast_to(attn_in[None], (n_space // frames, frames, tokens, D))
     rows = lax.all_to_all(outgoing.reshape(n_space, tokens, D), "space", 0, 0, tiled=True)
     rows = rows.reshape(n_space * tokens, D)
-    attn_part = attend(rows, qkv_own, out_own) + attend(rows, near[:3], near[3])
-    attn_part = attn_part.astype(BF16).reshape(n_space, tokens, D)
+    attn_part = attend(rows, qkv_own.reshape(-1, D), out_own, near.reshape(-1, D))
+    attn_part = attn_part.reshape(n_space, tokens, D)
     far = after(far, attn_part)
     turned = [far]
     for k in range(1, members // 2):

time: 240 us -> 233 us (0.971)
  the two profiles are of different devices: /device:TPU:64 before, /device:TPU:192 now
where the time goes in v4:
time: 233 us; the launch traced here: 232 us
  waiting for transfers between devices  131 us (56%)
  starting transfers between devices  75.3 us (32%)
  local copies, waits for them, and re-layouts  8.46 us (4%)
  Pallas kernels  7.76 us (3%)
  other arithmetic  5.08 us (2%)
  matrix products  3.8 us (2%)
    ppermute x1, waiting for transfers between devices, rotate(): lax.ppermute(block, axis, [(i, (i + steps) % count) for i in range(count)])  36.4 us
    ppermute x3, waiting for transfers between devices, flip(): lax.ppermute(block, axis, [(i, i ^ 1) for i in range(lax.axis_size(axis))])  35.7 us
    ppermute x3, waiting for transfers between devices, turn_z(): lax.ppermute(block, 'tm', [(i, (i + 2 * steps) % count) for i in range(co...  25.2 us
    ppermute x6, waiting for transfers between devices, mirrored(): return lax.ppermute(block, ('tm', 'space'), route)  17.7 us
    ppermute x6, starting transfers between devices, mirrored(): return lax.ppermute(block, ('tm', 'space'), route)  16.7 us
    ppermute x3, starting transfers between devices, turn_z(): lax.ppermute(block, 'tm', [(i, (i + 2 * steps) % count) for i in range(co...  11.4 us
    ppermute x2, starting transfers between devices, crossing(): lax.ppermute(block, 'section', [(s, (s + 4) % sections) for s in range(x,...  11.2 us
    ppermute x1, starting transfers between devices, rotate(): lax.ppermute(block, axis, [(i, (i + steps) % count) for i in range(count)])  7.84 us
  transfers between devices with their start and end apart: 20, of which 14 were waited for; matrix products, arithmetic and copies ran while one was open for 4% of the time, Pallas kernels for 0%

profile of v4, /device:TPU:192, one launch (start us, length us, event | category | flops | bytes accessed | tf_op | source)
XLA Modules:
  0.0 232.1 jit_solution(6809784279309470939)
XLA Ops:
  0.0 2.0 collective-permute-start
  4.8 3.6 %collective-permute-done = bf16[2,64,1152]{2,1,0:T(8,128)(2,1)S(1)} collective-permute-done((bf16[2,64,1152]{2,1,0:T(8,128)(2,1)}, bf16[2,64,1152]{2,1,0:T(8,128)(2,1)S(1)}, u32[]{:S(2)}, u32[]{:S(2)}) %collective-permute-start) | collective-permute-done | bytes 294944 | tf_op jit(solution)/shard_map/ppermute | solution.py:20
  10.4 7.2 %all-to-all-start = ((bf16[8,64,1152]{2,1,0:T(8,128)(2,1)}), bf16[8,64,1152]{2,1,0:T(8,128)(2,1)S(1)}, u32[]{:S(2)}, u32[]{:S(2)}) async-start(bf16[8,64,1152]{2,1,0:T(8,128)(2,1)} %bitcast.1), calls=%async_computation | async-start | bytes 2359296 | tf_op jit(solution)/shard_map/all_to_all | solution.py:146
  17.7 3.9 %collective-permute-start.1 = (bf16[4,72,1152]{2,1,0:T(8,128)(2,1)S(1)}, bf16[4,72,1152]{2,1,0:T(8,128)(2,1)S(1)}, u32[]{:S(2)}, u32[]{:S(2)}) collective-permute-start(bf16[4,72,1152]{2,1,0:T(8,128)(2,1)S(1)} %pad_maximum_fusion.3), channel_id=1, source_target_pairs={{0,1},{1,0},{2,3},{3,2},{4,5},{5,4},{6,7},{7,6},{8,9},{9,8},{10,11... | collective-permute-start | bytes 1990664 | tf_op jit(solution)/shard_map/ppermute | solution.py:29
  21.7 33.6 %collective-permute-done.1 = bf16[4,72,1152]{2,1,0:T(8,128)(2,1)S(1)} collective-permute-done((bf16[4,72,1152]{2,1,0:T(8,128)(2,1)S(1)}, bf16[4,72,1152]{2,1,0:T(8,128)(2,1)S(1)}, u32[]{:S(2)}, u32[]{:S(2)}) %collective-permute-start.1) | collective-permute-done | bytes 663584 | tf_op jit(solution)/shard_map/ppermute | solution.py:29
  57.2 2.1 collective-permute-done.2
  61.5 7.8 %frame_attention.1 = bf16[512,1152]{1,0:T(8,128)(2,1)} custom-call(bf16[512,1152]{1,0:T(8,128)(2,1)} %bitcast.60, bf16[432,1152]{1,0:T(8,128)(2,1)} %bitcast.62, bf16[144,1152]{1,0:T(8,128)(2,1)} %bitcast.66, bf16[576,1152]{1,0:T(8,128)(2,1)} %bitcast.58), custom_call_target="tpu_custom_call" | custom-call | tf_op jit(solution)/shard_map/frame_attention/pallas_call | solution.py:87
  69.2 5.8 %all-to-all-start.1 = ((bf16[8,64,1152]{2,1,0:T(8,128)(2,1)}), bf16[8,64,1152]{2,1,0:T(8,128)(2,1)S(1)}, u32[]{:S(2)}, u32[]{:S(2)}) async-start(bf16[8,64,1152]{2,1,0:T(8,128)(2,1)} %bitcast.59), calls=%async_computation.1 | async-start | bytes 2359296 | tf_op jit(solution)/shard_map/all_to_all | solution.py:155
  76.9 7.8 %collective-permute-start.6 = (bf16[144,1152]{1,0:T(8,128)(2,1)S(1)}, bf16[144,1152]{1,0:T(8,128)(2,1)S(1)}, u32[]{:S(2)}, u32[]{:S(2)}) collective-permute-start(bf16[144,1152]{1,0:T(8,128)(2,1)S(1)} %pad_maximum_fusion.4), channel_id=1, source_target_pairs={{0,4},{1,5},{2,6},{3,7},{4,0},{5,1},{6,2},{7,3},{8,12},{9,13},{10,... | collective-permute-start | bytes 995336 | tf_op jit(solution)/shard_map/ppermute | solution.py:25
  84.8 36.4 %collective-permute-done.6 = bf16[144,1152]{1,0:T(8,128)(2,1)S(1)} collective-permute-done((bf16[144,1152]{1,0:T(8,128)(2,1)S(1)}, bf16[144,1152]{1,0:T(8,128)(2,1)S(1)}, u32[]{:S(2)}, u32[]{:S(2)}) %collective-permute-start.6) | collective-permute-done | bytes 331808 | tf_op jit(solution)/shard_map/ppermute | solution.py:25
  121.2 4.5 %collective-permute-start.7 = (bf16[144,1152]{1,0:T(8,128)(2,1)S(1)}, bf16[144,1152]{1,0:T(8,128)(2,1)S(1)}, u32[]{:S(2)}, u32[]{:S(2)}) collective-permute-start(bf16[144,1152]{1,0:T(8,128)(2,1)S(1)} %collective-permute-done.6), channel_id=1, source_target_pairs={{0,16},{8,24},{16,32},{24,40},{32,48},{40,56},{48,0},{56,8},{1,17}... | collective-permute-start | bytes 995336 | tf_op jit(solution)/shard_map/ppermute | solution.py:44
  125.7 4.9 %collective-permute-start.8 = (bf16[144,1152]{1,0:T(8,128)(2,1)S(1)}, bf16[144,1152]{1,0:T(8,128)(2,1)S(1)}, u32[]{:S(2)}, u32[]{:S(2)}) collective-permute-start(bf16[144,1152]{1,0:T(8,128)(2,1)S(1)} %collective-permute-done.6), channel_id=1, source_target_pairs={{0,32},{8,40},{16,48},{24,56},{32,0},{40,8},{48,16},{56,24},{1,33}... | collective-permute-start | bytes 995336 | tf_op jit(solution)/shard_map/ppermute | solution.py:44
  130.6 1.9 collective-permute-start.9
  132.6 2.7 %collective-permute-done.7 = bf16[144,1152]{1,0:T(8,128)(2,1)S(1)} collective-permute-done((bf16[144,1152]{1,0:T(8,128)(2,1)S(1)}, bf16[144,1152]{1,0:T(8,128)(2,1)S(1)}, u32[]{:S(2)}, u32[]{:S(2)}) %collective-permute-start.7) | collective-permute-done | bytes 331808 | tf_op jit(solution)/shard_map/ppermute | solution.py:44
  135.2 22.5 %collective-permute-done.8 = bf16[144,1152]{1,0:T(8,128)(2,1)S(1)} collective-permute-done((bf16[144,1152]{1,0:T(8,128)(2,1)S(1)}, bf16[144,1152]{1,0:T(8,128)(2,1)S(1)}, u32[]{:S(2)}, u32[]{:S(2)}) %collective-permute-start.8) | collective-permute-done | bytes 331808 | tf_op jit(solution)/shard_map/ppermute | solution.py:44
  157.9 1.9 collective-permute-start.10
  161.6 1.9 collective-permute-start.3
  165.5 5.1 %collective-permute-start.5 = (bf16[2,64,1152]{2,1,0:T(8,128)(2,1)S(1)}, bf16[2,64,1152]{2,1,0:T(8,128)(2,1)S(1)}, u32[]{:S(2)}, u32[]{:S(2)}) collective-permute-start(bf16[2,64,1152]{2,1,0:T(8,128)(2,1)S(1)} %add_convert_fusion), channel_id=1, source_target_pairs={{0,7},{1,0},{2,1},{3,2},{4,3},{5,4},{6,5},{7,6},{8,9},{9,10},{10,1... | collective-permute-start | bytes 884744 | tf_op jit(solution)/shard_map/ppermute | solution.py:39
  172.0 2.3 %collective-permute-done.3 = bf16[2,64,1152]{2,1,0:T(8,128)(2,1)S(1)} collective-permute-done((bf16[2,64,1152]{2,1,0:T(8,128)(2,1)S(1)}, bf16[2,64,1152]{2,1,0:T(8,128)(2,1)S(1)}, u32[]{:S(2)}, u32[]{:S(2)}) %collective-permute-start.3) | collective-permute-done | bytes 294944 | tf_op jit(solution)/shard_map/ppermute | solution.py:39
  174.4 5.4 %collective-permute-done.4 = bf16[2,64,1152]{2,1,0:T(8,128)(2,1)S(1)} collective-permute-done((bf16[2,64,1152]{2,1,0:T(8,128)(2,1)S(1)}, bf16[2,64,1152]{2,1,0:T(8,128)(2,1)S(1)}, u32[]{:S(2)}, u32[]{:S(2)}) %collective-permute-start.4) | collective-permute-done | bytes 294944 | tf_op jit(solution)/shard_map/ppermute | solution.py:39
  180.0 1.9 fusion.20
  183.9 1.9 collective-permute-start.11
  185.9 3.5 %collective-permute-start.12 = (bf16[2,64,1152]{2,1,0:T(8,128)(2,1)S(1)}, bf16[2,64,1152]{2,1,0:T(8,128)(2,1)S(1)}, u32[]{:S(2)}, u32[]{:S(2)}) collective-permute-start(bf16[2,64,1152]{2,1,0:T(8,128)(2,1)S(1)} %bitcast.79), channel_id=1, source_target_pairs={{0,7},{1,0},{2,1},{3,2},{4,3},{5,4},{6,5},{7,6},{8,9},{9,10},{10,1... | collective-permute-start | bytes 884744 | tf_op jit(solution)/shard_map/ppermute | solution.py:39
  189.4 2.4 %collective-permute-start.13 = (bf16[2,64,1152]{2,1,0:T(8,128)(2,1)S(1)}, bf16[2,64,1152]{2,1,0:T(8,128)(2,1)S(1)}, u32[]{:S(2)}, u32[]{:S(2)}) collective-permute-start(bf16[2,64,1152]{2,1,0:T(8,128)(2,1)S(1)} %bitcast.77), channel_id=1, source_target_pairs={{0,1},{1,2},{2,3},{3,4},{4,5},{5,6},{6,7},{7,0},{8,15},{9,8},{10,9... | collective-permute-start | bytes 884744 | tf_op jit(solution)/shard_map/ppermute | solution.py:39
  191.7 6.0 %collective-permute-done.11 = bf16[2,64,1152]{2,1,0:T(8,128)(2,1)S(1)} collective-permute-done((bf16[2,64,1152]{2,1,0:T(8,128)(2,1)S(1)}, bf16[2,64,1152]{2,1,0:T(8,128)(2,1)S(1)}, u32[]{:S(2)}, u32[]{:S(2)}) %collective-permute-start.11) | collective-permute-done | bytes 294944 | tf_op jit(solution)/shard_map/ppermute | solution.py:39
  197.7 3.6 %collective-permute-done.12 = bf16[2,64,1152]{2,1,0:T(8,128)(2,1)S(1)} collective-permute-done((bf16[2,64,1152]{2,1,0:T(8,128)(2,1)S(1)}, bf16[2,64,1152]{2,1,0:T(8,128)(2,1)S(1)}, u32[]{:S(2)}, u32[]{:S(2)}) %collective-permute-start.12) | collective-permute-done | bytes 294944 | tf_op jit(solution)/shard_map/ppermute | solution.py:39
  201.9 3.4 %collective-permute-start.16 = (bf16[64,1152]{1,0:T(8,128)(2,1)S(1)}, bf16[64,1152]{1,0:T(8,128)(2,1)S(1)}, u32[]{:S(2)}, u32[]{:S(2)}) collective-permute-start(bf16[64,1152]{1,0:T(8,128)(2,1)S(1)} %get-tuple-element.27), channel_id=1, source_target_pairs={{0,64},{64,128},{128,192},{192,0},{256,320},{320,384},{384,448},{4... | collective-permute-start | bytes 442376 | tf_op jit(solution)/shard_map/ppermute | solution.py:181
  206.0 4.2 %collective-permute-done.16 = bf16[64,1152]{1,0:T(8,128)(2,1)S(1)} collective-permute-done((bf16[64,1152]{1,0:T(8,128)(2,1)S(1)}, bf16[64,1152]{1,0:T(8,128)(2,1)S(1)}, u32[]{:S(2)}, u32[]{:S(2)}) %collective-permute-start.16) | collective-permute-done | bytes 147488 | tf_op jit(solution)/shard_map/ppermute | solution.py:181
  210.2 10.5 %collective-permute-start.17 = (bf16[64,1152]{1,0:T(8,128)(2,1)S(1)}, bf16[64,1152]{1,0:T(8,128)(2,1)S(1)}, u32[]{:S(2)}, u32[]{:S(2)}) collective-permute-start(bf16[64,1152]{1,0:T(8,128)(2,1)S(1)} %collective-permute-done.16), channel_id=1, source_target_pairs={{0,256},{256,512},{512,0},{1,257},{257,513},{513,1},{2,258},{258,5... | collective-permute-start | bytes 442376 | tf_op jit(solution)/shard_map/ppermute | solution.py:179
  220.7 1.9 collective-permute-start.15
  222.7 5.0 %collective-permute-done.17 = bf16[64,1152]{1,0:T(8,128)(2,1)S(1)} collective-permute-done((bf16[64,1152]{1,0:T(8,128)(2,1)S(1)}, bf16[64,1152]{1,0:T(8,128)(2,1)S(1)}, u32[]{:S(2)}, u32[]{:S(2)}) %collective-permute-start.17) | collective-permute-done | bytes 147488 | tf_op jit(solution)/shard_map/ppermute | solution.py:179
  227.7 3.6 %collective-permute-done.15 = bf16[64,1152]{1,0:T(8,128)(2,1)S(1)} collective-permute-done((bf16[64,1152]{1,0:T(8,128)(2,1)S(1)}, bf16[64,1152]{1,0:T(8,128)(2,1)S(1)}, u32[]{:S(2)}, u32[]{:S(2)}) %collective-permute-start.15) | collective-permute-done | bytes 147488 | tf_op jit(solution)/shard_map/ppermute | solution.py:184
  (55 shorter events, 20.2 us)
Async XLA Ops:
  0.0 8.4 %copy-start.3 = (bf16[1,2,64,1152]{3,2,1,0:T(8,128)(2,1)S(1)}, bf16[1,2,64,1152]{3,2,1,0:T(8,128)(2,1)}, u32[]{:S(2)}) copy-start(bf16[1,2,64,1152]{3,2,1,0:T(8,128)(2,1)} %param.7) | copy-start | bytes 884740
  0.0 8.4 %collective-permute-start = (bf16[2,64,1152]{2,1,0:T(8,128)(2,1)}, bf16[2,64,1152]{2,1,0:T(8,128)(2,1)S(1)}, u32[]{:S(2)}, u32[]{:S(2)}) collective-permute-start(bf16[2,64,1152]{2,1,0:T(8,128)(2,1)} %bitcast.81), channel_id=1, source_target_pairs={{0,8},{8,16},{16,24},{24,32},{32,40},{40,48},{48,56},{1,9},{9,17},... | collective-permute-start | bytes 884744 | tf_op jit(solution)/shard_map/ppermute | solution.py:20
  10.4 7.2 %copy-start.1 = (bf16[1,144,1152]{2,1,0:T(8,128)(2,1)S(1)}, bf16[1,144,1152]{2,1,0:T(8,128)(2,1)}, u32[]{:S(2)}) copy-start(bf16[1,144,1152]{2,1,0:T(8,128)(2,1)} %param.11) | copy-start | bytes 995332
  10.4 50.0 %all-to-all-start = ((bf16[8,64,1152]{2,1,0:T(8,128)(2,1)}), bf16[8,64,1152]{2,1,0:T(8,128)(2,1)S(1)}, u32[]{:S(2)}, u32[]{:S(2)}) async-start(bf16[8,64,1152]{2,1,0:T(8,128)(2,1)} %bitcast.1), calls=%async_computation | async-start | bytes 2359296 | tf_op jit(solution)/shard_map/all_to_all | solution.py:146
  17.7 37.5 %collective-permute-start.1 = (bf16[4,72,1152]{2,1,0:T(8,128)(2,1)S(1)}, bf16[4,72,1152]{2,1,0:T(8,128)(2,1)S(1)}, u32[]{:S(2)}, u32[]{:S(2)}) collective-permute-start(bf16[4,72,1152]{2,1,0:T(8,128)(2,1)S(1)} %pad_maximum_fusion.3), channel_id=1, source_target_pairs={{0,1},{1,0},{2,3},{3,2},{4,5},{5,4},{6,7},{7,6},{8,9},{9,8},{10,11... | collective-permute-start | bytes 1990664 | tf_op jit(solution)/shard_map/ppermute | solution.py:29
  55.3 4.0 %collective-permute-start.2 = (bf16[4,72,1152]{2,1,0:T(8,128)(2,1)S(1)}, bf16[4,72,1152]{2,1,0:T(8,128)(2,1)S(1)}, u32[]{:S(2)}, u32[]{:S(2)}) collective-permute-start(bf16[4,72,1152]{2,1,0:T(8,128)(2,1)S(1)} %collective-permute-done.1), channel_id=1, source_target_pairs={{0,8},{8,0},{16,24},{24,16},{32,40},{40,32},{48,56},{56,48},{1,9},... | collective-permute-start | bytes 1990664 | tf_op jit(solution)/shard_map/ppermute | solution.py:29
  60.4 1.0 copy-start
  69.2 91.6 %all-to-all-start.1 = ((bf16[8,64,1152]{2,1,0:T(8,128)(2,1)}), bf16[8,64,1152]{2,1,0:T(8,128)(2,1)S(1)}, u32[]{:S(2)}, u32[]{:S(2)}) async-start(bf16[8,64,1152]{2,1,0:T(8,128)(2,1)} %bitcast.59), calls=%async_computation.1 | async-start | bytes 2359296 | tf_op jit(solution)/shard_map/all_to_all | solution.py:155
  76.9 44.2 %collective-permute-start.6 = (bf16[144,1152]{1,0:T(8,128)(2,1)S(1)}, bf16[144,1152]{1,0:T(8,128)(2,1)S(1)}, u32[]{:S(2)}, u32[]{:S(2)}) collective-permute-start(bf16[144,1152]{1,0:T(8,128)(2,1)S(1)} %pad_maximum_fusion.4), channel_id=1, source_target_pairs={{0,4},{1,5},{2,6},{3,7},{4,0},{5,1},{6,2},{7,3},{8,12},{9,13},{10,... | collective-permute-start | bytes 995336 | tf_op jit(solution)/shard_map/ppermute | solution.py:25
  121.2 14.1 %collective-permute-start.7 = (bf16[144,1152]{1,0:T(8,128)(2,1)S(1)}, bf16[144,1152]{1,0:T(8,128)(2,1)S(1)}, u32[]{:S(2)}, u32[]{:S(2)}) collective-permute-start(bf16[144,1152]{1,0:T(8,128)(2,1)S(1)} %collective-permute-done.6), channel_id=1, source_target_pairs={{0,16},{8,24},{16,32},{24,40},{32,48},{40,56},{48,0},{56,8},{1,17}... | collective-permute-start | bytes 995336 | tf_op jit(solution)/shard_map/ppermute | solution.py:44
  125.7 32.0 %collective-permute-start.8 = (bf16[144,1152]{1,0:T(8,128)(2,1)S(1)}, bf16[144,1152]{1,0:T(8,128)(2,1)S(1)}, u32[]{:S(2)}, u32[]{:S(2)}) collective-permute-start(bf16[144,1152]{1,0:T(8,128)(2,1)S(1)} %collective-permute-done.6), channel_id=1, source_target_pairs={{0,32},{8,40},{16,48},{24,56},{32,0},{40,8},{48,16},{56,24},{1,33}... | collective-permute-start | bytes 995336 | tf_op jit(solution)/shard_map/ppermute | solution.py:44
  130.6 27.1 %collective-permute-start.9 = (bf16[144,1152]{1,0:T(8,128)(2,1)S(1)}, bf16[144,1152]{1,0:T(8,128)(2,1)S(1)}, u32[]{:S(2)}, u32[]{:S(2)}) collective-permute-start(bf16[144,1152]{1,0:T(8,128)(2,1)S(1)} %collective-permute-done.6), channel_id=1, source_target_pairs={{0,48},{8,56},{16,0},{24,8},{32,16},{40,24},{48,32},{56,40},{1,49}... | collective-permute-start | bytes 995336 | tf_op jit(solution)/shard_map/ppermute | solution.py:44
  157.9 12.7 %collective-permute-start.10 = (bf16[4,144,1152]{2,1,0:T(8,128)(2,1)S(1)}, bf16[4,144,1152]{2,1,0:T(8,128)(2,1)}, u32[]{:S(2)}, u32[]{:S(2)}) collective-permute-start(bf16[4,144,1152]{2,1,0:T(8,128)(2,1)S(1)} %pad_maximum_fusion.1), channel_id=1, source_target_pairs={{0,8},{8,0},{16,24},{24,16},{32,40},{40,32},{48,56},{56,48},{1,9},... | collective-permute-start | bytes 3981320 | tf_op jit(solution)/shard_map/ppermute | solution.py:29
  161.6 12.8 %collective-permute-start.3 = (bf16[2,64,1152]{2,1,0:T(8,128)(2,1)S(1)}, bf16[2,64,1152]{2,1,0:T(8,128)(2,1)S(1)}, u32[]{:S(2)}, u32[]{:S(2)}) collective-permute-start(bf16[2,64,1152]{2,1,0:T(8,128)(2,1)S(1)} %add_convert_fusion), channel_id=1, source_target_pairs={{0,2},{1,3},{2,4},{3,5},{4,6},{5,7},{6,0},{7,1},{8,14},{9,15},{10,... | collective-permute-start | bytes 884744 | tf_op jit(solution)/shard_map/ppermute | solution.py:39
  163.5 16.3 %collective-permute-start.4 = (bf16[2,64,1152]{2,1,0:T(8,128)(2,1)S(1)}, bf16[2,64,1152]{2,1,0:T(8,128)(2,1)S(1)}, u32[]{:S(2)}, u32[]{:S(2)}) collective-permute-start(bf16[2,64,1152]{2,1,0:T(8,128)(2,1)S(1)} %add_convert_fusion), channel_id=1, source_target_pairs={{0,1},{1,2},{2,3},{3,4},{4,5},{5,6},{6,7},{7,0},{8,15},{9,8},{10,9... | collective-permute-start | bytes 884744 | tf_op jit(solution)/shard_map/ppermute | solution.py:39
  165.5 14.3 %collective-permute-start.5 = (bf16[2,64,1152]{2,1,0:T(8,128)(2,1)S(1)}, bf16[2,64,1152]{2,1,0:T(8,128)(2,1)S(1)}, u32[]{:S(2)}, u32[]{:S(2)}) collective-permute-start(bf16[2,64,1152]{2,1,0:T(8,128)(2,1)S(1)} %add_convert_fusion), channel_id=1, source_target_pairs={{0,7},{1,0},{2,1},{3,2},{4,3},{5,4},{6,5},{7,6},{8,9},{9,10},{10,1... | collective-permute-start | bytes 884744 | tf_op jit(solution)/shard_map/ppermute | solution.py:39
  172.0 8.0 %copy-start.2 = (bf16[4,72,1152]{2,1,0:T(8,128)(2,1)S(1)}, bf16[4,72,1152]{2,1,0:T(8,128)(2,1)}, u32[]{:S(2)}) copy-start(bf16[4,72,1152]{2,1,0:T(8,128)(2,1)} %get-tuple-element.19) | copy-start | bytes 1990660
  172.0 8.0 %copy-start.4 = (bf16[1,1152,576]{1,2,0:T(8,128)(2,1)S(1)}, bf16[1,1152,576]{1,2,0:T(8,128)(2,1)}, u32[]{:S(2)}) copy-start(bf16[1,1152,576]{1,2,0:T(8,128)(2,1)} %param.12) | copy-start | bytes 3981316
  180.0 2.0 copy-start.5
  183.9 13.8 %collective-permute-start.11 = (bf16[2,64,1152]{2,1,0:T(8,128)(2,1)S(1)}, bf16[2,64,1152]{2,1,0:T(8,128)(2,1)S(1)}, u32[]{:S(2)}, u32[]{:S(2)}) collective-permute-start(bf16[2,64,1152]{2,1,0:T(8,128)(2,1)S(1)} %bitcast.80), channel_id=1, source_target_pairs={{0,6},{1,7},{2,0},{3,1},{4,2},{5,3},{6,4},{7,5},{8,10},{9,11},{10,... | collective-permute-start | bytes 884744 | tf_op jit(solution)/shard_map/ppermute | solution.py:39
  185.9 15.5 %collective-permute-start.12 = (bf16[2,64,1152]{2,1,0:T(8,128)(2,1)S(1)}, bf16[2,64,1152]{2,1,0:T(8,128)(2,1)S(1)}, u32[]{:S(2)}, u32[]{:S(2)}) collective-permute-start(bf16[2,64,1152]{2,1,0:T(8,128)(2,1)S(1)} %bitcast.79), channel_id=1, source_target_pairs={{0,7},{1,0},{2,1},{3,2},{4,3},{5,4},{6,5},{7,6},{8,9},{9,10},{10,1... | collective-permute-start | bytes 884744 | tf_op jit(solution)/shard_map/ppermute | solution.py:39
  189.4 12.2 %collective-permute-start.13 = (bf16[2,64,1152]{2,1,0:T(8,128)(2,1)S(1)}, bf16[2,64,1152]{2,1,0:T(8,128)(2,1)S(1)}, u32[]{:S(2)}, u32[]{:S(2)}) collective-permute-start(bf16[2,64,1152]{2,1,0:T(8,128)(2,1)S(1)} %bitcast.77), channel_id=1, source_target_pairs={{0,1},{1,2},{2,3},{3,4},{4,5},{5,6},{6,7},{7,0},{8,15},{9,8},{10,9... | collective-permute-start | bytes 884744 | tf_op jit(solution)/shard_map/ppermute | solution.py:39
  201.9 8.2 %collective-permute-start.16 = (bf16[64,1152]{1,0:T(8,128)(2,1)S(1)}, bf16[64,1152]{1,0:T(8,128)(2,1)S(1)}, u32[]{:S(2)}, u32[]{:S(2)}) collective-permute-start(bf16[64,1152]{1,0:T(8,128)(2,1)S(1)} %get-tuple-element.27), channel_id=1, source_target_pairs={{0,64},{64,128},{128,192},{192,0},{256,320},{320,384},{384,448},{4... | collective-permute-start | bytes 442376 | tf_op jit(solution)/shard_map/ppermute | solution.py:181
  205.3 15.4 %collective-permute-start.14 = (bf16[64,1152]{1,0:T(8,128)(2,1)S(1)}, bf16[64,1152]{1,0:T(8,128)(2,1)S(1)}, u32[]{:S(2)}, u32[]{:S(2)}) collective-permute-start(bf16[64,1152]{1,0:T(8,128)(2,1)S(1)} %get-tuple-element.26), channel_id=1, source_target_pairs={{192,448},{448,704},{704,192},{193,449},{449,705},{705,193},{194,4... | collective-permute-start | bytes 442376 | tf_op jit(solution)/shard_map/ppermute | solution.py:179
  210.2 17.6 %collective-permute-start.17 = (bf16[64,1152]{1,0:T(8,128)(2,1)S(1)}, bf16[64,1152]{1,0:T(8,128)(2,1)S(1)}, u32[]{:S(2)}, u32[]{:S(2)}) collective-permute-start(bf16[64,1152]{1,0:T(8,128)(2,1)S(1)} %collective-permute-done.16), channel_id=1, source_target_pairs={{0,256},{256,512},{512,0},{1,257},{257,513},{513,1},{2,258},{258,5... | collective-permute-start | bytes 442376 | tf_op jit(solution)/shard_map/ppermute | solution.py:179
  220.7 10.6 %collective-permute-start.15 = (bf16[64,1152]{1,0:T(8,128)(2,1)S(1)}, bf16[64,1152]{1,0:T(8,128)(2,1)S(1)}, u32[]{:S(2)}, u32[]{:S(2)}) collective-permute-start(bf16[64,1152]{1,0:T(8,128)(2,1)S(1)} %broadcast_select_fusion), channel_id=1, source_target_pairs={{0,64},{64,128},{128,192},{192,0},{256,320},{320,384},{384,448},{4... | collective-permute-start | bytes 442376 | tf_op jit(solution)/shard_map/ppermute | solution.py:184

commit v5 on v4

--- a/solution.py
+++ b/solution.py
@@ -180,11 +180,11 @@
 
     second = lax.ppermute(layer_out[1], "section", along_x)
     crossed = crossing(layer_out[0], 3)
-    first = jnp.where(place_x == 3, crossed, layer_out[0])
-    first = lax.ppermute(first, "section", along_x)
-    crossed = crossing(second, 0)
-    second = jnp.where(place_x == 0, crossed, second)
-    return jnp.stack([first, second])[None]
+    first = lax.ppermute(layer_out[0], "section", [(s, d) for s, d in along_x if d == s + 1])
+    crossed_second = crossing(second, 0)
+    first_end = lax.ppermute(crossed, "section", [(s, d) for s, d in along_x if d != s + 1])
+    arrived = [jnp.where(place_x == 0, first_end, first), jnp.where(place_x == 0, crossed_second, second)]
+    return jnp.stack(arrived)[None]
 
 
 def solution(mesh):

time: 233 us -> 233 us (level)
  the two profiles are of different devices: /device:TPU:192 before, /device:TPU:64 now
where the time goes in v5:
time: 233 us; the launch traced here: 232 us
  waiting for transfers between devices  133 us (57%)
  starting transfers between devices  73.4 us (32%)
  local copies, waits for them, and re-layouts  8.46 us (4%)
  Pallas kernels  7.76 us (3%)
  other arithmetic  5.08 us (2%)
  matrix products  3.79 us (2%)
    ppermute x3, waiting for transfers between devices, flip(): lax.ppermute(block, axis, [(i, i ^ 1) for i in range(lax.axis_size(axis))])  40.2 us
    ppermute x1, waiting for transfers between devices, rotate(): lax.ppermute(block, axis, [(i, (i + steps) % count) for i in range(count)])  36.4 us
    ppermute x3, waiting for transfers between devices, turn_z(): lax.ppermute(block, 'tm', [(i, (i + 2 * steps) % count) for i in range(co...  23.6 us
    ppermute x6, waiting for transfers between devices, mirrored(): return lax.ppermute(block, ('tm', 'space'), route)  17.7 us
    ppermute x6, starting transfers between devices, mirrored(): return lax.ppermute(block, ('tm', 'space'), route)  16.7 us
    ppermute x2, starting transfers between devices, crossing(): lax.ppermute(block, 'section', [(s, (s + 4) % sections) for s in range(x,...  10.8 us
    ppermute x3, starting transfers between devices, turn_z(): lax.ppermute(block, 'tm', [(i, (i + 2 * steps) % count) for i in range(co...  9.55 us
    ppermute x1, starting transfers between devices, rotate(): lax.ppermute(block, axis, [(i, (i + steps) % count) for i in range(count)])  7.84 us
  transfers between devices with their start and end apart: 21, of which 15 were waited for; matrix products, arithmetic and copies ran while one was open for 4% of the time, Pallas kernels for 0%

profile of v5, /device:TPU:64, one launch (start us, length us, event | category | flops | bytes accessed | tf_op | source)
XLA Modules:
  0.0 231.9 jit_solution(13647008973525547137)
XLA Ops:
  0.0 2.0 collective-permute-start
  4.8 3.6 %collective-permute-done = bf16[2,64,1152]{2,1,0:T(8,128)(2,1)S(1)} collective-permute-done((bf16[2,64,1152]{2,1,0:T(8,128)(2,1)}, bf16[2,64,1152]{2,1,0:T(8,128)(2,1)S(1)}, u32[]{:S(2)}, u32[]{:S(2)}) %collective-permute-start) | collective-permute-done | bytes 294944 | tf_op jit(solution)/shard_map/ppermute | solution.py:20
  10.4 7.2 %all-to-all-start = ((bf16[8,64,1152]{2,1,0:T(8,128)(2,1)}), bf16[8,64,1152]{2,1,0:T(8,128)(2,1)S(1)}, u32[]{:S(2)}, u32[]{:S(2)}) async-start(bf16[8,64,1152]{2,1,0:T(8,128)(2,1)} %bitcast.1), calls=%async_computation | async-start | bytes 2359296 | tf_op jit(solution)/shard_map/all_to_all | solution.py:146
  17.7 3.9 %collective-permute-start.1 = (bf16[4,72,1152]{2,1,0:T(8,128)(2,1)S(1)}, bf16[4,72,1152]{2,1,0:T(8,128)(2,1)S(1)}, u32[]{:S(2)}, u32[]{:S(2)}) collective-permute-start(bf16[4,72,1152]{2,1,0:T(8,128)(2,1)S(1)} %pad_maximum_fusion.3), channel_id=1, source_target_pairs={{0,1},{1,0},{2,3},{3,2},{4,5},{5,4},{6,7},{7,6},{8,9},{9,8},{10,11... | collective-permute-start | bytes 1990664 | tf_op jit(solution)/shard_map/ppermute | solution.py:29
  21.7 38.1 %collective-permute-done.1 = bf16[4,72,1152]{2,1,0:T(8,128)(2,1)S(1)} collective-permute-done((bf16[4,72,1152]{2,1,0:T(8,128)(2,1)S(1)}, bf16[4,72,1152]{2,1,0:T(8,128)(2,1)S(1)}, u32[]{:S(2)}, u32[]{:S(2)}) %collective-permute-start.1) | collective-permute-done | bytes 663584 | tf_op jit(solution)/shard_map/ppermute | solution.py:29
  61.7 2.1 collective-permute-done.2
  66.0 7.8 %frame_attention.1 = bf16[512,1152]{1,0:T(8,128)(2,1)} custom-call(bf16[512,1152]{1,0:T(8,128)(2,1)} %bitcast.59, bf16[432,1152]{1,0:T(8,128)(2,1)} %bitcast.61, bf16[144,1152]{1,0:T(8,128)(2,1)} %bitcast.65, bf16[576,1152]{1,0:T(8,128)(2,1)} %bitcast.57), custom_call_target="tpu_custom_call" | custom-call | tf_op jit(solution)/shard_map/frame_attention/pallas_call | solution.py:87
  73.7 5.8 %all-to-all-start.1 = ((bf16[8,64,1152]{2,1,0:T(8,128)(2,1)}), bf16[8,64,1152]{2,1,0:T(8,128)(2,1)S(1)}, u32[]{:S(2)}, u32[]{:S(2)}) async-start(bf16[8,64,1152]{2,1,0:T(8,128)(2,1)} %bitcast.58), calls=%async_computation.1 | async-start | bytes 2359296 | tf_op jit(solution)/shard_map/all_to_all | solution.py:155
  81.5 7.8 %collective-permute-start.6 = (bf16[144,1152]{1,0:T(8,128)(2,1)S(1)}, bf16[144,1152]{1,0:T(8,128)(2,1)S(1)}, u32[]{:S(2)}, u32[]{:S(2)}) collective-permute-start(bf16[144,1152]{1,0:T(8,128)(2,1)S(1)} %pad_maximum_fusion.4), channel_id=1, source_target_pairs={{0,4},{1,5},{2,6},{3,7},{4,0},{5,1},{6,2},{7,3},{8,12},{9,13},{10,... | collective-permute-start | bytes 995336 | tf_op jit(solution)/shard_map/ppermute | solution.py:25
  89.3 36.4 %collective-permute-done.6 = bf16[144,1152]{1,0:T(8,128)(2,1)S(1)} collective-permute-done((bf16[144,1152]{1,0:T(8,128)(2,1)S(1)}, bf16[144,1152]{1,0:T(8,128)(2,1)S(1)}, u32[]{:S(2)}, u32[]{:S(2)}) %collective-permute-start.6) | collective-permute-done | bytes 331808 | tf_op jit(solution)/shard_map/ppermute | solution.py:25
  125.7 4.3 %collective-permute-start.7 = (bf16[144,1152]{1,0:T(8,128)(2,1)S(1)}, bf16[144,1152]{1,0:T(8,128)(2,1)S(1)}, u32[]{:S(2)}, u32[]{:S(2)}) collective-permute-start(bf16[144,1152]{1,0:T(8,128)(2,1)S(1)} %collective-permute-done.6), channel_id=1, source_target_pairs={{0,16},{8,24},{16,32},{24,40},{32,48},{40,56},{48,0},{56,8},{1,17}... | collective-permute-start | bytes 995336 | tf_op jit(solution)/shard_map/ppermute | solution.py:44
  130.0 1.9 collective-permute-start.8
  131.9 3.4 %collective-permute-start.9 = (bf16[144,1152]{1,0:T(8,128)(2,1)S(1)}, bf16[144,1152]{1,0:T(8,128)(2,1)S(1)}, u32[]{:S(2)}, u32[]{:S(2)}) collective-permute-start(bf16[144,1152]{1,0:T(8,128)(2,1)S(1)} %collective-permute-done.6), channel_id=1, source_target_pairs={{0,48},{8,56},{16,0},{24,8},{32,16},{40,24},{48,32},{56,40},{1,49}... | collective-permute-start | bytes 995336 | tf_op jit(solution)/shard_map/ppermute | solution.py:44
  135.3 17.1 %collective-permute-done.7 = bf16[144,1152]{1,0:T(8,128)(2,1)S(1)} collective-permute-done((bf16[144,1152]{1,0:T(8,128)(2,1)S(1)}, bf16[144,1152]{1,0:T(8,128)(2,1)S(1)}, u32[]{:S(2)}, u32[]{:S(2)}) %collective-permute-start.7) | collective-permute-done | bytes 331808 | tf_op jit(solution)/shard_map/ppermute | solution.py:44
  152.4 6.2 %collective-permute-done.8 = bf16[144,1152]{1,0:T(8,128)(2,1)S(1)} collective-permute-done((bf16[144,1152]{1,0:T(8,128)(2,1)S(1)}, bf16[144,1152]{1,0:T(8,128)(2,1)S(1)}, u32[]{:S(2)}, u32[]{:S(2)}) %collective-permute-start.8) | collective-permute-done | bytes 331808 | tf_op jit(solution)/shard_map/ppermute | solution.py:44
  159.1 1.9 collective-permute-start.10
  162.8 1.9 collective-permute-start.3
  164.7 1.9 collective-permute-start.4
  166.6 5.1 %collective-permute-start.5 = (bf16[2,64,1152]{2,1,0:T(8,128)(2,1)S(1)}, bf16[2,64,1152]{2,1,0:T(8,128)(2,1)S(1)}, u32[]{:S(2)}, u32[]{:S(2)}) collective-permute-start(bf16[2,64,1152]{2,1,0:T(8,128)(2,1)S(1)} %add_convert_fusion), channel_id=1, source_target_pairs={{0,7},{1,0},{2,1},{3,2},{4,3},{5,4},{6,5},{7,6},{8,9},{9,10},{10,1... | collective-permute-start | bytes 884744 | tf_op jit(solution)/shard_map/ppermute | solution.py:39
  173.2 2.3 %collective-permute-done.3 = bf16[2,64,1152]{2,1,0:T(8,128)(2,1)S(1)} collective-permute-done((bf16[2,64,1152]{2,1,0:T(8,128)(2,1)S(1)}, bf16[2,64,1152]{2,1,0:T(8,128)(2,1)S(1)}, u32[]{:S(2)}, u32[]{:S(2)}) %collective-permute-start.3) | collective-permute-done | bytes 294944 | tf_op jit(solution)/shard_map/ppermute | solution.py:39
  175.5 5.5 %collective-permute-done.4 = bf16[2,64,1152]{2,1,0:T(8,128)(2,1)S(1)} collective-permute-done((bf16[2,64,1152]{2,1,0:T(8,128)(2,1)S(1)}, bf16[2,64,1152]{2,1,0:T(8,128)(2,1)S(1)}, u32[]{:S(2)}, u32[]{:S(2)}) %collective-permute-start.4) | collective-permute-done | bytes 294944 | tf_op jit(solution)/shard_map/ppermute | solution.py:39
  181.2 1.9 fusion.20
  185.1 1.9 collective-permute-start.11
  187.1 3.5 %collective-permute-start.12 = (bf16[2,64,1152]{2,1,0:T(8,128)(2,1)S(1)}, bf16[2,64,1152]{2,1,0:T(8,128)(2,1)S(1)}, u32[]{:S(2)}, u32[]{:S(2)}) collective-permute-start(bf16[2,64,1152]{2,1,0:T(8,128)(2,1)S(1)} %bitcast.78), channel_id=1, source_target_pairs={{0,7},{1,0},{2,1},{3,2},{4,3},{5,4},{6,5},{7,6},{8,9},{9,10},{10,1... | collective-permute-start | bytes 884744 | tf_op jit(solution)/shard_map/ppermute | solution.py:39
  190.5 2.4 %collective-permute-start.13 = (bf16[2,64,1152]{2,1,0:T(8,128)(2,1)S(1)}, bf16[2,64,1152]{2,1,0:T(8,128)(2,1)S(1)}, u32[]{:S(2)}, u32[]{:S(2)}) collective-permute-start(bf16[2,64,1152]{2,1,0:T(8,128)(2,1)S(1)} %bitcast.76), channel_id=1, source_target_pairs={{0,1},{1,2},{2,3},{3,4},{4,5},{5,6},{6,7},{7,0},{8,15},{9,8},{10,9... | collective-permute-start | bytes 884744 | tf_op jit(solution)/shard_map/ppermute | solution.py:39
  192.9 5.9 %collective-permute-done.11 = bf16[2,64,1152]{2,1,0:T(8,128)(2,1)S(1)} collective-permute-done((bf16[2,64,1152]{2,1,0:T(8,128)(2,1)S(1)}, bf16[2,64,1152]{2,1,0:T(8,128)(2,1)S(1)}, u32[]{:S(2)}, u32[]{:S(2)}) %collective-permute-start.11) | collective-permute-done | bytes 294944 | tf_op jit(solution)/shard_map/ppermute | solution.py:39
  198.8 3.8 %collective-permute-done.12 = bf16[2,64,1152]{2,1,0:T(8,128)(2,1)S(1)} collective-permute-done((bf16[2,64,1152]{2,1,0:T(8,128)(2,1)S(1)}, bf16[2,64,1152]{2,1,0:T(8,128)(2,1)S(1)}, u32[]{:S(2)}, u32[]{:S(2)}) %collective-permute-start.12) | collective-permute-done | bytes 294944 | tf_op jit(solution)/shard_map/ppermute | solution.py:39
  203.1 3.0 %collective-permute-start.17 = (bf16[64,1152]{1,0:T(8,128)(2,1)S(1)}, bf16[64,1152]{1,0:T(8,128)(2,1)S(1)}, u32[]{:S(2)}, u32[]{:S(2)}) collective-permute-start(bf16[64,1152]{1,0:T(8,128)(2,1)S(1)} %get-tuple-element.27), channel_id=1, source_target_pairs={{0,64},{64,128},{128,192},{192,0},{256,320},{320,384},{384,448},{4... | collective-permute-start | bytes 442376 | tf_op jit(solution)/shard_map/ppermute | solution.py:181
  206.8 4.6 %collective-permute-done.17 = bf16[64,1152]{1,0:T(8,128)(2,1)S(1)} collective-permute-done((bf16[64,1152]{1,0:T(8,128)(2,1)S(1)}, bf16[64,1152]{1,0:T(8,128)(2,1)S(1)}, u32[]{:S(2)}, u32[]{:S(2)}) %collective-permute-start.17) | collective-permute-done | bytes 147488 | tf_op jit(solution)/shard_map/ppermute | solution.py:181
  211.3 10.2 %collective-permute-start.18 = (bf16[64,1152]{1,0:T(8,128)(2,1)S(1)}, bf16[64,1152]{1,0:T(8,128)(2,1)S(1)}, u32[]{:S(2)}, u32[]{:S(2)}) collective-permute-start(bf16[64,1152]{1,0:T(8,128)(2,1)S(1)} %collective-permute-done.17), channel_id=1, source_target_pairs={{0,256},{256,512},{512,0},{1,257},{257,513},{513,1},{2,258},{258,5... | collective-permute-start | bytes 442376 | tf_op jit(solution)/shard_map/ppermute | solution.py:179
  224.1 3.5 %collective-permute-done.18 = bf16[64,1152]{1,0:T(8,128)(2,1)S(1)} collective-permute-done((bf16[64,1152]{1,0:T(8,128)(2,1)S(1)}, bf16[64,1152]{1,0:T(8,128)(2,1)S(1)}, u32[]{:S(2)}, u32[]{:S(2)}) %collective-permute-start.18) | collective-permute-done | bytes 147488 | tf_op jit(solution)/shard_map/ppermute | solution.py:179
  227.7 3.4 %collective-permute-done.15 = bf16[64,1152]{1,0:T(8,128)(2,1)S(1)} collective-permute-done((bf16[64,1152]{1,0:T(8,128)(2,1)S(1)}, bf16[64,1152]{1,0:T(8,128)(2,1)S(1)}, u32[]{:S(2)}, u32[]{:S(2)}) %collective-permute-start.15) | collective-permute-done | bytes 147488 | tf_op jit(solution)/shard_map/ppermute | solution.py:185
  (57 shorter events, 21.2 us)
Async XLA Ops:
  0.0 8.4 %copy-start.3 = (bf16[1,2,64,1152]{3,2,1,0:T(8,128)(2,1)S(1)}, bf16[1,2,64,1152]{3,2,1,0:T(8,128)(2,1)}, u32[]{:S(2)}) copy-start(bf16[1,2,64,1152]{3,2,1,0:T(8,128)(2,1)} %param.7) | copy-start | bytes 884740
  0.0 8.4 %collective-permute-start = (bf16[2,64,1152]{2,1,0:T(8,128)(2,1)}, bf16[2,64,1152]{2,1,0:T(8,128)(2,1)S(1)}, u32[]{:S(2)}, u32[]{:S(2)}) collective-permute-start(bf16[2,64,1152]{2,1,0:T(8,128)(2,1)} %bitcast.80), channel_id=1, source_target_pairs={{0,8},{8,16},{16,24},{24,32},{32,40},{40,48},{48,56},{1,9},{9,17},... | collective-permute-start | bytes 884744 | tf_op jit(solution)/shard_map/ppermute | solution.py:20
  10.4 7.2 %copy-start.1 = (bf16[1,144,1152]{2,1,0:T(8,128)(2,1)S(1)}, bf16[1,144,1152]{2,1,0:T(8,128)(2,1)}, u32[]{:S(2)}) copy-start(bf16[1,144,1152]{2,1,0:T(8,128)(2,1)} %param.11) | copy-start | bytes 995332
  10.4 54.5 %all-to-all-start = ((bf16[8,64,1152]{2,1,0:T(8,128)(2,1)}), bf16[8,64,1152]{2,1,0:T(8,128)(2,1)S(1)}, u32[]{:S(2)}, u32[]{:S(2)}) async-start(bf16[8,64,1152]{2,1,0:T(8,128)(2,1)} %bitcast.1), calls=%async_computation | async-start | bytes 2359296 | tf_op jit(solution)/shard_map/all_to_all | solution.py:146
  17.7 42.0 %collective-permute-start.1 = (bf16[4,72,1152]{2,1,0:T(8,128)(2,1)S(1)}, bf16[4,72,1152]{2,1,0:T(8,128)(2,1)S(1)}, u32[]{:S(2)}, u32[]{:S(2)}) collective-permute-start(bf16[4,72,1152]{2,1,0:T(8,128)(2,1)S(1)} %pad_maximum_fusion.3), channel_id=1, source_target_pairs={{0,1},{1,0},{2,3},{3,2},{4,5},{5,4},{6,7},{7,6},{8,9},{9,8},{10,11... | collective-permute-start | bytes 1990664 | tf_op jit(solution)/shard_map/ppermute | solution.py:29
  59.8 4.0 %collective-permute-start.2 = (bf16[4,72,1152]{2,1,0:T(8,128)(2,1)S(1)}, bf16[4,72,1152]{2,1,0:T(8,128)(2,1)S(1)}, u32[]{:S(2)}, u32[]{:S(2)}) collective-permute-start(bf16[4,72,1152]{2,1,0:T(8,128)(2,1)S(1)} %collective-permute-done.1), channel_id=1, source_target_pairs={{0,8},{8,0},{16,24},{24,16},{32,40},{40,32},{48,56},{56,48},{1,9},... | collective-permute-start | bytes 1990664 | tf_op jit(solution)/shard_map/ppermute | solution.py:29
  64.9 1.0 copy-start
  73.7 88.3 %all-to-all-start.1 = ((bf16[8,64,1152]{2,1,0:T(8,128)(2,1)}), bf16[8,64,1152]{2,1,0:T(8,128)(2,1)S(1)}, u32[]{:S(2)}, u32[]{:S(2)}) async-start(bf16[8,64,1152]{2,1,0:T(8,128)(2,1)} %bitcast.58), calls=%async_computation.1 | async-start | bytes 2359296 | tf_op jit(solution)/shard_map/all_to_all | solution.py:155
  81.5 44.3 %collective-permute-start.6 = (bf16[144,1152]{1,0:T(8,128)(2,1)S(1)}, bf16[144,1152]{1,0:T(8,128)(2,1)S(1)}, u32[]{:S(2)}, u32[]{:S(2)}) collective-permute-start(bf16[144,1152]{1,0:T(8,128)(2,1)S(1)} %pad_maximum_fusion.4), channel_id=1, source_target_pairs={{0,4},{1,5},{2,6},{3,7},{4,0},{5,1},{6,2},{7,3},{8,12},{9,13},{10,... | collective-permute-start | bytes 995336 | tf_op jit(solution)/shard_map/ppermute | solution.py:25
  125.7 26.7 %collective-permute-start.7 = (bf16[144,1152]{1,0:T(8,128)(2,1)S(1)}, bf16[144,1152]{1,0:T(8,128)(2,1)S(1)}, u32[]{:S(2)}, u32[]{:S(2)}) collective-permute-start(bf16[144,1152]{1,0:T(8,128)(2,1)S(1)} %collective-permute-done.6), channel_id=1, source_target_pairs={{0,16},{8,24},{16,32},{24,40},{32,48},{40,56},{48,0},{56,8},{1,17}... | collective-permute-start | bytes 995336 | tf_op jit(solution)/shard_map/ppermute | solution.py:44
  130.0 28.5 %collective-permute-start.8 = (bf16[144,1152]{1,0:T(8,128)(2,1)S(1)}, bf16[144,1152]{1,0:T(8,128)(2,1)S(1)}, u32[]{:S(2)}, u32[]{:S(2)}) collective-permute-start(bf16[144,1152]{1,0:T(8,128)(2,1)S(1)} %collective-permute-done.6), channel_id=1, source_target_pairs={{0,32},{8,40},{16,48},{24,56},{32,0},{40,8},{48,16},{56,24},{1,33}... | collective-permute-start | bytes 995336 | tf_op jit(solution)/shard_map/ppermute | solution.py:44
  131.9 27.0 %collective-permute-start.9 = (bf16[144,1152]{1,0:T(8,128)(2,1)S(1)}, bf16[144,1152]{1,0:T(8,128)(2,1)S(1)}, u32[]{:S(2)}, u32[]{:S(2)}) collective-permute-start(bf16[144,1152]{1,0:T(8,128)(2,1)S(1)} %collective-permute-done.6), channel_id=1, source_target_pairs={{0,48},{8,56},{16,0},{24,8},{32,16},{40,24},{48,32},{56,40},{1,49}... | collective-permute-start | bytes 995336 | tf_op jit(solution)/shard_map/ppermute | solution.py:44
  159.1 12.7 %collective-permute-start.10 = (bf16[4,144,1152]{2,1,0:T(8,128)(2,1)S(1)}, bf16[4,144,1152]{2,1,0:T(8,128)(2,1)}, u32[]{:S(2)}, u32[]{:S(2)}) collective-permute-start(bf16[4,144,1152]{2,1,0:T(8,128)(2,1)S(1)} %pad_maximum_fusion.1), channel_id=1, source_target_pairs={{0,8},{8,0},{16,24},{24,16},{32,40},{40,32},{48,56},{56,48},{1,9},... | collective-permute-start | bytes 3981320 | tf_op jit(solution)/shard_map/ppermute | solution.py:29
  162.8 12.8 %collective-permute-start.3 = (bf16[2,64,1152]{2,1,0:T(8,128)(2,1)S(1)}, bf16[2,64,1152]{2,1,0:T(8,128)(2,1)S(1)}, u32[]{:S(2)}, u32[]{:S(2)}) collective-permute-start(bf16[2,64,1152]{2,1,0:T(8,128)(2,1)S(1)} %add_convert_fusion), channel_id=1, source_target_pairs={{0,2},{1,3},{2,4},{3,5},{4,6},{5,7},{6,0},{7,1},{8,14},{9,15},{10,... | collective-permute-start | bytes 884744 | tf_op jit(solution)/shard_map/ppermute | solution.py:39
  164.7 16.3 %collective-permute-start.4 = (bf16[2,64,1152]{2,1,0:T(8,128)(2,1)S(1)}, bf16[2,64,1152]{2,1,0:T(8,128)(2,1)S(1)}, u32[]{:S(2)}, u32[]{:S(2)}) collective-permute-start(bf16[2,64,1152]{2,1,0:T(8,128)(2,1)S(1)} %add_convert_fusion), channel_id=1, source_target_pairs={{0,1},{1,2},{2,3},{3,4},{4,5},{5,6},{6,7},{7,0},{8,15},{9,8},{10,9... | collective-permute-start | bytes 884744 | tf_op jit(solution)/shard_map/ppermute | solution.py:39
  166.6 14.4 %collective-permute-start.5 = (bf16[2,64,1152]{2,1,0:T(8,128)(2,1)S(1)}, bf16[2,64,1152]{2,1,0:T(8,128)(2,1)S(1)}, u32[]{:S(2)}, u32[]{:S(2)}) collective-permute-start(bf16[2,64,1152]{2,1,0:T(8,128)(2,1)S(1)} %add_convert_fusion), channel_id=1, source_target_pairs={{0,7},{1,0},{2,1},{3,2},{4,3},{5,4},{6,5},{7,6},{8,9},{9,10},{10,1... | collective-permute-start | bytes 884744 | tf_op jit(solution)/shard_map/ppermute | solution.py:39
  173.2 8.0 %copy-start.2 = (bf16[4,72,1152]{2,1,0:T(8,128)(2,1)S(1)}, bf16[4,72,1152]{2,1,0:T(8,128)(2,1)}, u32[]{:S(2)}) copy-start(bf16[4,72,1152]{2,1,0:T(8,128)(2,1)} %get-tuple-element.19) | copy-start | bytes 1990660
  173.2 8.0 %copy-start.4 = (bf16[1,1152,576]{1,2,0:T(8,128)(2,1)S(1)}, bf16[1,1152,576]{1,2,0:T(8,128)(2,1)}, u32[]{:S(2)}) copy-start(bf16[1,1152,576]{1,2,0:T(8,128)(2,1)} %param.12) | copy-start | bytes 3981316
  181.2 2.0 copy-start.5
  185.1 13.7 %collective-permute-start.11 = (bf16[2,64,1152]{2,1,0:T(8,128)(2,1)S(1)}, bf16[2,64,1152]{2,1,0:T(8,128)(2,1)S(1)}, u32[]{:S(2)}, u32[]{:S(2)}) collective-permute-start(bf16[2,64,1152]{2,1,0:T(8,128)(2,1)S(1)} %bitcast.79), channel_id=1, source_target_pairs={{0,6},{1,7},{2,0},{3,1},{4,2},{5,3},{6,4},{7,5},{8,10},{9,11},{10,... | collective-permute-start | bytes 884744 | tf_op jit(solution)/shard_map/ppermute | solution.py:39
  187.1 15.5 %collective-permute-start.12 = (bf16[2,64,1152]{2,1,0:T(8,128)(2,1)S(1)}, bf16[2,64,1152]{2,1,0:T(8,128)(2,1)S(1)}, u32[]{:S(2)}, u32[]{:S(2)}) collective-permute-start(bf16[2,64,1152]{2,1,0:T(8,128)(2,1)S(1)} %bitcast.78), channel_id=1, source_target_pairs={{0,7},{1,0},{2,1},{3,2},{4,3},{5,4},{6,5},{7,6},{8,9},{9,10},{10,1... | collective-permute-start | bytes 884744 | tf_op jit(solution)/shard_map/ppermute | solution.py:39
  190.5 12.3 %collective-permute-start.13 = (bf16[2,64,1152]{2,1,0:T(8,128)(2,1)S(1)}, bf16[2,64,1152]{2,1,0:T(8,128)(2,1)S(1)}, u32[]{:S(2)}, u32[]{:S(2)}) collective-permute-start(bf16[2,64,1152]{2,1,0:T(8,128)(2,1)S(1)} %bitcast.76), channel_id=1, source_target_pairs={{0,1},{1,2},{2,3},{3,4},{4,5},{5,6},{6,7},{7,0},{8,15},{9,8},{10,9... | collective-permute-start | bytes 884744 | tf_op jit(solution)/shard_map/ppermute | solution.py:39
  203.1 8.2 %collective-permute-start.17 = (bf16[64,1152]{1,0:T(8,128)(2,1)S(1)}, bf16[64,1152]{1,0:T(8,128)(2,1)S(1)}, u32[]{:S(2)}, u32[]{:S(2)}) collective-permute-start(bf16[64,1152]{1,0:T(8,128)(2,1)S(1)} %get-tuple-element.27), channel_id=1, source_target_pairs={{0,64},{64,128},{128,192},{192,0},{256,320},{320,384},{384,448},{4... | collective-permute-start | bytes 442376 | tf_op jit(solution)/shard_map/ppermute | solution.py:181
  206.1 16.8 %collective-permute-start.14 = (bf16[64,1152]{1,0:T(8,128)(2,1)S(1)}, bf16[64,1152]{1,0:T(8,128)(2,1)S(1)}, u32[]{:S(2)}, u32[]{:S(2)}) collective-permute-start(bf16[64,1152]{1,0:T(8,128)(2,1)S(1)} %get-tuple-element.26), channel_id=1, source_target_pairs={{192,448},{448,704},{704,192},{193,449},{449,705},{705,193},{194,4... | collective-permute-start | bytes 442376 | tf_op jit(solution)/shard_map/ppermute | solution.py:179
  211.3 16.3 %collective-permute-start.18 = (bf16[64,1152]{1,0:T(8,128)(2,1)S(1)}, bf16[64,1152]{1,0:T(8,128)(2,1)S(1)}, u32[]{:S(2)}, u32[]{:S(2)}) collective-permute-start(bf16[64,1152]{1,0:T(8,128)(2,1)S(1)} %collective-permute-done.17), channel_id=1, source_target_pairs={{0,256},{256,512},{512,0},{1,257},{257,513},{513,1},{2,258},{258,5... | collective-permute-start | bytes 442376 | tf_op jit(solution)/shard_map/ppermute | solution.py:179
  221.5 6.2 %collective-permute-start.16 = (bf16[64,1152]{1,0:T(8,128)(2,1)S(1)}, bf16[64,1152]{1,0:T(8,128)(2,1)S(1)}, u32[]{:S(2)}, u32[]{:S(2)}) collective-permute-start(bf16[64,1152]{1,0:T(8,128)(2,1)S(1)} %get-tuple-element.26), channel_id=1, source_target_pairs={{0,64},{64,128},{128,192},{256,320},{320,384},{384,448},{512,576},... | collective-permute-start | bytes 442376 | tf_op jit(solution)/shard_map/ppermute | solution.py:183
  222.8 8.2 %collective-permute-start.15 = (bf16[64,1152]{1,0:T(8,128)(2,1)S(1)}, bf16[64,1152]{1,0:T(8,128)(2,1)S(1)}, u32[]{:S(2)}, u32[]{:S(2)}) collective-permute-start(bf16[64,1152]{1,0:T(8,128)(2,1)S(1)} %collective-permute-done.14), channel_id=1, source_target_pairs={{192,0},{448,256},{704,512},{193,1},{449,257},{705,513},{194,2},{4... | collective-permute-start | bytes 442376 | tf_op jit(solution)/shard_map/ppermute | solution.py:185

commit v6 on v5

--- a/solution.py
+++ b/solution.py
@@ -54,15 +54,12 @@
     return (normalize(values_in) * (1.0 + scale_row) + shift_row).astype(BF16)
 
 
-def attention_kernel(rows_ref, own_ref, own_out_ref, near_ref, part_ref, heads_ref):
+def attention_kernel(rows_ref, own_ref, near_ref, own_heads_ref, near_heads_ref, heads_ref):
     rows = rows_ref[...]
-    columns = own_out_ref.shape[0]
-    total = None
-    for side in range(2):
-        qkv_w = own_ref[...] if side == 0 else near_ref[: 3 * columns]
-        out_w = own_out_ref[...] if side == 0 else near_ref[3 * columns :]
+    columns = own_ref.shape[0] // 3
+    for qkv_ref, out_ref in ((own_ref, own_heads_ref), (near_ref, near_heads_ref)):
         projected = lax.dot_general(
-            qkv_w, rows, (((1,), (1,)), ((), ())), preferred_element_type=F32
+            qkv_ref[...], rows, (((1,), (1,)), ((), ())), preferred_element_type=F32
         )
         for head in range(columns // HEAD):
             q, k, v = (
@@ -75,21 +72,17 @@
             mass = jnp.sum(weight, axis=0, keepdims=True)
             mixed = jnp.dot(v, weight.astype(BF16), preferred_element_type=F32)
             heads_ref[head * HEAD : (head + 1) * HEAD] = mixed / mass
-        part = lax.dot_general(
-            heads_ref[...].astype(BF16), out_w, (((0,), (0,)), ((), ())), preferred_element_type=F32
-        )
-        total = part if total is None else total + part
-    part_ref[...] = total.astype(BF16)
-
-
-def attend(rows, qkv_own, out_own, near):
-    tokens, columns = rows.shape[0], out_own.shape[0]
+        out_ref[...] = heads_ref[...].T.astype(BF16)
+
+
+def attend(rows, qkv_own, qkv_near):
+    tokens, columns = rows.shape[0], qkv_own.shape[0] // 3
     return pl.pallas_call(
         attention_kernel,
-        out_shape=jax.ShapeDtypeStruct((tokens, D), BF16),
+        out_shape=[jax.ShapeDtypeStruct((tokens, columns), BF16)] * 2,
         scratch_shapes=[pltpu.VMEM((columns, tokens), F32)],
         name="frame_attention",
-    )(rows, qkv_own, out_own, near)
+    )(rows, qkv_own, qkv_near)
 
 
 def feed_forward(rows, up_w, down_w):
@@ -123,10 +116,23 @@
     share = up_own.shape[0] // members
 
     earlier = shifted(frames_in, "tm", 1)
-    near = jnp.concatenate([core_half(qkv_own, half), core_half(out_own, half)[None]], axis=0)
+    core = place % 2
+    out_share = out_own.shape[0] // (members - 2)
+    mine = lax.dynamic_slice_in_dim(
+        out_own, jnp.minimum(place, members - 3) * out_share, out_share, 0
+    )
+    out_rows = lax.all_to_all(
+        jnp.broadcast_to(mine[None], (n_space, out_share, D)), "space", 0, 0, tiled=True
+    )
+    out_rows = out_rows.reshape(n_space * out_share, D)
+    out_turned = [out_rows]
+    for k in range(1, members // 2):
+        out_turned.append(turn_z(out_rows, k))
+    near = core_half(qkv_own, half)
     near = flip(near, "space")
     near_more = flip(near, "tm")
-    near = jnp.concatenate([near, near_more], axis=1)
+    halves = [jnp.where(core == 0, near, near_more), jnp.where(core == 0, near_more, near)]
+    near = jnp.concatenate(halves, axis=1)
     far = jnp.concatenate(
         [lax.dynamic_slice_in_dim(w, place * share, share, 0) for w in (up_own, down_own)], axis=0
     )
@@ -145,15 +151,29 @@
     outgoing = jnp.broadcast_to(attn_in[None], (n_space // frames, frames, tokens, D))
     rows = lax.all_to_all(outgoing.reshape(n_space, tokens, D), "space", 0, 0, tiled=True)
     rows = rows.reshape(n_space * tokens, D)
-    attn_part = attend(rows, qkv_own.reshape(-1, D), out_own, near.reshape(-1, D))
-    attn_part = attn_part.reshape(n_space, tokens, D)
-    far = after(far, attn_part)
+    own_heads, near_heads = attend(rows, qkv_own.reshape(-1, D), near.reshape(-1, D))
+    odd = lax.axis_index("space") % 2 == 1
+    pair = [jnp.where(odd, near_heads, own_heads), jnp.where(odd, own_heads, near_heads)]
+    pair = jnp.concatenate(pair, axis=1).reshape(n_space, tokens, -1)
+    parts = lax.all_to_all(pair, "space", 0, 0, tiled=True)
+
+    out_turned = lax.optimization_barrier((*out_turned, own_heads))[:-1]
+    out_mine = jnp.zeros((members // 2, n_space * out_share, D), BF16)
+    for k, rows_k in enumerate(out_turned):
+        out_mine = lax.dynamic_update_slice_in_dim(
+            out_mine, rows_k[None], (place // 2 - k) % (members // 2), 0
+        )
+    out_other = flip(out_mine, "tm")
+    far = after(far, own_heads)
     turned = [far]
     for k in range(1, members // 2):
         turned.append(turn_z(far, k))
     far = jnp.stack(turned)
-    parts = lax.all_to_all(attn_part, "space", 0, 0, tiled=True)
-    attn_sum = jnp.sum(parts.reshape(n_space // frames, frames, tokens, D).astype(F32), axis=0)
+    by_core = [jnp.where(core == 0, out_mine, out_other), jnp.where(core == 0, out_other, out_mine)]
+    out_all = jnp.stack([w[: members // 2 - 1].reshape(-1, n_space, out_share, D) for w in by_core])
+    out_all = out_all.transpose(2, 1, 0, 3, 4).reshape(n_space // frames, -1, D)
+    parts = parts.reshape(n_space // frames, frames, tokens, -1)
+    attn_sum = jnp.einsum("jftc,jcd->ftd", parts, out_all, preferred_element_type=F32)
     hidden_state = mixed_f32 + mod_table[2] * attn_sum
     mlp_in = modulated(hidden_state, mod_table[3], mod_table[4])
     far_more = flip(far, "tm")

time: 233 us -> 265 us (1.14)
  the two profiles are of different devices: /device:TPU:64 before, /device:TPU:8 now
where the time goes in v6:
time: 265 us; the launch traced here: 263 us
  starting transfers between devices  125 us (47%)
  waiting for transfers between devices  102 us (38%)
  local copies, waits for them, and re-layouts  13.6 us (5%)
  other arithmetic  10.3 us (4%)
  Pallas kernels  6.33 us (2%)
  matrix products  5.56 us (2%)
    ppermute x6, starting transfers between devices, turn_z(): lax.ppermute(block, 'tm', [(i, (i + 2 * steps) % count) for i in range(co...  46 us
    ppermute x4, waiting for transfers between devices, flip(): lax.ppermute(block, axis, [(i, i ^ 1) for i in range(lax.axis_size(axis))])  31.3 us
    ppermute x6, starting transfers between devices, mirrored(): return lax.ppermute(block, ('tm', 'space'), route)  20.4 us
    ppermute x6, waiting for transfers between devices, turn_z(): lax.ppermute(block, 'tm', [(i, (i + 2 * steps) % count) for i in range(co...  17 us
    ppermute x6, waiting for transfers between devices, mirrored(): return lax.ppermute(block, ('tm', 'space'), route)  17 us
    ppermute x2, waiting for transfers between devices, crossing(): lax.ppermute(block, 'section', [(s, (s + 4) % sections) for s in range(x,...  13.4 us
    all_to_all x1, starting transfers between devices, body(): lax.all_to_all(jnp.broadcast_to(mine[None], (n_space, out_share, D)), 'sp...  12.4 us
    ppermute x2, starting transfers between devices, crossing(): lax.ppermute(block, 'section', [(s, (s + 4) % sections) for s in range(x,...  12.3 us
  transfers between devices with their start and end apart: 26, of which 11 were waited for; matrix products, arithmetic and copies ran while one was open for 7% of the time, Pallas kernels for 2%

profile of v6, /device:TPU:8, one launch (start us, length us, event | category | flops | bytes accessed | tf_op | source)
XLA Modules:
  0.0 263.3 jit_solution(5642804908276915541)
XLA Ops:
  2.7 12.4 %all-to-all-start.2 = ((bf16[8,24,1152]{2,1,0:T(8,128)(2,1)}), bf16[8,24,1152]{2,1,0:T(8,128)(2,1)S(1)}, u32[]{:S(2)}, u32[]{:S(2)}) async-start(bf16[8,24,1152]{2,1,0:T(8,128)(2,1)} %broadcast_in_dim.41), calls=%async_computation.2 | async-start | bytes 884736 | tf_op jit(solution)/shard_map/all_to_all | solution.py:124
  18.0 9.3 %all-to-all-done.2 = bf16[8,24,1152]{2,1,0:T(8,128)(2,1)S(1)} async-done(((bf16[8,24,1152]{2,1,0:T(8,128)(2,1)}), bf16[8,24,1152]{2,1,0:T(8,128)(2,1)S(1)}, u32[]{:S(2)}, u32[]{:S(2)}) %all-to-all-start.2) | async-done | bytes 442400 | tf_op jit(solution)/shard_map/all_to_all | solution.py:124
  28.5 4.9 %all-to-all-start = ((bf16[8,64,1152]{2,1,0:T(8,128)(2,1)}), bf16[8,64,1152]{2,1,0:T(8,128)(2,1)S(1)}, u32[]{:S(2)}, u32[]{:S(2)}) async-start(bf16[8,64,1152]{2,1,0:T(8,128)(2,1)} %bitcast.1), calls=%async_computation | async-start | bytes 2359296 | tf_op jit(solution)/shard_map/all_to_all | solution.py:152
  33.5 2.0 collective-permute-start.1
  35.6 31.3 %collective-permute-done.1 = bf16[3,72,1152]{2,1,0:T(8,128)(2,1)S(1)} collective-permute-done((bf16[3,72,1152]{2,1,0:T(8,128)(2,1)S(1)}, bf16[3,72,1152]{2,1,0:T(8,128)(2,1)S(1)}, u32[]{:S(2)}, u32[]{:S(2)}) %collective-permute-start.1) | collective-permute-done | bytes 497696 | tf_op jit(solution)/shard_map/ppermute | solution.py:29
  71.4 7.5 %collective-permute-start.10 = (bf16[144,1152]{1,0:T(8,128)(2,1)}, bf16[144,1152]{1,0:T(8,128)(2,1)}, u32[]{:S(2)}, u32[]{:S(2)}) collective-permute-start(bf16[144,1152]{1,0:T(8,128)(2,1)} %pad_maximum_fusion.4), channel_id=1, source_target_pairs={{0,4},{1,5},{2,6},{3,7},{4,0},{5,1},{6,2},{7,3},{8,12},{9,13},{10,... | collective-permute-start | bytes 995336 | tf_op jit(solution)/shard_map/ppermute | solution.py:25
  79.0 6.6 %collective-permute-start.3 = (bf16[192,1152]{1,0:T(8,128)(2,1)S(1)}, bf16[192,1152]{1,0:T(8,128)(2,1)}, u32[]{:S(2)}, u32[]{:S(2)}) collective-permute-start(bf16[192,1152]{1,0:T(8,128)(2,1)S(1)} %bitcast.90), channel_id=1, source_target_pairs={{0,16},{8,24},{16,32},{24,40},{32,48},{40,56},{48,0},{56,8},{1,17}... | collective-permute-start | bytes 1327112 | tf_op jit(solution)/shard_map/ppermute | solution.py:44
  85.7 3.7 %collective-permute-start.4 = (bf16[192,1152]{1,0:T(8,128)(2,1)S(1)}, bf16[192,1152]{1,0:T(8,128)(2,1)}, u32[]{:S(2)}, u32[]{:S(2)}) collective-permute-start(bf16[192,1152]{1,0:T(8,128)(2,1)S(1)} %bitcast.91), channel_id=1, source_target_pairs={{0,32},{8,40},{16,48},{24,56},{32,0},{40,8},{48,16},{56,24},{1,33}... | collective-permute-start | bytes 1327112 | tf_op jit(solution)/shard_map/ppermute | solution.py:44
  89.4 4.8 %collective-permute-start.5 = (bf16[192,1152]{1,0:T(8,128)(2,1)S(1)}, bf16[192,1152]{1,0:T(8,128)(2,1)}, u32[]{:S(2)}, u32[]{:S(2)}) collective-permute-start(bf16[192,1152]{1,0:T(8,128)(2,1)S(1)} %bitcast.92), channel_id=1, source_target_pairs={{0,48},{8,56},{16,0},{24,8},{32,16},{40,24},{48,32},{56,40},{1,49}... | collective-permute-start | bytes 1327112 | tf_op jit(solution)/shard_map/ppermute | solution.py:44
  96.5 6.3 %frame_attention.1 = (bf16[512,144]{1,0:T(8,128)(2,1)}, bf16[512,144]{1,0:T(8,128)(2,1)}) custom-call(bf16[512,1152]{1,0:T(8,128)(2,1)} %bitcast.87, bf16[432,1152]{1,0:T(8,128)(2,1)} %bitcast.89, bf16[432,1152]{1,0:T(8,128)(2,1)} %bitcast.88), custom_call_target="tpu_custom_call" | custom-call | tf_op jit(solution)/shard_map/frame_attention/pallas_call | solution.py:80
  104.7 2.5 collective-permute-start.12
  107.2 26.4 %collective-permute-start.11 = (bf16[144,1152]{1,0:T(8,128)(2,1)}, bf16[144,1152]{1,0:T(8,128)(2,1)S(1)}, u32[]{:S(2)}, u32[]{:S(2)}) collective-permute-start(bf16[144,1152]{1,0:T(8,128)(2,1)} %collective-permute-done.10), channel_id=1, source_target_pairs={{0,16},{8,24},{16,32},{24,40},{32,48},{40,56},{48,0},{56,8},{1,17}... | collective-permute-start | bytes 995336 | tf_op jit(solution)/shard_map/ppermute | solution.py:44
  136.0 17.0 %collective-permute-done.12 = bf16[144,1152]{1,0:T(8,128)(2,1)S(1)} collective-permute-done((bf16[144,1152]{1,0:T(8,128)(2,1)}, bf16[144,1152]{1,0:T(8,128)(2,1)S(1)}, u32[]{:S(2)}, u32[]{:S(2)}) %collective-permute-start.12) | collective-permute-done | bytes 331808 | tf_op jit(solution)/shard_map/ppermute | solution.py:44
  154.2 1.9 collective-permute-start.14
  157.2 2.4 collective-permute-start.6
  161.6 4.5 %all-to-all-start.1 = ((bf16[8,64,288]{2,1,0:T(8,128)(2,1)}), bf16[8,64,288]{2,1,0:T(8,128)(2,1)}, u32[]{:S(2)}, u32[]{:S(2)}) async-start(bf16[8,64,288]{2,1,0:T(8,128)(2,1)} %bitcast.94), calls=%async_computation.1 | async-start | bytes 786432 | tf_op jit(solution)/shard_map/all_to_all | solution.py:158
  167.3 2.5 fusion.43
  171.9 8.1 %all-to-all-done.1 = bf16[8,64,288]{2,1,0:T(8,128)(2,1)} async-done(((bf16[8,64,288]{2,1,0:T(8,128)(2,1)}), bf16[8,64,288]{2,1,0:T(8,128)(2,1)}, u32[]{:S(2)}, u32[]{:S(2)}) %all-to-all-start.1) | async-done | bytes 294944 | tf_op jit(solution)/shard_map/all_to_all | solution.py:158
  182.2 3.5 %collective-permute-start.9 = (bf16[2,64,1152]{2,1,0:T(8,128)(2,1)S(1)}, bf16[2,64,1152]{2,1,0:T(8,128)(2,1)S(1)}, u32[]{:S(2)}, u32[]{:S(2)}) collective-permute-start(bf16[2,64,1152]{2,1,0:T(8,128)(2,1)S(1)} %add_convert_fusion), channel_id=1, source_target_pairs={{0,7},{1,0},{2,1},{3,2},{4,3},{5,4},{6,5},{7,6},{8,9},{9,10},{10,1... | collective-permute-start | bytes 884744 | tf_op jit(solution)/shard_map/ppermute | solution.py:39
  185.6 2.5 collective-permute-start.8
  188.1 3.3 %collective-permute-start.7 = (bf16[2,64,1152]{2,1,0:T(8,128)(2,1)S(1)}, bf16[2,64,1152]{2,1,0:T(8,128)(2,1)S(1)}, u32[]{:S(2)}, u32[]{:S(2)}) collective-permute-start(bf16[2,64,1152]{2,1,0:T(8,128)(2,1)S(1)} %add_convert_fusion), channel_id=1, source_target_pairs={{0,2},{1,3},{2,4},{3,5},{4,6},{5,7},{6,0},{7,1},{8,14},{9,15},{10,... | collective-permute-start | bytes 884744 | tf_op jit(solution)/shard_map/ppermute | solution.py:39
  194.3 6.5 %collective-permute-done.7 = bf16[2,64,1152]{2,1,0:T(8,128)(2,1)S(1)} collective-permute-done((bf16[2,64,1152]{2,1,0:T(8,128)(2,1)S(1)}, bf16[2,64,1152]{2,1,0:T(8,128)(2,1)S(1)}, u32[]{:S(2)}, u32[]{:S(2)}) %collective-permute-start.7) | collective-permute-done | bytes 294944 | tf_op jit(solution)/shard_map/ppermute | solution.py:39
  201.0 2.0 fusion.22
  204.9 1.9 collective-permute-start.17
  206.9 4.6 %collective-permute-start.16 = (bf16[2,64,1152]{2,1,0:T(8,128)(2,1)S(1)}, bf16[2,64,1152]{2,1,0:T(8,128)(2,1)S(1)}, u32[]{:S(2)}, u32[]{:S(2)}) collective-permute-start(bf16[2,64,1152]{2,1,0:T(8,128)(2,1)S(1)} %bitcast.107), channel_id=1, source_target_pairs={{0,7},{1,0},{2,1},{3,2},{4,3},{5,4},{6,5},{7,6},{8,9},{9,10},{10,1... | collective-permute-start | bytes 884744 | tf_op jit(solution)/shard_map/ppermute | solution.py:39
  211.5 4.6 %collective-permute-start.15 = (bf16[2,64,1152]{2,1,0:T(8,128)(2,1)S(1)}, bf16[2,64,1152]{2,1,0:T(8,128)(2,1)S(1)}, u32[]{:S(2)}, u32[]{:S(2)}) collective-permute-start(bf16[2,64,1152]{2,1,0:T(8,128)(2,1)S(1)} %bitcast.105), channel_id=1, source_target_pairs={{0,6},{1,7},{2,0},{3,1},{4,2},{5,3},{6,4},{7,5},{8,10},{9,11},{10,... | collective-permute-start | bytes 884744 | tf_op jit(solution)/shard_map/ppermute | solution.py:39
  216.1 7.9 %collective-permute-done.15 = bf16[2,64,1152]{2,1,0:T(8,128)(2,1)S(1)} collective-permute-done((bf16[2,64,1152]{2,1,0:T(8,128)(2,1)S(1)}, bf16[2,64,1152]{2,1,0:T(8,128)(2,1)S(1)}, u32[]{:S(2)}, u32[]{:S(2)}) %collective-permute-start.15) | collective-permute-done | bytes 294944 | tf_op jit(solution)/shard_map/ppermute | solution.py:39
  224.2 4.2 %collective-permute-start.21 = (bf16[64,1152]{1,0:T(8,128)(2,1)S(1)}, bf16[64,1152]{1,0:T(8,128)(2,1)S(1)}, u32[]{:S(2)}, u32[]{:S(2)}) collective-permute-start(bf16[64,1152]{1,0:T(8,128)(2,1)S(1)} %get-tuple-element.45), channel_id=1, source_target_pairs={{0,64},{64,128},{128,192},{192,0},{256,320},{320,384},{384,448},{4... | collective-permute-start | bytes 442376 | tf_op jit(solution)/shard_map/ppermute | solution.py:201
  229.1 3.8 %collective-permute-done.21 = bf16[64,1152]{1,0:T(8,128)(2,1)S(1)} collective-permute-done((bf16[64,1152]{1,0:T(8,128)(2,1)S(1)}, bf16[64,1152]{1,0:T(8,128)(2,1)S(1)}, u32[]{:S(2)}, u32[]{:S(2)}) %collective-permute-start.21) | collective-permute-done | bytes 147488 | tf_op jit(solution)/shard_map/ppermute | solution.py:201
  232.8 11.6 %collective-permute-start.22 = (bf16[64,1152]{1,0:T(8,128)(2,1)S(1)}, bf16[64,1152]{1,0:T(8,128)(2,1)S(1)}, u32[]{:S(2)}, u32[]{:S(2)}) collective-permute-start(bf16[64,1152]{1,0:T(8,128)(2,1)S(1)} %collective-permute-done.21), channel_id=1, source_target_pairs={{0,256},{256,512},{512,0},{1,257},{257,513},{513,1},{2,258},{258,5... | collective-permute-start | bytes 442376 | tf_op jit(solution)/shard_map/ppermute | solution.py:199
  247.1 13.4 %collective-permute-done.22 = bf16[64,1152]{1,0:T(8,128)(2,1)S(1)} collective-permute-done((bf16[64,1152]{1,0:T(8,128)(2,1)S(1)}, bf16[64,1152]{1,0:T(8,128)(2,1)S(1)}, u32[]{:S(2)}, u32[]{:S(2)}) %collective-permute-start.22) | collective-permute-done | bytes 147488 | tf_op jit(solution)/shard_map/ppermute | solution.py:199
  260.5 1.9 collective-permute-done.19
  (90 shorter events, 36.6 us)
Async XLA Ops:
  0.0 16.7 %copy-start.9 = (bf16[1,2,64,1152]{3,2,1,0:T(8,128)(2,1)S(1)}, bf16[1,2,64,1152]{3,2,1,0:T(8,128)(2,1)}, u32[]{:S(2)}) copy-start(bf16[1,2,64,1152]{3,2,1,0:T(8,128)(2,1)} %param.7) | copy-start | bytes 884740
  0.0 16.7 %collective-permute-start = (bf16[2,64,1152]{2,1,0:T(8,128)(2,1)}, bf16[2,64,1152]{2,1,0:T(8,128)(2,1)S(1)}, u32[]{:S(2)}, u32[]{:S(2)}) collective-permute-start(bf16[2,64,1152]{2,1,0:T(8,128)(2,1)} %bitcast.110), channel_id=1, source_target_pairs={{0,8},{8,16},{16,24},{24,32},{32,40},{40,48},{48,56},{1,9},{9,17},... | collective-permute-start | bytes 884744 | tf_op jit(solution)/shard_map/ppermute | solution.py:20
  2.7 24.6 %all-to-all-start.2 = ((bf16[8,24,1152]{2,1,0:T(8,128)(2,1)}), bf16[8,24,1152]{2,1,0:T(8,128)(2,1)S(1)}, u32[]{:S(2)}, u32[]{:S(2)}) async-start(bf16[8,24,1152]{2,1,0:T(8,128)(2,1)} %broadcast_in_dim.41), calls=%async_computation.2 | async-start | bytes 884736 | tf_op jit(solution)/shard_map/all_to_all | solution.py:124
  18.0 15.5 %copy-start.4 = (bf16[1,1152,3,144]{1,3,2,0:T(8,128)(2,1)S(1)}, bf16[1,1152,3,144]{1,3,2,0:T(8,128)(2,1)}, u32[]{:S(2)}) copy-start(bf16[1,1152,3,144]{1,3,2,0:T(8,128)(2,1)} %param.10) | copy-start | bytes 2985988
  28.5 66.9 %all-to-all-start = ((bf16[8,64,1152]{2,1,0:T(8,128)(2,1)}), bf16[8,64,1152]{2,1,0:T(8,128)(2,1)S(1)}, u32[]{:S(2)}, u32[]{:S(2)}) async-start(bf16[8,64,1152]{2,1,0:T(8,128)(2,1)} %bitcast.1), calls=%async_computation | async-start | bytes 2359296 | tf_op jit(solution)/shard_map/all_to_all | solution.py:152
  33.5 33.3 %collective-permute-start.1 = (bf16[3,72,1152]{2,1,0:T(8,128)(2,1)S(1)}, bf16[3,72,1152]{2,1,0:T(8,128)(2,1)S(1)}, u32[]{:S(2)}, u32[]{:S(2)}) collective-permute-start(bf16[3,72,1152]{2,1,0:T(8,128)(2,1)S(1)} %dynamic-slice_bitcast_fusion), channel_id=1, source_target_pairs={{0,1},{1,0},{2,3},{3,2},{4,5},{5,4},{6,7},{7,6},{8,9},{9,8},{10,11... | collective-permute-start | bytes 1493000 | tf_op jit(solution)/shard_map/ppermute | solution.py:29
  66.8 27.4 %collective-permute-start.2 = (bf16[3,72,1152]{2,1,0:T(8,128)(2,1)S(1)}, bf16[3,72,1152]{2,1,0:T(8,128)(2,1)S(1)}, u32[]{:S(2)}, u32[]{:S(2)}) collective-permute-start(bf16[3,72,1152]{2,1,0:T(8,128)(2,1)S(1)} %collective-permute-done.1), channel_id=1, source_target_pairs={{0,8},{8,0},{16,24},{24,16},{32,40},{40,32},{48,56},{56,48},{1,9},... | collective-permute-start | bytes 1493000 | tf_op jit(solution)/shard_map/ppermute | solution.py:29
  71.4 31.4 %collective-permute-start.10 = (bf16[144,1152]{1,0:T(8,128)(2,1)}, bf16[144,1152]{1,0:T(8,128)(2,1)}, u32[]{:S(2)}, u32[]{:S(2)}) collective-permute-start(bf16[144,1152]{1,0:T(8,128)(2,1)} %pad_maximum_fusion.4), channel_id=1, source_target_pairs={{0,4},{1,5},{2,6},{3,7},{4,0},{5,1},{6,2},{7,3},{8,12},{9,13},{10,... | collective-permute-start | bytes 995336 | tf_op jit(solution)/shard_map/ppermute | solution.py:25
  79.0 28.2 %collective-permute-start.3 = (bf16[192,1152]{1,0:T(8,128)(2,1)S(1)}, bf16[192,1152]{1,0:T(8,128)(2,1)}, u32[]{:S(2)}, u32[]{:S(2)}) collective-permute-start(bf16[192,1152]{1,0:T(8,128)(2,1)S(1)} %bitcast.90), channel_id=1, source_target_pairs={{0,16},{8,24},{16,32},{24,40},{32,48},{40,56},{48,0},{56,8},{1,17}... | collective-permute-start | bytes 1327112 | tf_op jit(solution)/shard_map/ppermute | solution.py:44
  85.7 48.0 %collective-permute-start.4 = (bf16[192,1152]{1,0:T(8,128)(2,1)S(1)}, bf16[192,1152]{1,0:T(8,128)(2,1)}, u32[]{:S(2)}, u32[]{:S(2)}) collective-permute-start(bf16[192,1152]{1,0:T(8,128)(2,1)S(1)} %bitcast.91), channel_id=1, source_target_pairs={{0,32},{8,40},{16,48},{24,56},{32,0},{40,8},{48,16},{56,24},{1,33}... | collective-permute-start | bytes 1327112 | tf_op jit(solution)/shard_map/ppermute | solution.py:44
  89.4 44.3 %collective-permute-start.5 = (bf16[192,1152]{1,0:T(8,128)(2,1)S(1)}, bf16[192,1152]{1,0:T(8,128)(2,1)}, u32[]{:S(2)}, u32[]{:S(2)}) collective-permute-start(bf16[192,1152]{1,0:T(8,128)(2,1)S(1)} %bitcast.92), channel_id=1, source_target_pairs={{0,48},{8,56},{16,0},{24,8},{32,16},{40,24},{48,32},{56,40},{1,49}... | collective-permute-start | bytes 1327112 | tf_op jit(solution)/shard_map/ppermute | solution.py:44
  102.8 33.2 %collective-permute-start.13 = (bf16[144,1152]{1,0:T(8,128)(2,1)}, bf16[144,1152]{1,0:T(8,128)(2,1)S(1)}, u32[]{:S(2)}, u32[]{:S(2)}) collective-permute-start(bf16[144,1152]{1,0:T(8,128)(2,1)} %collective-permute-done.10), channel_id=1, source_target_pairs={{0,48},{8,56},{16,0},{24,8},{32,16},{40,24},{48,32},{56,40},{1,49}... | collective-permute-start | bytes 995336 | tf_op jit(solution)/shard_map/ppermute | solution.py:44
  104.7 48.3 %collective-permute-start.12 = (bf16[144,1152]{1,0:T(8,128)(2,1)}, bf16[144,1152]{1,0:T(8,128)(2,1)S(1)}, u32[]{:S(2)}, u32[]{:S(2)}) collective-permute-start(bf16[144,1152]{1,0:T(8,128)(2,1)} %collective-permute-done.10), channel_id=1, source_target_pairs={{0,32},{8,40},{16,48},{24,56},{32,0},{40,8},{48,16},{56,24},{1,33}... | collective-permute-start | bytes 995336 | tf_op jit(solution)/shard_map/ppermute | solution.py:44
  107.2 45.8 %collective-permute-start.11 = (bf16[144,1152]{1,0:T(8,128)(2,1)}, bf16[144,1152]{1,0:T(8,128)(2,1)S(1)}, u32[]{:S(2)}, u32[]{:S(2)}) collective-permute-start(bf16[144,1152]{1,0:T(8,128)(2,1)} %collective-permute-done.10), channel_id=1, source_target_pairs={{0,16},{8,24},{16,32},{24,40},{32,48},{40,56},{48,0},{56,8},{1,17}... | collective-permute-start | bytes 995336 | tf_op jit(solution)/shard_map/ppermute | solution.py:44
  154.2 13.1 %collective-permute-start.14 = (bf16[4,144,1152]{2,1,0:T(8,128)(2,1)S(1)}, bf16[4,144,1152]{2,1,0:T(8,128)(2,1)}, u32[]{:S(2)}, u32[]{:S(2)}) collective-permute-start(bf16[4,144,1152]{2,1,0:T(8,128)(2,1)S(1)} %pad_maximum_fusion), channel_id=1, source_target_pairs={{0,8},{8,0},{16,24},{24,16},{32,40},{40,32},{48,56},{56,48},{1,9},... | collective-permute-start | bytes 3981320 | tf_op jit(solution)/shard_map/ppermute | solution.py:29
  157.2 12.6 %collective-permute-start.6 = (bf16[4,192,1152]{2,1,0:T(8,128)(2,1)S(1)}, bf16[4,192,1152]{2,1,0:T(8,128)(2,1)}, u32[]{:S(2)}, u32[]{:S(2)}) collective-permute-start(bf16[4,192,1152]{2,1,0:T(8,128)(2,1)S(1)} %bitcast_dynamic-update-slice_fusion), channel_id=1, source_target_pairs={{0,8},{8,0},{16,24},{24,16},{32,40},{40,32},{48,56},{56,48},{1,9},... | collective-permute-start | bytes 5308424 | tf_op jit(solution)/shard_map/ppermute | solution.py:29
  161.6 18.4 %all-to-all-start.1 = ((bf16[8,64,288]{2,1,0:T(8,128)(2,1)}), bf16[8,64,288]{2,1,0:T(8,128)(2,1)}, u32[]{:S(2)}, u32[]{:S(2)}) async-start(bf16[8,64,288]{2,1,0:T(8,128)(2,1)} %bitcast.94), calls=%async_computation.1 | async-start | bytes 786432 | tf_op jit(solution)/shard_map/all_to_all | solution.py:158
  171.7 8.3 %copy-start.3 = (bf16[2,64,1152]{2,1,0:T(8,128)(2,1)S(1)}, bf16[2,64,1152]{2,1,0:T(8,128)(2,1)}, u32[]{:S(2)}) copy-start(bf16[2,64,1152]{2,1,0:T(8,128)(2,1)} %copy-done.2) | copy-start | bytes 884740
  182.1 18.8 %copy-start.6 = (bf16[4,72,1152]{2,1,0:T(8,128)(2,1)S(1)}, bf16[4,72,1152]{2,1,0:T(8,128)(2,1)}, u32[]{:S(2)}) copy-start(bf16[4,72,1152]{2,1,0:T(8,128)(2,1)} %get-tuple-element.33) | copy-start | bytes 1990660
  182.1 18.8 %copy-start.8 = (bf16[4,72,1152]{2,1,0:T(8,128)(2,1)S(1)}, bf16[4,72,1152]{2,1,0:T(8,128)(2,1)}, u32[]{:S(2)}) copy-start(bf16[4,72,1152]{2,1,0:T(8,128)(2,1)} %get-tuple-element.35) | copy-start | bytes 1990660
  182.1 18.8 %copy-start.10 = (bf16[1,1152,576]{1,2,0:T(8,128)(2,1)S(1)}, bf16[1,1152,576]{1,2,0:T(8,128)(2,1)}, u32[]{:S(2)}) copy-start(bf16[1,1152,576]{1,2,0:T(8,128)(2,1)} %param.12) | copy-start | bytes 3981316
  182.2 10.8 %collective-permute-start.9 = (bf16[2,64,1152]{2,1,0:T(8,128)(2,1)S(1)}, bf16[2,64,1152]{2,1,0:T(8,128)(2,1)S(1)}, u32[]{:S(2)}, u32[]{:S(2)}) collective-permute-start(bf16[2,64,1152]{2,1,0:T(8,128)(2,1)S(1)} %add_convert_fusion), channel_id=1, source_target_pairs={{0,7},{1,0},{2,1},{3,2},{4,3},{5,4},{6,5},{7,6},{8,9},{9,10},{10,1... | collective-permute-start | bytes 884744 | tf_op jit(solution)/shard_map/ppermute | solution.py:39
  185.6 8.6 %collective-permute-start.8 = (bf16[2,64,1152]{2,1,0:T(8,128)(2,1)S(1)}, bf16[2,64,1152]{2,1,0:T(8,128)(2,1)S(1)}, u32[]{:S(2)}, u32[]{:S(2)}) collective-permute-start(bf16[2,64,1152]{2,1,0:T(8,128)(2,1)S(1)} %add_convert_fusion), channel_id=1, source_target_pairs={{0,1},{1,2},{2,3},{3,4},{4,5},{5,6},{6,7},{7,0},{8,15},{9,8},{10,9... | collective-permute-start | bytes 884744 | tf_op jit(solution)/shard_map/ppermute | solution.py:39
  188.1 12.6 %collective-permute-start.7 = (bf16[2,64,1152]{2,1,0:T(8,128)(2,1)S(1)}, bf16[2,64,1152]{2,1,0:T(8,128)(2,1)S(1)}, u32[]{:S(2)}, u32[]{:S(2)}) collective-permute-start(bf16[2,64,1152]{2,1,0:T(8,128)(2,1)S(1)} %add_convert_fusion), channel_id=1, source_target_pairs={{0,2},{1,3},{2,4},{3,5},{4,6},{5,7},{6,0},{7,1},{8,14},{9,15},{10,... | collective-permute-start | bytes 884744 | tf_op jit(solution)/shard_map/ppermute | solution.py:39
  204.9 11.1 %collective-permute-start.17 = (bf16[2,64,1152]{2,1,0:T(8,128)(2,1)S(1)}, bf16[2,64,1152]{2,1,0:T(8,128)(2,1)S(1)}, u32[]{:S(2)}, u32[]{:S(2)}) collective-permute-start(bf16[2,64,1152]{2,1,0:T(8,128)(2,1)S(1)} %bitcast.109), channel_id=1, source_target_pairs={{0,1},{1,2},{2,3},{3,4},{4,5},{5,6},{6,7},{7,0},{8,15},{9,8},{10,9... | collective-permute-start | bytes 884744 | tf_op jit(solution)/shard_map/ppermute | solution.py:39
  206.9 9.2 %collective-permute-start.16 = (bf16[2,64,1152]{2,1,0:T(8,128)(2,1)S(1)}, bf16[2,64,1152]{2,1,0:T(8,128)(2,1)S(1)}, u32[]{:S(2)}, u32[]{:S(2)}) collective-permute-start(bf16[2,64,1152]{2,1,0:T(8,128)(2,1)S(1)} %bitcast.107), channel_id=1, source_target_pairs={{0,7},{1,0},{2,1},{3,2},{4,3},{5,4},{6,5},{7,6},{8,9},{9,10},{10,1... | collective-permute-start | bytes 884744 | tf_op jit(solution)/shard_map/ppermute | solution.py:39
  211.5 12.5 %collective-permute-start.15 = (bf16[2,64,1152]{2,1,0:T(8,128)(2,1)S(1)}, bf16[2,64,1152]{2,1,0:T(8,128)(2,1)S(1)}, u32[]{:S(2)}, u32[]{:S(2)}) collective-permute-start(bf16[2,64,1152]{2,1,0:T(8,128)(2,1)S(1)} %bitcast.105), channel_id=1, source_target_pairs={{0,6},{1,7},{2,0},{3,1},{4,2},{5,3},{6,4},{7,5},{8,10},{9,11},{10,... | collective-permute-start | bytes 884744 | tf_op jit(solution)/shard_map/ppermute | solution.py:39
  224.2 8.6 %collective-permute-start.21 = (bf16[64,1152]{1,0:T(8,128)(2,1)S(1)}, bf16[64,1152]{1,0:T(8,128)(2,1)S(1)}, u32[]{:S(2)}, u32[]{:S(2)}) collective-permute-start(bf16[64,1152]{1,0:T(8,128)(2,1)S(1)} %get-tuple-element.45), channel_id=1, source_target_pairs={{0,64},{64,128},{128,192},{192,0},{256,320},{320,384},{384,448},{4... | collective-permute-start | bytes 442376 | tf_op jit(solution)/shard_map/ppermute | solution.py:201
  228.4 17.4 %collective-permute-start.18 = (bf16[64,1152]{1,0:T(8,128)(2,1)S(1)}, bf16[64,1152]{1,0:T(8,128)(2,1)S(1)}, u32[]{:S(2)}, u32[]{:S(2)}) collective-permute-start(bf16[64,1152]{1,0:T(8,128)(2,1)S(1)} %get-tuple-element.44), channel_id=1, source_target_pairs={{192,448},{448,704},{704,192},{193,449},{449,705},{705,193},{194,4... | collective-permute-start | bytes 442376 | tf_op jit(solution)/shard_map/ppermute | solution.py:199
  232.8 27.7 %collective-permute-start.22 = (bf16[64,1152]{1,0:T(8,128)(2,1)S(1)}, bf16[64,1152]{1,0:T(8,128)(2,1)S(1)}, u32[]{:S(2)}, u32[]{:S(2)}) collective-permute-start(bf16[64,1152]{1,0:T(8,128)(2,1)S(1)} %collective-permute-done.21), channel_id=1, source_target_pairs={{0,256},{256,512},{512,0},{1,257},{257,513},{513,1},{2,258},{258,5... | collective-permute-start | bytes 442376 | tf_op jit(solution)/shard_map/ppermute | solution.py:199
  244.5 16.1 %collective-permute-start.20 = (bf16[64,1152]{1,0:T(8,128)(2,1)S(1)}, bf16[64,1152]{1,0:T(8,128)(2,1)S(1)}, u32[]{:S(2)}, u32[]{:S(2)}) collective-permute-start(bf16[64,1152]{1,0:T(8,128)(2,1)S(1)} %get-tuple-element.44), channel_id=1, source_target_pairs={{0,64},{64,128},{128,192},{256,320},{320,384},{384,448},{512,576},... | collective-permute-start | bytes 442376 | tf_op jit(solution)/shard_map/ppermute | solution.py:203
  245.8 16.7 %collective-permute-start.19 = (bf16[64,1152]{1,0:T(8,128)(2,1)S(1)}, bf16[64,1152]{1,0:T(8,128)(2,1)S(1)}, u32[]{:S(2)}, u32[]{:S(2)}) collective-permute-start(bf16[64,1152]{1,0:T(8,128)(2,1)S(1)} %collective-permute-done.18), channel_id=1, source_target_pairs={{192,0},{448,256},{704,512},{193,1},{449,257},{705,513},{194,2},{4... | collective-permute-start | bytes 442376 | tf_op jit(solution)/shard_map/ppermute | solution.py:205
  (6 other events, 9.7 us)

commit v7 on v5

--- a/solution.py
+++ b/solution.py
@@ -52,6 +52,20 @@
 
 def modulated(values_in, shift_row, scale_row):
     return (normalize(values_in) * (1.0 + scale_row) + shift_row).astype(BF16)
+
+
+def mixing_kernel(earlier_ref, frames_ref, taps_ref, mod_ref, mixed_ref, outgoing_ref):
+    frames = [earlier_ref[0], earlier_ref[1], frames_ref[0], frames_ref[1]]
+    frames = [frame.astype(F32) for frame in frames]
+    for f in range(2):
+        current, previous, second = frames[f + 2], frames[f + 1], frames[f]
+        mixed = (
+            current + taps_ref[0:1] * current + taps_ref[1:2] * previous + taps_ref[2:3] * second
+        ).astype(BF16)
+        mixed_ref[f] = mixed
+        attn_in = modulated(mixed.astype(F32), mod_ref[0:1], mod_ref[1:2])
+        for k in range(outgoing_ref.shape[0]):
+            outgoing_ref[k, f] = attn_in
 
 
 def attention_kernel(rows_ref, own_ref, own_out_ref, near_ref, part_ref, heads_ref):
@@ -132,17 +146,15 @@
     )
     far = rotate(far, "space", n_space // 2)
 
-    extended = jnp.concatenate([earlier, frames_in], axis=0).astype(F32)
-    mixed_rows = (
-        extended[2:]
-        + tap_set[0] * extended[2:]
-        + tap_set[1] * extended[1:-1]
-        + tap_set[2] * extended[:-2]
-    ).astype(BF16)
+    mixed_rows, outgoing = pl.pallas_call(
+        mixing_kernel,
+        out_shape=[
+            jax.ShapeDtypeStruct(frames_in.shape, BF16),
+            jax.ShapeDtypeStruct((n_space // frames, frames, tokens, D), BF16),
+        ],
+        name="mix_and_norm",
+    )(earlier, frames_in, tap_set, mod_table)
     mixed_f32 = mixed_rows.astype(F32)
-
-    attn_in = modulated(mixed_f32, mod_table[0], mod_table[1])
-    outgoing = jnp.broadcast_to(attn_in[None], (n_space // frames, frames, tokens, D))
     rows = lax.all_to_all(outgoing.reshape(n_space, tokens, D), "space", 0, 0, tiled=True)
     rows = rows.reshape(n_space * tokens, D)
     attn_part = attend(rows, qkv_own.reshape(-1, D), out_own, near.reshape(-1, D))
@@ -174,17 +186,20 @@
     sections = lax.axis_size("section")
     place_x = lax.axis_index("section") % 4
     along_x = [(s, s // 4 * 4 + (s + 1) % 4) for s in range(sections)]
+    layer_out = layer_out.reshape(-1, D)
+    cut = layer_out.shape[0] // 2
 
     def crossing(block, x):
         return lax.ppermute(block, "section", [(s, (s + 4) % sections) for s in range(x, sections, 4)])
 
-    second = lax.ppermute(layer_out[1], "section", along_x)
-    crossed = crossing(layer_out[0], 3)
-    first = lax.ppermute(layer_out[0], "section", [(s, d) for s, d in along_x if d == s + 1])
+    second = lax.ppermute(layer_out[cut:], "section", along_x)
+    crossed = crossing(layer_out[:cut], 3)
+    first = lax.ppermute(layer_out[:cut], "section", [(s, d) for s, d in along_x if d == s + 1])
     crossed_second = crossing(second, 0)
     first_end = lax.ppermute(crossed, "section", [(s, d) for s, d in along_x if d != s + 1])
-    arrived = [jnp.where(place_x == 0, first_end, first), jnp.where(place_x == 0, crossed_second, second)]
-    return jnp.stack(arrived)[None]
+    first = jnp.where(place_x == 0, first_end, first)
+    second = jnp.where(place_x == 0, crossed_second, second)
+    return jnp.concatenate([first, second]).reshape(video.shape)
 
 
 def solution(mesh):

time: 233 us -> 235 us (level)
  the two profiles are of different devices: /device:TPU:64 before, /device:TPU:192 now
where the time goes in v7:
time: 235 us; the launch traced here: 234 us
  waiting for transfers between devices  130 us (55%)
  starting transfers between devices  75 us (32%)
  local copies, waits for them, and re-layouts  10.7 us (5%)
  Pallas kernels  10.2 us (4%)
  matrix products  3.77 us (2%)
  other arithmetic  3.46 us (1%)
    ppermute x3, waiting for transfers between devices, flip(): lax.ppermute(block, axis, [(i, i ^ 1) for i in range(lax.axis_size(axis))])  36.7 us
    ppermute x1, waiting for transfers between devices, rotate(): lax.ppermute(block, axis, [(i, (i + steps) % count) for i in range(count)])  36.4 us
    ppermute x3, waiting for transfers between devices, turn_z(): lax.ppermute(block, 'tm', [(i, (i + 2 * steps) % count) for i in range(co...  25.1 us
    ppermute x6, waiting for transfers between devices, mirrored(): return lax.ppermute(block, ('tm', 'space'), route)  17.6 us
    ppermute x6, starting transfers between devices, mirrored(): return lax.ppermute(block, ('tm', 'space'), route)  16.8 us
    ppermute x2, starting transfers between devices, crossing(): lax.ppermute(block, 'section', [(s, (s + 4) % sections) for s in range(x,...  11.3 us
    ppermute x3, starting transfers between devices, turn_z(): lax.ppermute(block, 'tm', [(i, (i + 2 * steps) % count) for i in range(co...  10.3 us
    ppermute x1, starting transfers between devices, rotate(): lax.ppermute(block, axis, [(i, (i + steps) % count) for i in range(count)])  7.84 us
  transfers between devices with their start and end apart: 21, of which 14 were waited for; matrix products, arithmetic and copies ran while one was open for 4% of the time, Pallas kernels for 0%

profile of v7, /device:TPU:192, one launch (start us, length us, event | category | flops | bytes accessed | tf_op | source)
XLA Modules:
  0.0 234.0 jit_solution(13595458368529769262)
XLA Ops:
  5.7 2.5 %collective-permute-done.earlier_ref = bf16[2,64,1152]{2,1,0:T(8,128)(2,1)S(1)} collective-permute-done((bf16[2,64,1152]{2,1,0:T(8,128)(2,1)}, bf16[2,64,1152]{2,1,0:T(8,128)(2,1)S(1)}, u32[]{:S(2)}, u32[]{:S(2)}) %collective-permute-start) | collective-permute-done | bytes 294944 | tf_op jit(solution)/shard_map/ppermute | solution.py:20
  9.0 2.5 %mix_and_norm.1 = (bf16[2,64,1152]{2,1,0:T(8,128)(2,1)}, bf16[4,2,64,1152]{3,2,1,0:T(8,128)(2,1)}) custom-call(bf16[2,64,1152]{2,1,0:T(8,128)(2,1)} %copy-done.4, bf16[2,64,1152]{2,1,0:T(8,128)(2,1)} %bitcast.83, f32[3,1152]{1,0:T(4,128)} %bitcast.85, f32[6,1152]{1,0:T(8,128)} %bitcast.84), custom_call_target="tpu_custom_call" | custom-call | tf_op jit(solution)/shard_map/mix_and_norm/pallas_call | solution.py:149
  11.5 7.2 %all-to-all-start = ((bf16[8,64,1152]{2,1,0:T(8,128)(2,1)}), bf16[8,64,1152]{2,1,0:T(8,128)(2,1)S(1)}, u32[]{:S(2)}, u32[]{:S(2)}) async-start(bf16[8,64,1152]{2,1,0:T(8,128)(2,1)} %bitcast.65), calls=%async_computation | async-start | bytes 2359296 | tf_op jit(solution)/shard_map/all_to_all | solution.py:158
  18.8 3.9 %collective-permute-start.1 = (bf16[4,72,1152]{2,1,0:T(8,128)(2,1)S(1)}, bf16[4,72,1152]{2,1,0:T(8,128)(2,1)S(1)}, u32[]{:S(2)}, u32[]{:S(2)}) collective-permute-start(bf16[4,72,1152]{2,1,0:T(8,128)(2,1)S(1)} %pad_maximum_fusion.3), channel_id=1, source_target_pairs={{0,1},{1,0},{2,3},{3,2},{4,5},{5,4},{6,7},{7,6},{8,9},{9,8},{10,11... | collective-permute-start | bytes 1990664 | tf_op jit(solution)/shard_map/ppermute | solution.py:29
  22.7 34.6 %collective-permute-done.1 = bf16[4,72,1152]{2,1,0:T(8,128)(2,1)S(1)} collective-permute-done((bf16[4,72,1152]{2,1,0:T(8,128)(2,1)S(1)}, bf16[4,72,1152]{2,1,0:T(8,128)(2,1)S(1)}, u32[]{:S(2)}, u32[]{:S(2)}) %collective-permute-start.1) | collective-permute-done | bytes 663584 | tf_op jit(solution)/shard_map/ppermute | solution.py:29
  59.3 2.1 collective-permute-done.2
  63.6 7.7 %frame_attention.1 = bf16[512,1152]{1,0:T(8,128)(2,1)} custom-call(bf16[512,1152]{1,0:T(8,128)(2,1)} %bitcast.60, bf16[432,1152]{1,0:T(8,128)(2,1)} %bitcast.62, bf16[144,1152]{1,0:T(8,128)(2,1)} %bitcast.67, bf16[576,1152]{1,0:T(8,128)(2,1)} %bitcast.58), custom_call_target="tpu_custom_call" | custom-call | tf_op jit(solution)/shard_map/frame_attention/pallas_call | solution.py:101
  71.3 5.9 %all-to-all-start.1 = ((bf16[8,64,1152]{2,1,0:T(8,128)(2,1)}), bf16[8,64,1152]{2,1,0:T(8,128)(2,1)S(1)}, u32[]{:S(2)}, u32[]{:S(2)}) async-start(bf16[8,64,1152]{2,1,0:T(8,128)(2,1)} %bitcast.59), calls=%async_computation.1 | async-start | bytes 2359296 | tf_op jit(solution)/shard_map/all_to_all | solution.py:167
  79.1 7.8 %collective-permute-start.6 = (bf16[144,1152]{1,0:T(8,128)(2,1)S(1)}, bf16[144,1152]{1,0:T(8,128)(2,1)S(1)}, u32[]{:S(2)}, u32[]{:S(2)}) collective-permute-start(bf16[144,1152]{1,0:T(8,128)(2,1)S(1)} %pad_maximum_fusion.4), channel_id=1, source_target_pairs={{0,4},{1,5},{2,6},{3,7},{4,0},{5,1},{6,2},{7,3},{8,12},{9,13},{10,... | collective-permute-start | bytes 995336 | tf_op jit(solution)/shard_map/ppermute | solution.py:25
  87.0 36.4 %collective-permute-done.6 = bf16[144,1152]{1,0:T(8,128)(2,1)S(1)} collective-permute-done((bf16[144,1152]{1,0:T(8,128)(2,1)S(1)}, bf16[144,1152]{1,0:T(8,128)(2,1)S(1)}, u32[]{:S(2)}, u32[]{:S(2)}) %collective-permute-start.6) | collective-permute-done | bytes 331808 | tf_op jit(solution)/shard_map/ppermute | solution.py:25
  123.4 3.5 %collective-permute-start.7 = (bf16[144,1152]{1,0:T(8,128)(2,1)S(1)}, bf16[144,1152]{1,0:T(8,128)(2,1)S(1)}, u32[]{:S(2)}, u32[]{:S(2)}) collective-permute-start(bf16[144,1152]{1,0:T(8,128)(2,1)S(1)} %collective-permute-done.6), channel_id=1, source_target_pairs={{0,16},{8,24},{16,32},{24,40},{32,48},{40,56},{48,0},{56,8},{1,17}... | collective-permute-start | bytes 995336 | tf_op jit(solution)/shard_map/ppermute | solution.py:44
  126.9 4.9 %collective-permute-start.8 = (bf16[144,1152]{1,0:T(8,128)(2,1)S(1)}, bf16[144,1152]{1,0:T(8,128)(2,1)S(1)}, u32[]{:S(2)}, u32[]{:S(2)}) collective-permute-start(bf16[144,1152]{1,0:T(8,128)(2,1)S(1)} %collective-permute-done.6), channel_id=1, source_target_pairs={{0,32},{8,40},{16,48},{24,56},{32,0},{40,8},{48,16},{56,24},{1,33}... | collective-permute-start | bytes 995336 | tf_op jit(solution)/shard_map/ppermute | solution.py:44
  131.8 1.9 collective-permute-start.9
  133.8 2.6 %collective-permute-done.7 = bf16[144,1152]{1,0:T(8,128)(2,1)S(1)} collective-permute-done((bf16[144,1152]{1,0:T(8,128)(2,1)S(1)}, bf16[144,1152]{1,0:T(8,128)(2,1)S(1)}, u32[]{:S(2)}, u32[]{:S(2)}) %collective-permute-start.7) | collective-permute-done | bytes 331808 | tf_op jit(solution)/shard_map/ppermute | solution.py:44
  136.4 22.5 %collective-permute-done.8 = bf16[144,1152]{1,0:T(8,128)(2,1)S(1)} collective-permute-done((bf16[144,1152]{1,0:T(8,128)(2,1)S(1)}, bf16[144,1152]{1,0:T(8,128)(2,1)S(1)}, u32[]{:S(2)}, u32[]{:S(2)}) %collective-permute-start.8) | collective-permute-done | bytes 331808 | tf_op jit(solution)/shard_map/ppermute | solution.py:44
  159.1 1.9 collective-permute-start.10
  163.5 1.9 collective-permute-start.3
  165.5 1.9 collective-permute-start.4
  167.4 5.1 %collective-permute-start.5 = (bf16[2,64,1152]{2,1,0:T(8,128)(2,1)S(1)}, bf16[2,64,1152]{2,1,0:T(8,128)(2,1)S(1)}, u32[]{:S(2)}, u32[]{:S(2)}) collective-permute-start(bf16[2,64,1152]{2,1,0:T(8,128)(2,1)S(1)} %add_convert_fusion), channel_id=1, source_target_pairs={{0,7},{1,0},{2,1},{3,2},{4,3},{5,4},{6,5},{7,6},{8,9},{9,10},{10,1... | collective-permute-start | bytes 884744 | tf_op jit(solution)/shard_map/ppermute | solution.py:39
  174.0 2.3 collective-permute-done.3
  176.3 5.4 %collective-permute-done.4 = bf16[2,64,1152]{2,1,0:T(8,128)(2,1)S(1)} collective-permute-done((bf16[2,64,1152]{2,1,0:T(8,128)(2,1)S(1)}, bf16[2,64,1152]{2,1,0:T(8,128)(2,1)S(1)}, u32[]{:S(2)}, u32[]{:S(2)}) %collective-permute-start.4) | collective-permute-done | bytes 294944 | tf_op jit(solution)/shard_map/ppermute | solution.py:39
  181.9 1.9 fusion.20
  185.8 2.0 collective-permute-start.11
  187.8 3.5 %collective-permute-start.12 = (bf16[2,64,1152]{2,1,0:T(8,128)(2,1)S(1)}, bf16[2,64,1152]{2,1,0:T(8,128)(2,1)S(1)}, u32[]{:S(2)}, u32[]{:S(2)}) collective-permute-start(bf16[2,64,1152]{2,1,0:T(8,128)(2,1)S(1)} %bitcast.80), channel_id=1, source_target_pairs={{0,7},{1,0},{2,1},{3,2},{4,3},{5,4},{6,5},{7,6},{8,9},{9,10},{10,1... | collective-permute-start | bytes 884744 | tf_op jit(solution)/shard_map/ppermute | solution.py:39
  191.3 2.4 %collective-permute-start.13 = (bf16[2,64,1152]{2,1,0:T(8,128)(2,1)S(1)}, bf16[2,64,1152]{2,1,0:T(8,128)(2,1)S(1)}, u32[]{:S(2)}, u32[]{:S(2)}) collective-permute-start(bf16[2,64,1152]{2,1,0:T(8,128)(2,1)S(1)} %bitcast.78), channel_id=1, source_target_pairs={{0,1},{1,2},{2,3},{3,4},{4,5},{5,6},{6,7},{7,0},{8,15},{9,8},{10,9... | collective-permute-start | bytes 884744 | tf_op jit(solution)/shard_map/ppermute | solution.py:39
  193.7 5.6 %collective-permute-done.11 = bf16[2,64,1152]{2,1,0:T(8,128)(2,1)S(1)} collective-permute-done((bf16[2,64,1152]{2,1,0:T(8,128)(2,1)S(1)}, bf16[2,64,1152]{2,1,0:T(8,128)(2,1)S(1)}, u32[]{:S(2)}, u32[]{:S(2)}) %collective-permute-start.11) | collective-permute-done | bytes 294944 | tf_op jit(solution)/shard_map/ppermute | solution.py:39
  199.3 4.0 %collective-permute-done.12 = bf16[2,64,1152]{2,1,0:T(8,128)(2,1)S(1)} collective-permute-done((bf16[2,64,1152]{2,1,0:T(8,128)(2,1)S(1)}, bf16[2,64,1152]{2,1,0:T(8,128)(2,1)S(1)}, u32[]{:S(2)}, u32[]{:S(2)}) %collective-permute-start.12) | collective-permute-done | bytes 294944 | tf_op jit(solution)/shard_map/ppermute | solution.py:39
  203.8 3.4 %collective-permute-start.17 = (bf16[64,1152]{1,0:T(8,128)(2,1)S(1)}, bf16[64,1152]{1,0:T(8,128)(2,1)S(1)}, u32[]{:S(2)}, u32[]{:S(2)}) collective-permute-start(bf16[64,1152]{1,0:T(8,128)(2,1)S(1)} %get-tuple-element.24), channel_id=1, source_target_pairs={{0,64},{64,128},{128,192},{192,0},{256,320},{320,384},{384,448},{4... | collective-permute-start | bytes 442376 | tf_op jit(solution)/shard_map/ppermute | solution.py:195
  207.9 4.1 %collective-permute-done.17 = bf16[64,1152]{1,0:T(8,128)(2,1)S(1)} collective-permute-done((bf16[64,1152]{1,0:T(8,128)(2,1)S(1)}, bf16[64,1152]{1,0:T(8,128)(2,1)S(1)}, u32[]{:S(2)}, u32[]{:S(2)}) %collective-permute-start.17) | collective-permute-done | bytes 147488 | tf_op jit(solution)/shard_map/ppermute | solution.py:195
  212.1 10.6 %collective-permute-start.18 = (bf16[64,1152]{1,0:T(8,128)(2,1)S(1)}, bf16[64,1152]{1,0:T(8,128)(2,1)S(1)}, u32[]{:S(2)}, u32[]{:S(2)}) collective-permute-start(bf16[64,1152]{1,0:T(8,128)(2,1)S(1)} %collective-permute-done.17), channel_id=1, source_target_pairs={{0,256},{256,512},{512,0},{1,257},{257,513},{513,1},{2,258},{258,5... | collective-permute-start | bytes 442376 | tf_op jit(solution)/shard_map/ppermute | solution.py:193
  225.3 5.3 %collective-permute-done.18 = bf16[64,1152]{1,0:T(8,128)(2,1)S(1)} collective-permute-done((bf16[64,1152]{1,0:T(8,128)(2,1)S(1)}, bf16[64,1152]{1,0:T(8,128)(2,1)S(1)}, u32[]{:S(2)}, u32[]{:S(2)}) %collective-permute-start.18) | collective-permute-done | bytes 147488 | tf_op jit(solution)/shard_map/ppermute | solution.py:193
  230.6 2.6 %collective-permute-done.15 = bf16[64,1152]{1,0:T(8,128)(2,1)S(1)} collective-permute-done((bf16[64,1152]{1,0:T(8,128)(2,1)S(1)}, bf16[64,1152]{1,0:T(8,128)(2,1)S(1)}, u32[]{:S(2)}, u32[]{:S(2)}) %collective-permute-start.15) | collective-permute-done | bytes 147488 | tf_op jit(solution)/shard_map/ppermute | solution.py:199
  (56 shorter events, 23.3 us)
Async XLA Ops:
  0.0 8.2 %collective-permute-start = (bf16[2,64,1152]{2,1,0:T(8,128)(2,1)}, bf16[2,64,1152]{2,1,0:T(8,128)(2,1)S(1)}, u32[]{:S(2)}, u32[]{:S(2)}) collective-permute-start(bf16[2,64,1152]{2,1,0:T(8,128)(2,1)} %bitcast.82), channel_id=1, source_target_pairs={{0,8},{8,16},{16,24},{24,32},{32,40},{40,48},{48,56},{1,9},{9,17},... | collective-permute-start | bytes 884744 | tf_op jit(solution)/shard_map/ppermute | solution.py:20
  8.2 0.7 copy-start.4
  11.5 7.2 %copy-start.2 = (bf16[1,144,1152]{2,1,0:T(8,128)(2,1)S(1)}, bf16[1,144,1152]{2,1,0:T(8,128)(2,1)}, u32[]{:S(2)}) copy-start(bf16[1,144,1152]{2,1,0:T(8,128)(2,1)} %param.11) | copy-start | bytes 995332
  11.5 51.1 %all-to-all-start = ((bf16[8,64,1152]{2,1,0:T(8,128)(2,1)}), bf16[8,64,1152]{2,1,0:T(8,128)(2,1)S(1)}, u32[]{:S(2)}, u32[]{:S(2)}) async-start(bf16[8,64,1152]{2,1,0:T(8,128)(2,1)} %bitcast.65), calls=%async_computation | async-start | bytes 2359296 | tf_op jit(solution)/shard_map/all_to_all | solution.py:158
  18.8 38.6 %collective-permute-start.1 = (bf16[4,72,1152]{2,1,0:T(8,128)(2,1)S(1)}, bf16[4,72,1152]{2,1,0:T(8,128)(2,1)S(1)}, u32[]{:S(2)}, u32[]{:S(2)}) collective-permute-start(bf16[4,72,1152]{2,1,0:T(8,128)(2,1)S(1)} %pad_maximum_fusion.3), channel_id=1, source_target_pairs={{0,1},{1,0},{2,3},{3,2},{4,5},{5,4},{6,7},{7,6},{8,9},{9,8},{10,11... | collective-permute-start | bytes 1990664 | tf_op jit(solution)/shard_map/ppermute | solution.py:29
  57.4 4.0 %collective-permute-start.2 = (bf16[4,72,1152]{2,1,0:T(8,128)(2,1)S(1)}, bf16[4,72,1152]{2,1,0:T(8,128)(2,1)S(1)}, u32[]{:S(2)}, u32[]{:S(2)}) collective-permute-start(bf16[4,72,1152]{2,1,0:T(8,128)(2,1)S(1)} %collective-permute-done.1), channel_id=1, source_target_pairs={{0,8},{8,0},{16,24},{24,16},{32,40},{40,32},{48,56},{56,48},{1,9},... | collective-permute-start | bytes 1990664 | tf_op jit(solution)/shard_map/ppermute | solution.py:29
  62.6 1.0 copy-start
  71.3 62.4 %copy-start.5 = (f32[1,6,1152]{2,0,1:T(1,128)S(1)}, f32[1,6,1152]{2,0,1:T(1,128)}, u32[]{:S(2)}) copy-start(f32[1,6,1152]{2,0,1:T(1,128)} %param.9) | copy-start | bytes 82948
  71.3 90.7 %all-to-all-start.1 = ((bf16[8,64,1152]{2,1,0:T(8,128)(2,1)}), bf16[8,64,1152]{2,1,0:T(8,128)(2,1)S(1)}, u32[]{:S(2)}, u32[]{:S(2)}) async-start(bf16[8,64,1152]{2,1,0:T(8,128)(2,1)} %bitcast.59), calls=%async_computation.1 | async-start | bytes 2359296 | tf_op jit(solution)/shard_map/all_to_all | solution.py:167
  79.1 44.2 %collective-permute-start.6 = (bf16[144,1152]{1,0:T(8,128)(2,1)S(1)}, bf16[144,1152]{1,0:T(8,128)(2,1)S(1)}, u32[]{:S(2)}, u32[]{:S(2)}) collective-permute-start(bf16[144,1152]{1,0:T(8,128)(2,1)S(1)} %pad_maximum_fusion.4), channel_id=1, source_target_pairs={{0,4},{1,5},{2,6},{3,7},{4,0},{5,1},{6,2},{7,3},{8,12},{9,13},{10,... | collective-permute-start | bytes 995336 | tf_op jit(solution)/shard_map/ppermute | solution.py:25
  123.4 13.0 %collective-permute-start.7 = (bf16[144,1152]{1,0:T(8,128)(2,1)S(1)}, bf16[144,1152]{1,0:T(8,128)(2,1)S(1)}, u32[]{:S(2)}, u32[]{:S(2)}) collective-permute-start(bf16[144,1152]{1,0:T(8,128)(2,1)S(1)} %collective-permute-done.6), channel_id=1, source_target_pairs={{0,16},{8,24},{16,32},{24,40},{32,48},{40,56},{48,0},{56,8},{1,17}... | collective-permute-start | bytes 995336 | tf_op jit(solution)/shard_map/ppermute | solution.py:44
  126.9 32.0 %collective-permute-start.8 = (bf16[144,1152]{1,0:T(8,128)(2,1)S(1)}, bf16[144,1152]{1,0:T(8,128)(2,1)S(1)}, u32[]{:S(2)}, u32[]{:S(2)}) collective-permute-start(bf16[144,1152]{1,0:T(8,128)(2,1)S(1)} %collective-permute-done.6), channel_id=1, source_target_pairs={{0,32},{8,40},{16,48},{24,56},{32,0},{40,8},{48,16},{56,24},{1,33}... | collective-permute-start | bytes 995336 | tf_op jit(solution)/shard_map/ppermute | solution.py:44
  131.8 27.1 %collective-permute-start.9 = (bf16[144,1152]{1,0:T(8,128)(2,1)S(1)}, bf16[144,1152]{1,0:T(8,128)(2,1)S(1)}, u32[]{:S(2)}, u32[]{:S(2)}) collective-permute-start(bf16[144,1152]{1,0:T(8,128)(2,1)S(1)} %collective-permute-done.6), channel_id=1, source_target_pairs={{0,48},{8,56},{16,0},{24,8},{32,16},{40,24},{48,32},{56,40},{1,49}... | collective-permute-start | bytes 995336 | tf_op jit(solution)/shard_map/ppermute | solution.py:44
  159.1 13.4 %collective-permute-start.10 = (bf16[4,144,1152]{2,1,0:T(8,128)(2,1)S(1)}, bf16[4,144,1152]{2,1,0:T(8,128)(2,1)}, u32[]{:S(2)}, u32[]{:S(2)}) collective-permute-start(bf16[4,144,1152]{2,1,0:T(8,128)(2,1)S(1)} %pad_maximum_fusion.1), channel_id=1, source_target_pairs={{0,8},{8,0},{16,24},{24,16},{32,40},{40,32},{48,56},{56,48},{1,9},... | collective-permute-start | bytes 3981320 | tf_op jit(solution)/shard_map/ppermute | solution.py:29
  162.0 1.0 copy-start.1
  163.5 12.8 %collective-permute-start.3 = (bf16[2,64,1152]{2,1,0:T(8,128)(2,1)S(1)}, bf16[2,64,1152]{2,1,0:T(8,128)(2,1)S(1)}, u32[]{:S(2)}, u32[]{:S(2)}) collective-permute-start(bf16[2,64,1152]{2,1,0:T(8,128)(2,1)S(1)} %add_convert_fusion), channel_id=1, source_target_pairs={{0,2},{1,3},{2,4},{3,5},{4,6},{5,7},{6,0},{7,1},{8,14},{9,15},{10,... | collective-permute-start | bytes 884744 | tf_op jit(solution)/shard_map/ppermute | solution.py:39
  165.5 16.3 %collective-permute-start.4 = (bf16[2,64,1152]{2,1,0:T(8,128)(2,1)S(1)}, bf16[2,64,1152]{2,1,0:T(8,128)(2,1)S(1)}, u32[]{:S(2)}, u32[]{:S(2)}) collective-permute-start(bf16[2,64,1152]{2,1,0:T(8,128)(2,1)S(1)} %add_convert_fusion), channel_id=1, source_target_pairs={{0,1},{1,2},{2,3},{3,4},{4,5},{5,6},{6,7},{7,0},{8,15},{9,8},{10,9... | collective-permute-start | bytes 884744 | tf_op jit(solution)/shard_map/ppermute | solution.py:39
  167.4 14.3 %collective-permute-start.5 = (bf16[2,64,1152]{2,1,0:T(8,128)(2,1)S(1)}, bf16[2,64,1152]{2,1,0:T(8,128)(2,1)S(1)}, u32[]{:S(2)}, u32[]{:S(2)}) collective-permute-start(bf16[2,64,1152]{2,1,0:T(8,128)(2,1)S(1)} %add_convert_fusion), channel_id=1, source_target_pairs={{0,7},{1,0},{2,1},{3,2},{4,3},{5,4},{6,5},{7,6},{8,9},{9,10},{10,1... | collective-permute-start | bytes 884744 | tf_op jit(solution)/shard_map/ppermute | solution.py:39
  174.0 8.0 %copy-start.3 = (bf16[4,72,1152]{2,1,0:T(8,128)(2,1)S(1)}, bf16[4,72,1152]{2,1,0:T(8,128)(2,1)}, u32[]{:S(2)}) copy-start(bf16[4,72,1152]{2,1,0:T(8,128)(2,1)} %get-tuple-element.16) | copy-start | bytes 1990660
  174.0 8.0 %copy-start.6 = (bf16[1,1152,576]{1,2,0:T(8,128)(2,1)S(1)}, bf16[1,1152,576]{1,2,0:T(8,128)(2,1)}, u32[]{:S(2)}) copy-start(bf16[1,1152,576]{1,2,0:T(8,128)(2,1)} %param.12) | copy-start | bytes 3981316
  181.9 1.9 copy-start.7
  185.8 13.5 %collective-permute-start.11 = (bf16[2,64,1152]{2,1,0:T(8,128)(2,1)S(1)}, bf16[2,64,1152]{2,1,0:T(8,128)(2,1)S(1)}, u32[]{:S(2)}, u32[]{:S(2)}) collective-permute-start(bf16[2,64,1152]{2,1,0:T(8,128)(2,1)S(1)} %bitcast.81), channel_id=1, source_target_pairs={{0,6},{1,7},{2,0},{3,1},{4,2},{5,3},{6,4},{7,5},{8,10},{9,11},{10,... | collective-permute-start | bytes 884744 | tf_op jit(solution)/shard_map/ppermute | solution.py:39
  187.8 15.5 %collective-permute-start.12 = (bf16[2,64,1152]{2,1,0:T(8,128)(2,1)S(1)}, bf16[2,64,1152]{2,1,0:T(8,128)(2,1)S(1)}, u32[]{:S(2)}, u32[]{:S(2)}) collective-permute-start(bf16[2,64,1152]{2,1,0:T(8,128)(2,1)S(1)} %bitcast.80), channel_id=1, source_target_pairs={{0,7},{1,0},{2,1},{3,2},{4,3},{5,4},{6,5},{7,6},{8,9},{9,10},{10,1... | collective-permute-start | bytes 884744 | tf_op jit(solution)/shard_map/ppermute | solution.py:39
  191.3 12.2 %collective-permute-start.13 = (bf16[2,64,1152]{2,1,0:T(8,128)(2,1)S(1)}, bf16[2,64,1152]{2,1,0:T(8,128)(2,1)S(1)}, u32[]{:S(2)}, u32[]{:S(2)}) collective-permute-start(bf16[2,64,1152]{2,1,0:T(8,128)(2,1)S(1)} %bitcast.78), channel_id=1, source_target_pairs={{0,1},{1,2},{2,3},{3,4},{4,5},{5,6},{6,7},{7,0},{8,15},{9,8},{10,9... | collective-permute-start | bytes 884744 | tf_op jit(solution)/shard_map/ppermute | solution.py:39
  203.8 8.2 %collective-permute-start.17 = (bf16[64,1152]{1,0:T(8,128)(2,1)S(1)}, bf16[64,1152]{1,0:T(8,128)(2,1)S(1)}, u32[]{:S(2)}, u32[]{:S(2)}) collective-permute-start(bf16[64,1152]{1,0:T(8,128)(2,1)S(1)} %get-tuple-element.24), channel_id=1, source_target_pairs={{0,64},{64,128},{128,192},{192,0},{256,320},{320,384},{384,448},{4... | collective-permute-start | bytes 442376 | tf_op jit(solution)/shard_map/ppermute | solution.py:195
  207.2 16.7 %collective-permute-start.14 = (bf16[64,1152]{1,0:T(8,128)(2,1)S(1)}, bf16[64,1152]{1,0:T(8,128)(2,1)S(1)}, u32[]{:S(2)}, u32[]{:S(2)}) collective-permute-start(bf16[64,1152]{1,0:T(8,128)(2,1)S(1)} %get-tuple-element.23), channel_id=1, source_target_pairs={{192,448},{448,704},{704,192},{193,449},{449,705},{705,193},{194,4... | collective-permute-start | bytes 442376 | tf_op jit(solution)/shard_map/ppermute | solution.py:193
  212.1 18.5 %collective-permute-start.18 = (bf16[64,1152]{1,0:T(8,128)(2,1)S(1)}, bf16[64,1152]{1,0:T(8,128)(2,1)S(1)}, u32[]{:S(2)}, u32[]{:S(2)}) collective-permute-start(bf16[64,1152]{1,0:T(8,128)(2,1)S(1)} %collective-permute-done.17), channel_id=1, source_target_pairs={{0,256},{256,512},{512,0},{1,257},{257,513},{513,1},{2,258},{258,5... | collective-permute-start | bytes 442376 | tf_op jit(solution)/shard_map/ppermute | solution.py:193
  222.7 7.9 %collective-permute-start.16 = (bf16[64,1152]{1,0:T(8,128)(2,1)S(1)}, bf16[64,1152]{1,0:T(8,128)(2,1)S(1)}, u32[]{:S(2)}, u32[]{:S(2)}) collective-permute-start(bf16[64,1152]{1,0:T(8,128)(2,1)S(1)} %get-tuple-element.23), channel_id=1, source_target_pairs={{0,64},{64,128},{128,192},{256,320},{320,384},{384,448},{512,576},... | collective-permute-start | bytes 442376 | tf_op jit(solution)/shard_map/ppermute | solution.py:197
  224.0 9.3 %collective-permute-start.15 = (bf16[64,1152]{1,0:T(8,128)(2,1)S(1)}, bf16[64,1152]{1,0:T(8,128)(2,1)S(1)}, u32[]{:S(2)}, u32[]{:S(2)}) collective-permute-start(bf16[64,1152]{1,0:T(8,128)(2,1)S(1)} %collective-permute-done.14), channel_id=1, source_target_pairs={{192,0},{448,256},{704,512},{193,1},{449,257},{705,513},{194,2},{4... | collective-permute-start | bytes 442376 | tf_op jit(solution)/shard_map/ppermute | solution.py:199
